TPU v7x, 32 devices: a whole 2x2x4 slice. The times are simulated.
32 devices in a mesh: queue: 8 (over z, core), tok: 4 (over y, x).
Axes of the slice: x: 2, y: 2, z: 4, core: 2. Of those that a mesh axis runs over, the one named last changes fastest.
Arguments:
- latents: float32 [8, 512, 64], P('queue', 'tok'), may hold values from -6 to 6
- step_index: int32 [8], replicated, may hold values from 0 to 31, as said below
- tail_noise: float32 [512, 64], P('tok'), may hold values from -6 to 6
- patch_weight: bfloat16 [64, 1536], replicated, may hold values from -0.75 to 0.75
- time_table: float32 [32, 3, 1536], replicated, may hold values from -3 to 3
- qkv_weight: bfloat16 [1536, 4608], replicated, may hold values from -1 to 1
- q_gain: float32 [1536], replicated, may hold values from 1 to 3
- k_gain: float32 [1536], replicated, may hold values from 1 to 3
- out_weight: bfloat16 [1536, 1536], replicated, may hold values from -0.15625 to 0.15625
- head_weight: bfloat16 [1536, 64], replicated, may hold values from -0.15625 to 0.15625
Outputs:
- velocity: float32 [8, 512, 64], P('queue', 'tok')
- queue_next: float32 [8, 512, 64], P('queue', 'tok')
- leaving: float32 [64, 512], P('queue', 'tok')
Inputs may be any that keep to these rules, and one draw needn't show every extreme that they name: `step_index`: strictly rising along the queue, by 1 to 4 from one frame to the next; the tail frame is at level 31.
All inputs are finite; a program needn't handle non-finite values.
Results may differ from a plain program's by a relative error of at most 0.0095.
Values may be sent and summed in bfloat16 or wider, within the bound.
No kernel may reach another device: no remote copies, remote signals or barrier semaphores. Data moves between devices by JAX's collectives and lax.ppermute only.
A program may use at most 320 MiB of HBM per device.

v0:
```python
import jax
import jax.numpy as jnp
from jax import lax
from jax.sharding import PartitionSpec as P

HEAD_DIM = 128


def passed_along(value, axis, by):
    peers = lax.axis_size(axis)
    pairs = [(i, i + by) for i in range(peers) if 0 <= i + by < peers]
    return lax.ppermute(value, axis, pairs)


def spread(value, axis, root):
    mine = lax.axis_index(axis) == root
    return lax.psum(jnp.where(mine, value, jnp.zeros_like(value)), axis)


def layer_norm(values):
    mean_row = jnp.mean(values, axis=-1, keepdims=True)
    centred = values - mean_row
    variance = jnp.mean(centred * centred, axis=-1, keepdims=True)
    return centred * lax.rsqrt(variance + 1e-06)


def rms_norm(values, gain_vec):
    return values * lax.rsqrt(jnp.mean(values * values, axis=-1, keepdims=True) + 1e-06) * gain_vec


def fold_keys(carried, queries, portion, scaling):
    run_max, run_sum, run_out = carried
    head_count = queries.shape[1]
    head_size = queries.shape[2]
    feature = head_count * head_size
    key_rows = portion[:, :feature].reshape(portion.shape[0], head_count, head_size)
    value_rows = portion[:, feature:].reshape(portion.shape[0], head_count, head_size)
    scores = (
        jnp.einsum("rhd,khd->rhk", queries, key_rows, preferred_element_type=jnp.float32) * scaling
    )
    new_max = jnp.maximum(run_max, jnp.max(scores, axis=-1))
    factor = jnp.exp(run_max - new_max)
    weights = jnp.exp(scores - new_max[..., None])
    run_sum = run_sum * factor + jnp.sum(weights, axis=-1)
    run_out = run_out * factor[..., None] + jnp.einsum(
        "rhk,khd->rhd", weights.astype(jnp.bfloat16), value_rows, preferred_element_type=jnp.float32
    )
    return (new_max, run_sum, run_out)


def merge_states(maxima, totals, outputs):
    top = jnp.max(maxima, axis=0)
    factor = jnp.exp(maxima - top[None])
    return (top, jnp.sum(totals * factor, axis=0), jnp.sum(outputs * factor[..., None], axis=0))


def fresh_state(row_count, head_count, head_size):
    return (
        jnp.full((row_count, head_count), -1e30, jnp.float32),
        jnp.zeros((row_count, head_count), jnp.float32),
        jnp.zeros((row_count, head_count, head_size), jnp.float32),
    )


def key_value_rows(normed, qkv_weight, k_gain, feature):
    projected = jnp.dot(normed, qkv_weight[:, feature:], preferred_element_type=jnp.float32)
    key_part = rms_norm(projected[:, :feature], k_gain).astype(jnp.bfloat16)
    return jnp.concatenate([key_part, projected[:, feature:].astype(jnp.bfloat16)], axis=1)


def per_device(
    latents,
    step_index,
    tail_noise,
    patch_weight,
    time_table,
    qkv_weight,
    q_gain,
    k_gain,
    out_weight,
    head_weight,
):
    feature = patch_weight.shape[1]
    head_size = HEAD_DIM
    head_count = feature // head_size
    scaling = head_size ** (-0.5)
    levels = time_table.shape[0]
    frames = lax.axis_size("queue")
    position = lax.axis_index("queue")
    latent = latents[0]
    tok_rows = latent.shape[0]
    level_now = step_index[position]
    level_before = jnp.where(position > 0, step_index[jnp.maximum(position - 1, 0)], -1)
    one_hot = (jnp.arange(levels, dtype=jnp.int32) == level_now).astype(jnp.float32)[None, :]
    modulation = jnp.dot(
        one_hot, time_table.reshape(levels, 3 * feature), precision=lax.Precision.HIGHEST
    ).reshape(3, feature)
    hidden = jnp.dot(latent.astype(jnp.bfloat16), patch_weight, preferred_element_type=jnp.float32)
    normed = (layer_norm(hidden) * (1.0 + modulation[1]) + modulation[0]).astype(jnp.bfloat16)
    query_proj = jnp.dot(normed, qkv_weight[:, :feature], preferred_element_type=jnp.float32)
    queries = rms_norm(query_proj, q_gain).astype(jnp.bfloat16)
    every_latent = lax.all_gather(latent.astype(jnp.bfloat16), "queue", axis=0, tiled=True).astype(
        latent.dtype
    )
    all_hot = (step_index[:, None] == jnp.arange(levels, dtype=jnp.int32)[None, :]).astype(
        jnp.float32
    )
    all_mod = jnp.dot(
        all_hot, time_table.reshape(levels, 3 * feature), precision=lax.Precision.HIGHEST
    ).reshape(frames, 1, 3, feature)
    every_hidden = jnp.dot(
        every_latent.astype(jnp.bfloat16), patch_weight, preferred_element_type=jnp.float32
    ).reshape(frames, tok_rows, feature)
    every_normed = (layer_norm(every_hidden) * (1.0 + all_mod[:, :, 1]) + all_mod[:, :, 0]).astype(
        jnp.bfloat16
    )
    every_pair = key_value_rows(
        every_normed.reshape(frames * tok_rows, feature), qkv_weight, k_gain, feature
    ).reshape(frames, tok_rows, 2 * feature)
    whole_queries = lax.all_gather(queries, "tok", axis=0, tiled=True)
    frame_rows = whole_queries.shape[0]
    whole_queries = whole_queries.reshape(frame_rows, head_count, head_size)

    def step_frame(carried, portion):
        return (fold_keys(carried, whole_queries, portion, scaling), None)

    state, unused = lax.scan(step_frame, fresh_state(frame_rows, head_count, head_size), every_pair)
    parts = (
        lax.all_to_all(
            state[0][None].astype(jnp.bfloat16), "tok", split_axis=1, concat_axis=0, tiled=True
        ).astype(jnp.float32),
        lax.all_to_all(
            state[1][None].astype(jnp.bfloat16), "tok", split_axis=1, concat_axis=0, tiled=True
        ).astype(jnp.float32),
        lax.all_to_all(
            state[2][None].astype(jnp.bfloat16), "tok", split_axis=1, concat_axis=0, tiled=True
        ).astype(jnp.float32),
    )
    carried = merge_states(parts[0], parts[1], parts[2])
    run_max, run_sum, run_out = carried
    attended = (run_out / run_sum[..., None]).reshape(tok_rows, feature).astype(jnp.bfloat16)
    attn_out = jnp.dot(attended, out_weight, preferred_element_type=jnp.float32)
    residual = hidden + modulation[2] * attn_out
    velocity = jnp.dot(
        residual.astype(jnp.bfloat16), head_weight, preferred_element_type=jnp.float32
    )
    sigma_now = (level_now.astype(jnp.float32) + 1.0) / levels
    sigma_next = (level_before.astype(jnp.float32) + 1.0) / levels
    updated = latent + (sigma_next - sigma_now) * velocity
    arrived = passed_along(updated.astype(jnp.bfloat16), "queue", -1).astype(updated.dtype)
    queue_next = jnp.where(position == frames - 1, tail_noise, arrived)
    clean_frame = spread(updated.T.astype(jnp.bfloat16), "queue", 0).astype(jnp.float32)
    channel_share = clean_frame.shape[0] // frames
    leaving = lax.dynamic_slice_in_dim(clean_frame, position * channel_share, channel_share, 0)
    return (velocity[None], queue_next[None], leaving)


def solution(mesh):
    placed = (P("queue", "tok", None), P(), P("tok", None), P(), P(), P(), P(), P(), P(), P())
    return jax.shard_map(
        per_device,
        mesh=mesh,
        in_specs=placed,
        out_specs=(P("queue", "tok", None), P("queue", "tok", None), P("queue", "tok")),
        check_vma=False,
    )
```

profile of v0, /device:TPU:0, one launch (start us, length us, event | category | flops | bytes accessed | tf_op | source)
XLA Modules:
  0.0 238.6 jit_solution(16056265235811891979)
XLA Ops:
  8.4 1.4 fusion.36
  12.0 3.3 %multiply_reduce_fusion.2 = (f32[128]{0:T(128)S(1)}, f32[128,1536]{1,0:T(8,128)S(1)}) fusion(bf16[1536,4608]{1,0:T(8,128)(2,1)} %param.17, f32[128,1536]{1,0:T(8,128)S(1)} %get-tuple-element.135, f32[1536]{0:T(1024)S(1)} %get-tuple-element.126, f32[1536]{0:T(1024)S(1)} %get-tuple-element.127, f32[128]{0:T(128)S(1)} %add_rsqrt_fusion.3, ...), kind=kOutput, calls=%fused_computation.38 | convolution fusion | flops 605355904 | bytes 6305280 | tf_op jit(solution)/shard_map/dot_general | solution.py:100
  16.3 14.5 %all_gather.6 = bf16[1024,64]{0,1:T(8,128)(2,1)S(1)} all-gather(bf16[128,64]{0,1:T(8,128)(2,1)S(1)} %bitcast_convert_fusion), channel_id=1, replica_groups=mesh['queue'=8,'tok'=4] {'queue'}, dimensions={0}, use_global_device_ids=true | all-gather | bytes 147456 | tf_op jit(solution)/shard_map/all_gather | solution.py:102
  33.1 1.4 fusion.10
  34.7 1.4 slice-done.2
  36.5 12.4 %fusion.8 = f32[1024,3072]{1,0:T(8,128)} fusion(bf16[1024,1536]{1,0:T(8,128)(2,1)S(1)} %fusion.10, bf16[1536,4608]{1,0:T(8,128)(2,1)S(1)} %bitcast.130), kind=kOutput, calls=%fused_computation.15 | convolution fusion | flops 9663676416 | bytes 25165824 | tf_op jit(solution)/shard_map/dot_general | solution.py:66
  48.8 3.3 %slice.69 = bf16[1024,1536]{1,0:T(8,128)(2,1)S(1)} slice(f32[1024,3072]{1,0:T(8,128)} %fusion.8), slice={[0:1024], [1536:3072]} | slice | bytes 6291456 | tf_op jit(solution)/shard_map/slice | solution.py:68
  52.2 4.0 %multiply_reduce_fusion = f32[1024]{0:T(1024)S(1)} fusion(f32[1024,3072]{1,0:T(8,128)} %fusion.8), kind=kLoop, calls=%fused_computation.23 | loop fusion | flops 3144704 | bytes 6295552 | tf_op jit(solution)/shard_map/reduce_sum | solution.py:28
  57.6 3.6 %pad_maximum_fusion = bf16[1024,3072]{1,0:T(8,128)(2,1)} fusion(bf16[1024,1536]{1,0:T(8,128)(2,1)S(1)} %slice.69, bf16[1024,1536]{1,0:T(8,128)(2,1)S(1)} %multiply_convert_fusion), kind=kLoop, calls=%fused_computation.18 | loop fusion | flops 12582912 | bytes 12582912 | tf_op jit(solution)/shard_map/concatenate | solution.py:68
  61.3 1.7 copy.82
  63.0 1.6 copy.84
  64.6 82.9 %while.15 = (s32[]{:T(128)}, f32[512,12]{0,1:T(8,128)S(1)}, f32[512,12]{0,1:T(8,128)S(1)}, f32[512,12,128]{0,2,1:T(8,128)}, bf16[8,128,3072]{2,1,0:T(8,128)(2,1)...) while((s32[]{:T(128)}, f32[512,12]{0,1:T(8,128)S(1)}, f32[512,12]{0,1:T(8,128)S(1)}, ...), condition=%wide.region_9.10_spmd.clone, body=%wide.region_6.9_spmd.clone.sunk | while | flops 411334656 | bytes 48365724 | solution.py:127
  64.6 1.2 constant_dynamic-slice_fusion.2
  67.0 2.0 bitcast_reduce_fusion.2
  69.6 1.3 copy-done.2
  70.9 2.3 bitcast_add_fusion.4
  73.2 1.7 copy-done.3
  74.9 1.2 constant_dynamic-slice_fusion.2
  77.3 2.0 bitcast_reduce_fusion.2
  80.0 1.3 copy-done.2
  81.3 2.3 bitcast_add_fusion.4
  83.6 1.7 copy-done.3
  85.3 1.2 constant_dynamic-slice_fusion.2
  87.7 2.0 bitcast_reduce_fusion.2
  90.4 1.3 copy-done.2
  91.6 2.3 bitcast_add_fusion.4
  94.0 1.7 copy-done.3
  95.7 1.2 constant_dynamic-slice_fusion.2
  98.1 2.0 bitcast_reduce_fusion.2
  100.7 1.3 copy-done.2
  102.0 2.3 bitcast_add_fusion.4
  104.3 1.7 copy-done.3
  106.0 1.2 constant_dynamic-slice_fusion.2
  108.4 2.0 bitcast_reduce_fusion.2
  111.1 1.3 copy-done.2
  112.4 2.3 bitcast_add_fusion.4
  114.7 1.7 copy-done.3
  116.4 1.2 constant_dynamic-slice_fusion.2
  118.8 2.0 bitcast_reduce_fusion.2
  121.5 1.3 copy-done.2
  122.7 2.3 bitcast_add_fusion.4
  125.1 1.7 copy-done.3
  126.8 1.2 constant_dynamic-slice_fusion.2
  129.2 2.0 bitcast_reduce_fusion.2
  131.8 1.3 copy-done.2
  133.1 2.3 bitcast_add_fusion.4
  135.4 1.7 copy-done.3
  137.1 1.2 constant_dynamic-slice_fusion.2
  139.5 2.0 bitcast_reduce_fusion.2
  142.2 1.3 copy-done.2
  143.5 2.3 bitcast_add_fusion.4
  145.8 1.7 copy-done.3
  148.2 1.4 reduce.7
  150.5 3.7 %all-to-all-start.2 = ((bf16[4,2,768]{2,1,0:T(2,128)(2,1)}), bf16[4,2,768]{2,1,0:T(2,128)(2,1)S(1)}, u32[]{:S(2)}, u32[]{:S(2)}) async-start(bf16[4,2,768]{2,1,0:T(2,128)(2,1)} %reshape.170), calls=%async_computation.2 | async-start | bytes 24576 | tf_op jit(solution)/shard_map/all_to_all | solution.py:132
  154.4 1.4 reduce.8
  156.6 2.3 all-to-all-done.2
  158.9 3.3 %all-to-all-start.1 = ((bf16[4,2,768]{2,1,0:T(2,128)(2,1)}), bf16[4,2,768]{2,1,0:T(2,128)(2,1)S(1)}, u32[]{:S(2)}, u32[]{:S(2)}) async-start(bf16[4,2,768]{2,1,0:T(2,128)(2,1)} %reshape.168), calls=%async_computation.1 | async-start | bytes 24576 | tf_op jit(solution)/shard_map/all_to_all | solution.py:129
  162.1 4.8 %copy.85 = bf16[512,12,128]{2,1,0:T(8,128)(2,1)} copy(f32[512,12,128]{0,2,1:T(8,128)} %get-tuple-element.37) | data formatting | bytes 4718592 | tf_op jit(solution)/shard_map/while | solution.py:127
  166.9 4.2 %all-to-all-start = ((bf16[1,512,12,128]{3,2,0,1:T(8,128)(2,1)}), bf16[1,512,12,128]{3,2,0,1:T(8,128)(2,1)S(1)}, u32[]{:S(2)}, u32[]{:S(2)}) async-start(bf16[1,512,12,128]{3,2,0,1:T(8,128)(2,1)} %bitcast.69), calls=%async_computation | async-start | bytes 4194304 | tf_op jit(solution)/shard_map/all_to_all | solution.py:135
  173.7 21.1 %all-to-all-done = bf16[1,512,12,128]{3,2,0,1:T(8,128)(2,1)S(1)} async-done(((bf16[1,512,12,128]{3,2,0,1:T(8,128)(2,1)}), bf16[1,512,12,128]{3,2,0,1:T(8,128)(2,1)S(1)}, u32[]{:S(2)}, u32[]{:S(2)}) %all-to-all-start) | async-done | bytes 1572896 | tf_op jit(solution)/shard_map/all_to_all | solution.py:135
  194.8 1.5 fusion.13
  197.1 3.4 %fusion.16 = f32[128,64]{0,1:T(8,128)S(1)} fusion(bf16[1536,64]{0,1:T(8,128)(2,1)} %param.21, f32[128,1536]{1,0:T(8,128)S(1)} %copy-done.6, bf16[128,1536]{0,1:T(8,128)(2,1)S(1)} %bitcast.122, bf16[1536,1536]{1,0:T(8,128)(2,1)} %param.20, f32[1536]{0:T(1024)S(1)} %get-tuple-element.125), kind=kOutput, calls=%fused_computation.34 | convolution fusion | flops 629735424 | bytes 6133760 | tf_op jit(solution)/shard_map/dot_general | solution.py:144
  200.6 1.3 collective-permute-start
  201.9 28.7 %psum.7 = bf16[64,128]{1,0:T(8,128)(2,1)S(1)} all-reduce(bf16[64,128]{1,0:T(8,128)(2,1)S(1)} %get-tuple-element.117), channel_id=1, replica_groups=mesh['queue'=8,'tok'=4] {'queue'}, use_global_device_ids=true, to_apply=%region_13.14 | all-reduce | flops 8192 | bytes 32768 | tf_op jit(solution)/shard_map/psum | solution.py:17
  (144 shorter events, 28.8 us)
Async XLA Ops:
  7.2 4.2 %copy-start = (bf16[64,1536]{1,0:T(8,128)(2,1)S(1)}, bf16[64,1536]{1,0:T(8,128)(2,1)}, u32[]{:S(2)}) copy-start(bf16[64,1536]{1,0:T(8,128)(2,1)} %param.15) | copy-start | bytes 589828
  7.2 54.1 %all-gather.2.cloned.1.call-start = ((), (), s32[]{:S(2)}) async-start(), calls=%async_computation.3 | async-start | bytes 1966080 | tf_op jit(solution)/shard_map/all_gather | solution.py:120
  11.8 3.6 %copy-start.5 = (f32[128,1536]{1,0:T(8,128)}, f32[128,1536]{1,0:T(8,128)S(1)}, u32[]{:S(2)}) copy-start(f32[128,1536]{1,0:T(8,128)S(1)} %get-tuple-element.135) | copy-start | bytes 2359300
  11.8 3.6 %copy-start.11 = (f32[1536]{0:T(1024)S(1)}, f32[1536]{0:T(1024)}, u32[]{:S(2)}) copy-start(f32[1536]{0:T(1024)} %param.18) | copy-start | bytes 18436
  12.0 18.8 %copy-start.7 = (f32[32,3,1536]{2,0,1:T(8,128)S(1)}, f32[32,3,1536]{2,0,1:T(8,128)}, u32[]{:S(2)}) copy-start(f32[32,3,1536]{2,0,1:T(8,128)} %param.16) | copy-start | bytes 1769476
  12.0 18.8 %copy-start.13 = (s32[8]{0:T(128)S(1)}, s32[8]{0:T(128)}, u32[]{:S(2)}) copy-start(s32[8]{0:T(128)} %param.13) | copy-start | bytes 100
  31.2 3.3 %slice-start = ((s8[14155776]{0:T(1024)(128)(4,1)}), s8[4194304]{0:T(1024)(128)(4,1)S(1)}, s32[]{:S(2)}) async-start(s8[14155776]{0:T(1024)(128)(4,1)} %bitcast.129), calls=%async_computation.4 | async-start | bytes 8388608
  31.2 3.5 %slice-start.1 = ((s8[14155776]{0:T(1024)(128)(4,1)}), s8[4194304]{0:T(1024)(128)(4,1)S(1)}, s32[]{:S(2)}) async-start(s8[14155776]{0:T(1024)(128)(4,1)} %bitcast.129), calls=%async_computation.5 | async-start | bytes 8388608
  32.3 3.8 %slice-start.2 = ((s8[14155776]{0:T(1024)(128)(4,1)}), s8[4194304]{0:T(1024)(128)(4,1)S(1)}, s32[]{:S(2)}) async-start(s8[14155776]{0:T(1024)(128)(4,1)} %bitcast.129), calls=%async_computation.6 | async-start | bytes 8388608
  33.1 3.4 %slice-start.3 = ((s8[14155776]{0:T(1024)(128)(4,1)}), s8[1572864]{0:T(1024)(128)(4,1)S(1)}, s32[]{:S(2)}) async-start(s8[14155776]{0:T(1024)(128)(4,1)} %bitcast.129), calls=%async_computation.7 | async-start | bytes 3145728
  48.8 8.2 %copy-start.4 = (f32[1024,3072]{1,0:T(8,128)S(1)}, f32[1024,3072]{1,0:T(8,128)}, u32[]{:S(2)}) copy-start(f32[1024,3072]{1,0:T(8,128)} %fusion.8) | copy-start | bytes 37748740
  52.2 4.9 %copy-start.12 = (f32[1536]{0:T(1024)S(1)}, f32[1536]{0:T(1024)}, u32[]{:S(2)}) copy-start(f32[1536]{0:T(1024)} %param.19) | copy-start | bytes 18436
  69.0 1.9 copy-start.2
  73.2 1.7 copy-start.3
  79.4 1.9 copy-start.2
  83.6 1.7 copy-start.3
  89.8 1.9 copy-start.2
  94.0 1.7 copy-start.3
  100.1 1.9 copy-start.2
  104.3 1.7 copy-start.3
  110.5 1.9 copy-start.2
  114.7 1.7 copy-start.3
  120.8 1.9 copy-start.2
  125.1 1.7 copy-start.3
  131.2 1.9 copy-start.2
  135.4 1.7 copy-start.3
  141.6 1.9 copy-start.2
  145.8 1.7 copy-start.3
  150.5 8.4 %all-to-all-start.2 = ((bf16[4,2,768]{2,1,0:T(2,128)(2,1)}), bf16[4,2,768]{2,1,0:T(2,128)(2,1)S(1)}, u32[]{:S(2)}, u32[]{:S(2)}) async-start(bf16[4,2,768]{2,1,0:T(2,128)(2,1)} %reshape.170), calls=%async_computation.2 | async-start | bytes 24576 | tf_op jit(solution)/shard_map/all_to_all | solution.py:132
  158.9 8.1 %all-to-all-start.1 = ((bf16[4,2,768]{2,1,0:T(2,128)(2,1)}), bf16[4,2,768]{2,1,0:T(2,128)(2,1)S(1)}, u32[]{:S(2)}, u32[]{:S(2)}) async-start(bf16[4,2,768]{2,1,0:T(2,128)(2,1)} %reshape.168), calls=%async_computation.1 | async-start | bytes 24576 | tf_op jit(solution)/shard_map/all_to_all | solution.py:129
  166.9 27.8 %all-to-all-start = ((bf16[1,512,12,128]{3,2,0,1:T(8,128)(2,1)}), bf16[1,512,12,128]{3,2,0,1:T(8,128)(2,1)S(1)}, u32[]{:S(2)}, u32[]{:S(2)}) async-start(bf16[1,512,12,128]{3,2,0,1:T(8,128)(2,1)} %bitcast.69), calls=%async_computation | async-start | bytes 4194304 | tf_op jit(solution)/shard_map/all_to_all | solution.py:135
  171.1 26.0 %copy-start.6 = (f32[128,1536]{1,0:T(8,128)S(1)}, f32[128,1536]{1,0:T(8,128)}, u32[]{:S(2)}) copy-start(f32[128,1536]{1,0:T(8,128)} %copy-done.5) | copy-start | bytes 2359300
  194.8 37.0 %copy-start.1 = (bf16[64,1536]{1,0:T(8,128)(2,1)S(1)}, bf16[64,1536]{1,0:T(8,128)(2,1)}, u32[]{:S(2)}) copy-start(bf16[64,1536]{1,0:T(8,128)(2,1)} %param.15) | copy-start | bytes 589828
  196.3 4.2 %copy-start.9 = (f32[1,128,64]{1,2,0:T(8,128)S(1)}, f32[1,128,64]{1,2,0:T(8,128)}, u32[]{:S(2)}) copy-start(f32[1,128,64]{1,2,0:T(8,128)} %param.12) | copy-start | bytes 98308
  196.3 34.8 %copy-start.10 = (f32[128,64]{0,1:T(8,128)S(1)}, f32[128,64]{0,1:T(8,128)}, u32[]{:S(2)}) copy-start(f32[128,64]{0,1:T(8,128)} %param.14) | copy-start | bytes 98308
  200.5 31.2 %copy-start.8 = (f32[128,64]{0,1:T(8,128)}, f32[128,64]{0,1:T(8,128)S(1)}, u32[]{:S(2)}) copy-start(f32[128,64]{0,1:T(8,128)S(1)} %fusion.16) | copy-start | bytes 98308
  200.6 30.6 %collective-permute-start = (bf16[128,64]{0,1:T(8,128)(2,1)S(1)}, bf16[128,64]{0,1:T(8,128)(2,1)S(1)}, u32[]{:S(2)}, u32[]{:S(2)}) collective-permute-start(bf16[128,64]{0,1:T(8,128)(2,1)S(1)} %get-tuple-element.118), channel_id=1, source_target_pairs={{4,0},{8,4},{12,8},{16,12},{20,16},{24,20},{28,24},{5,1},{9,5},{13... | collective-permute-start | bytes 49160 | tf_op jit(solution)/shard_map/ppermute | solution.py:12
Sparse Core Ops, SparseCore 0:
  16.4 33.5 all-gather.1
where the time goes:
time: 240 us; the launch traced here: 239 us
  local copies, waits for them, and re-layouts  63.4 us (26%)
  matrix products  56.7 us (24%)
  blocking collectives  43.2 us (18%)
  waiting for transfers between devices  23.3 us (10%)
  other arithmetic  23.2 us (10%)
  between operations  15.7 us (7%)
  starting transfers between devices  12.4 us (5%)
    psum x1, blocking collectives, spread(): return lax.psum(jnp.where(mine, value, jnp.zeros_like(value)), axis)  28.7 us
    while x40, local copies, waits for them, and re-layouts  23.5 us
    all_to_all x1, waiting for transfers between devices, per_device(): lax.all_to_all(state[2][None].astype(jnp.bfloat16), 'tok', split_axis=1,...  21.1 us
    dot_general x8, matrix products, fold_keys(): jnp.einsum('rhk,khd->rhd', weights.astype(jnp.bfloat16), value_rows, pref...  18.6 us
    dot_general x8, matrix products, fold_keys(): jnp.einsum('rhd,khd->rhk', queries, key_rows, preferred_element_type=jnp....  16.4 us
    all_gather x1, blocking collectives, per_device(): lax.all_gather(latent.astype(jnp.bfloat16), 'queue', axis=0, tiled=True)  14.5 us
    dynamic_slice x16, local copies, waits for them, and re-layouts, per_device(): lax.scan(step_frame, fresh_state(frame_rows, head_count, head_size), ever...  12.4 us
    dot_general x1, matrix products, key_value_rows(): jnp.dot(normed, qkv_weight[:, feature:], preferred_element_type=jnp.float32)  12.4 us
  transfers between devices with their start and end apart: 5, of which 2 were waited for; matrix products, arithmetic and copies ran while one was open for 15% of the time, Pallas kernels for 0%

commit v1 on v0

v1 whole, which is shorter than its diff:
```python
import functools
import math

import jax
import jax.numpy as jnp
from jax import lax
from jax.experimental import pallas as pl
from jax.experimental.pallas import tpu as pltpu
from jax.sharding import PartitionSpec as P

HEAD_DIM = 128
EPS = 1e-06
UROWS = 80
GROUPS = 4
CHUNK = 256
EXACT = lax.Precision.HIGHEST
VMEM = pl.BlockSpec(memory_space=pltpu.VMEM)
SMEM = pl.BlockSpec(memory_space=pltpu.SMEM)
ANY = pl.BlockSpec(memory_space=pl.ANY)


def nt_dot(a, b, **kw):
    return lax.dot_general(a, b, (((1,), (1,)), ((), ())), preferred_element_type=jnp.float32, **kw)


def tn_dot(a, b, **kw):
    return lax.dot_general(a, b, (((0,), (0,)), ((), ())), preferred_element_type=jnp.float32, **kw)


def nn_dot(a, b, **kw):
    return jnp.dot(a, b, preferred_element_type=jnp.float32, **kw)


def frame_at(place, mine, frames):
    half = frames // 2
    return mine ^ (((place % half) << 1) | (place // half))


def place_of(frame, mine, frames):
    apart = mine ^ frame
    return (apart >> 1) + (apart & 1) * (frames // 2)


def query_frames(mine, frames):
    first = mine - (mine & 1)
    return (first, first + 1, jnp.minimum(first + 2, frames - 1), 0 * first)


def tables_kernel(
    frames,
    step_ref,
    time_ref,
    patch_ref,
    qkv_ref,
    q_gain_ref,
    k_gain_ref,
    out_ref,
    head_ref,
    ak_ref,
    av_ref,
    aq_ref,
    hk_ref,
    hq_ref,
    gram_ref,
    mix_ref,
    skip_ref,
    lhs,
    lhs_q,
    head_g,
    wbuf,
    obuf,
    sems,
):
    feature = patch_ref.shape[1]
    channels = patch_ref.shape[0]
    half = ak_ref.shape[2]
    mine = lax.axis_index("queue")
    core = mine & 1
    per_half = half // CHUNK
    whole = feature // CHUNK

    def column(j):
        return pl.multiple_of(lax.rem(core * half + j * CHUNK, feature), CHUNK)

    def fetch(slot, base, j):
        at = pl.multiple_of(base + column(j), CHUNK)
        return pltpu.make_async_copy(qkv_ref.at[:, pl.ds(at, CHUNK)], wbuf.at[slot], sems.at[slot])

    k_slot, v_slot, q_slot = 0, whole, whole + per_half
    for j in range(whole):
        fetch(k_slot + j, feature, j).start()
    for j in range(per_half):
        fetch(v_slot + j, 2 * feature, j).start()
    for j in range(whole):
        fetch(q_slot + j, 0, j).start()
    last = whole + per_half + whole
    out_copy = pltpu.make_async_copy(
        out_ref.at[pl.ds(pl.multiple_of(core * half, half), half), :], obuf, sems.at[last]
    )
    out_copy.start()

    patch = patch_ref[...].astype(jnp.float32)
    centred = patch - jnp.mean(patch, axis=-1, keepdims=True)
    gram_ref[...] = nt_dot(centred, centred, precision=EXACT) / feature
    rest = UROWS - channels
    first_row = lax.broadcasted_iota(jnp.int32, (rest, feature), 0) == 0
    for place in range(frames):
        level = step_ref[frame_at(place, mine, frames)]
        shift = time_ref[0, pl.ds(level, 1), :]
        scale = time_ref[1, pl.ds(level, 1), :]
        lhs[place * UROWS : place * UROWS + channels, :] = (centred * (1.0 + scale)).astype(jnp.bfloat16)
        lhs[place * UROWS + channels : (place + 1) * UROWS, :] = jnp.where(
            first_row, jnp.broadcast_to(shift, (rest, feature)), 0.0
        ).astype(jnp.bfloat16)
    head = head_ref[...].astype(jnp.float32)
    for g, frame in enumerate(query_frames(mine, frames)):
        place = place_of(frame, mine, frames)
        lhs_q[g * UROWS : (g + 1) * UROWS, :] = lhs[pl.ds(pl.multiple_of(place * UROWS, 16), UROWS), :]
        gate = time_ref[2, pl.ds(step_ref[frame], 1), :]
        head_g[g * channels : (g + 1) * channels, :] = (head * gate).astype(jnp.bfloat16)
    skip_ref[...] = nt_dot(head_ref[...], patch_ref[...])

    hk_ref[...] = jnp.zeros_like(hk_ref)
    hq_ref[...] = jnp.zeros_like(hq_ref)

    def gained(slot, base, j, rows_ref, count, gain_ref, table_ref, square_ref, keep):
        fetch(slot + j, base, j).wait()
        made = nn_dot(rows_ref[...], wbuf[slot + j])
        made_lo = made.astype(jnp.bfloat16)
        for f in range(count):
            block = made_lo[f * UROWS : (f + 1) * UROWS, :]
            square_ref[f] += nt_dot(block, block)
        if keep:
            table = (made * gain_ref[:, pl.ds(column(j), CHUNK)]).astype(jnp.bfloat16)
            at = pl.multiple_of(j * CHUNK, CHUNK)
            for f in range(count):
                table_ref[f, :, pl.ds(at, CHUNK)] = table[f * UROWS : (f + 1) * UROWS, :]

    def k_step(keep):
        def run(j, carry):
            gained(k_slot, feature, j, lhs, frames, k_gain_ref, ak_ref, hk_ref, keep)
            return carry

        return run

    def q_step(keep):
        def run(j, carry):
            gained(q_slot, 0, j, lhs_q, GROUPS, q_gain_ref, aq_ref, hq_ref, keep)
            return carry

        return run

    def v_step(j, carry):
        fetch(v_slot + j, 2 * feature, j).wait()
        made = nn_dot(lhs[...], wbuf[v_slot + j]).astype(jnp.bfloat16)
        at = pl.multiple_of(j * CHUNK, CHUNK)
        for f in range(frames):
            av_ref[f, :, pl.ds(at, CHUNK)] = made[f * UROWS : (f + 1) * UROWS, :]
        return carry

    lax.fori_loop(0, per_half, k_step(True), 0)
    lax.fori_loop(per_half, whole, k_step(False), 0)
    lax.fori_loop(0, per_half, v_step, 0)
    lax.fori_loop(0, per_half, q_step(True), 0)
    lax.fori_loop(per_half, whole, q_step(False), 0)
    out_copy.wait()
    mixed = nt_dot(head_g[...], obuf[...]).astype(jnp.bfloat16)
    for g in range(GROUPS):
        mix_ref[g] = mixed[g * channels : (g + 1) * channels, :]


def normed_rows(z, gram, square, feature):
    var = jnp.sum(z * nn_dot(gram, z, precision=EXACT), axis=0, keepdims=True)
    scaled = z * lax.rsqrt(var + EPS)
    tail = (UROWS - z.shape[0], z.shape[1])
    ones = (lax.broadcasted_iota(jnp.int32, tail, 0) == 0).astype(jnp.float32)
    rows = jnp.concatenate([scaled, ones], axis=0)
    mean_sq = jnp.sum(rows * nn_dot(square, rows, precision=EXACT), axis=0, keepdims=True) / feature
    return rows, lax.rsqrt(mean_sq + EPS)


def attend_kernel(
    frames,
    feature,
    z_ref,
    ak_ref,
    av_ref,
    aq_ref,
    hk_ref,
    hq_ref,
    gram_ref,
    mix_ref,
    skip_ref,
    part_ref,
    q_s,
    m_s,
    l_s,
    o_s,
):
    mine = lax.axis_index("queue")
    core = mine & 1
    heads = q_s.shape[0]
    tok = z_ref.shape[3]
    blocks = z_ref.shape[0]
    step = min(blocks, 4)
    gram = gram_ref[...]
    scaling = HEAD_DIM ** (-0.5) * math.log2(math.e)
    for g, frame in enumerate(query_frames(mine, frames)):
        z = z_ref[0, place_of(frame, mine, frames)].astype(jnp.float32)
        rows, factor = normed_rows(z, gram, hq_ref[g], feature)
        made = tn_dot((rows * (factor * scaling)).astype(jnp.bfloat16), aq_ref[g]).astype(jnp.bfloat16)
        for h in range(heads):
            q_s[h, g * tok : (g + 1) * tok, :] = made[:, h * HEAD_DIM : (h + 1) * HEAD_DIM]
    m_s[...] = jnp.full_like(m_s, -1e30)
    l_s[...] = jnp.zeros_like(l_s)
    o_s[...] = jnp.zeros_like(o_s)

    def portion(i, carry):
        place = lax.rem(i, frames)
        base = lax.div(i, frames) * step
        z = jnp.concatenate([z_ref[base + b, place] for b in range(step)], axis=1).astype(jnp.float32)
        rows, factor = normed_rows(z, gram, hk_ref[place], feature)
        keys = tn_dot((rows * factor).astype(jnp.bfloat16), ak_ref[place]).astype(jnp.bfloat16)
        values = tn_dot(rows.astype(jnp.bfloat16), av_ref[place]).astype(jnp.bfloat16)
        for h in range(heads):
            span = slice(h * HEAD_DIM, (h + 1) * HEAD_DIM)
            scores = nt_dot(q_s[h], keys[:, span])
            before = m_s[h]
            top = jnp.maximum(before, jnp.max(scores, axis=-1, keepdims=True))
            m_s[h] = top
            alpha = jnp.exp2(before - top)
            weights = jnp.exp2(scores - top[:, :1])
            folded = weights[:, :HEAD_DIM]
            for b in range(1, scores.shape[1] // HEAD_DIM):
                folded = folded + weights[:, b * HEAD_DIM : (b + 1) * HEAD_DIM]
            l_s[h] = l_s[h] * alpha + folded
            o_s[h] = o_s[h] * alpha + nn_dot(weights.astype(jnp.bfloat16), values[:, span])
        return carry

    lax.fori_loop(0, frames * (blocks // step), portion, 0)

    lead = jnp.where(core == 0, 1.0, 0.0)
    totals = []
    for g, frame in enumerate(query_frames(mine, frames)):
        z = z_ref[0, place_of(frame, mine, frames)].astype(jnp.float32)
        totals.append(nn_dot(skip_ref[...], z, precision=EXACT) * lead)
    for h in range(heads):
        done = (o_s[h] / jnp.sum(l_s[h], axis=-1, keepdims=True)).astype(jnp.bfloat16)
        for g in range(GROUPS):
            mix = mix_ref[g, :, h * HEAD_DIM : (h + 1) * HEAD_DIM]
            totals[g] = totals[g] + nt_dot(mix, done[g * tok : (g + 1) * tok, :])
    for g in range(GROUPS):
        part_ref[g] = totals[g]


def swapped(value, axis, bit):
    peers = lax.axis_size(axis)
    return lax.ppermute(value, axis, [(i, i ^ bit) for i in range(peers)])


def per_device(
    latents,
    step_index,
    tail_noise,
    patch_weight,
    time_table,
    qkv_weight,
    q_gain,
    k_gain,
    out_weight,
    head_weight,
):
    channels, feature = patch_weight.shape
    levels = time_table.shape[0]
    frames = lax.axis_size("queue")
    peers = lax.axis_size("tok")
    half = feature // 2
    heads = half // HEAD_DIM
    mine = lax.axis_index("queue")
    latent = latents[0].T
    tok = latent.shape[1]
    f32, bf16 = jnp.float32, jnp.bfloat16

    shapes = (
        ((frames, UROWS, half), bf16),
        ((frames, UROWS, half), bf16),
        ((GROUPS, UROWS, half), bf16),
        ((frames, UROWS, UROWS), f32),
        ((GROUPS, UROWS, UROWS), f32),
        ((channels, channels), f32),
        ((GROUPS, channels, half), bf16),
        ((channels, channels), f32),
    )
    slots = 2 * (feature // CHUNK) + half // CHUNK
    tables = pl.pallas_call(
        functools.partial(tables_kernel, frames),
        out_shape=[jax.ShapeDtypeStruct(*s) for s in shapes],
        in_specs=[SMEM, VMEM, VMEM, ANY, VMEM, VMEM, ANY, VMEM],
        out_specs=[VMEM] * len(shapes),
        scratch_shapes=[
            pltpu.VMEM((frames * UROWS, feature), bf16),
            pltpu.VMEM((GROUPS * UROWS, feature), bf16),
            pltpu.VMEM((GROUPS * channels, feature), bf16),
            pltpu.VMEM((slots, feature, CHUNK), bf16),
            pltpu.VMEM((half, feature), bf16),
            pltpu.SemaphoreType.DMA((slots + 1,)),
        ],
        compiler_params=pltpu.CompilerParams(vmem_limit_bytes=48 << 20),
        cost_estimate=pl.CostEstimate(flops=6 * 10**9, bytes_accessed=18 * 10**6, transcendentals=0),
        name="tables",
    )(
        step_index,
        time_table.transpose(1, 0, 2),
        patch_weight,
        qkv_weight,
        q_gain[None],
        k_gain[None],
        out_weight,
        head_weight.T,
    )

    known = latent.astype(bf16)[None]
    bit = 2
    while bit < frames:
        known = jnp.concatenate([known, swapped(known, "queue", bit)], axis=0)
        bit *= 2
    known = jnp.concatenate([known, swapped(known, "queue", 1)], axis=0)
    gathered = known[None]
    bit = 1
    while bit < peers:
        gathered = jnp.concatenate([gathered, swapped(gathered, "tok", bit)], axis=0)
        bit *= 2

    rows = GROUPS * tok
    part = pl.pallas_call(
        functools.partial(attend_kernel, frames, feature),
        out_shape=jax.ShapeDtypeStruct((GROUPS, channels, tok), f32),
        in_specs=[VMEM] * 9,
        out_specs=VMEM,
        scratch_shapes=[
            pltpu.VMEM((heads, rows, HEAD_DIM), bf16),
            pltpu.VMEM((heads, rows, HEAD_DIM), f32),
            pltpu.VMEM((heads, rows, HEAD_DIM), f32),
            pltpu.VMEM((heads, rows, HEAD_DIM), f32),
        ],
        compiler_params=pltpu.CompilerParams(vmem_limit_bytes=48 << 20),
        cost_estimate=pl.CostEstimate(flops=30 * 10**9, bytes_accessed=8 * 10**6, transcendentals=13 * 10**6),
        name="attend",
    )(gathered, *tables)

    core = mine & 1
    share = channels // frames
    clean = lax.dynamic_slice_in_dim(part[3], share * mine, share, 0)
    clean_other = lax.dynamic_slice_in_dim(part[3], share * (mine ^ 1), share, 0)
    kept = jnp.concatenate([lax.dynamic_slice_in_dim(part, core, 2, 0).reshape(2 * channels, tok), clean], 0)
    given = jnp.concatenate(
        [lax.dynamic_slice_in_dim(part, 1 - core, 2, 0).reshape(2 * channels, tok), clean_other], 0
    )
    total = kept + swapped(given, "queue", 1)
    velocity = total[:channels]

    def drop(frame):
        now = step_index[frame]
        before = jnp.where(frame > 0, step_index[jnp.maximum(frame - 1, 0)], -1)
        return ((before.astype(f32) + 1.0) - (now.astype(f32) + 1.0)) / levels

    following = jnp.minimum(mine + 1, frames - 1)
    there = lax.dynamic_index_in_dim(known, place_of(following, mine, frames), 0, False).astype(f32)
    arrived = there + drop(following) * total[channels : 2 * channels]
    queue_next = jnp.where(mine == frames - 1, tail_noise.T, arrived)
    oldest = lax.dynamic_index_in_dim(known, place_of(0, mine, frames), 0, False).astype(f32)
    oldest = lax.dynamic_slice_in_dim(oldest, share * mine, share, 0)
    leaving = oldest + drop(jnp.int32(0)) * total[2 * channels :]
    return (velocity.T[None], queue_next.T[None], leaving)


def solution(mesh):
    placed = (P("queue", "tok", None), P(), P("tok", None), P(), P(), P(), P(), P(), P(), P())
    return jax.shard_map(
        per_device,
        mesh=mesh,
        in_specs=placed,
        out_specs=(P("queue", "tok", None), P("queue", "tok", None), P("queue", "tok")),
        check_vma=False,
    )
```

time: 240 us -> 94.1 us (0.39)
  Pallas kernels: 0 us -> 62.2 us
  local copies, waits for them, and re-layouts: 63.4 us -> 5.62 us
  matrix products: 56.7 us -> 0 us
  blocking collectives: 43.2 us -> 0 us
  other arithmetic: 23.2 us -> 5.9 us
  waiting for transfers between devices: 23.3 us -> 7.27 us
  between operations: 15.7 us -> 2.74 us
  starting transfers between devices: 12.4 us -> 9.83 us
    pallas_call x0 -> x2, Pallas kernels: none -> 62.2 us  [the longest x1 47.7 us: per_device(): pl.pallas_call(functools.partial(attend_kernel, frames, feature), out_sha...]
    dot_general x23 -> x0, matrix products: 56.7 us -> none  [the longest x8 18.6 us: fold_keys(): jnp.einsum('rhk,khd->rhd', weights.astype(jnp.bfloat16), value_rows, pref...]
    psum x1 -> x0, blocking collectives: 28.7 us -> none  [spread(): return lax.psum(jnp.where(mine, value, jnp.zeros_like(value)), axis)]
    while x41 -> x0, local copies, waits for them, and re-layouts: 28.3 us -> none
    all_to_all x3 -> x0, waiting for transfers between devices: 23.3 us -> none  [the longest x1 21.1 us: per_device(): lax.all_to_all(state[2][None].astype(jnp.bfloat16), 'tok', split_axis=1,...]
    all_gather x1 -> x0, blocking collectives: 14.5 us -> none  [per_device(): lax.all_gather(latent.astype(jnp.bfloat16), 'queue', axis=0, tiled=True)]
    dynamic_slice x17 -> x3, local copies, waits for them, and re-layouts: 13.8 us -> 0.63 us  [the longest x1 0.59 us: drop(): before = jnp.where(frame > 0, step_index[jnp.maximum(frame - 1, 0)], -1)]
    reduce_sum x13 -> x0, other arithmetic: 11.2 us -> none  [the longest x8 4.55 us: fold_keys(): run_sum = run_sum * factor + jnp.sum(weights, axis=-1)]
  transfers between devices with their start and end apart: 5 -> 6, of which waited for: 2 -> 4; matrix products, arithmetic and copies ran while one was open for 15% -> 2% of each run, Pallas kernels for 0% -> 16%
where the time goes in v1:
time: 94.1 us; the launch traced here: 93.6 us
  Pallas kernels  62.2 us (66%)
  starting transfers between devices  9.83 us (10%)
  waiting for transfers between devices  7.27 us (8%)
  other arithmetic  5.9 us (6%)
  local copies, waits for them, and re-layouts  5.62 us (6%)
  between operations  2.74 us (3%)
    pallas_call x1, Pallas kernels, per_device(): pl.pallas_call(functools.partial(attend_kernel, frames, feature), out_sha...  47.7 us
    pallas_call x1, Pallas kernels, per_device(): pl.pallas_call(functools.partial(tables_kernel, frames), out_shape=[jax.S...  14.6 us
    ppermute x6, starting transfers between devices, swapped(): return lax.ppermute(value, axis, [(i, i ^ bit) for i in range(peers)])  9.83 us
    ppermute x6, waiting for transfers between devices, swapped(): return lax.ppermute(value, axis, [(i, i ^ bit) for i in range(peers)])  7.27 us
    unnamed x12, local copies, waits for them, and re-layouts  3.58 us
  transfers between devices with their start and end apart: 6, of which 4 were waited for; matrix products, arithmetic and copies ran while one was open for 2% of the time, Pallas kernels for 16%

profile of v1, /device:TPU:0, one launch (start us, length us, event | category | flops | bytes accessed | tf_op | source)
XLA Modules:
  0.0 93.6 jit_solution(256600511565598708)
XLA Ops:
  0.6 0.8 convert_bitcast_fusion
  1.4 3.1 %collective-permute-start = (bf16[1,64,128]{2,1,0:T(8,128)(2,1)S(1)}, bf16[1,64,128]{2,1,0:T(8,128)(2,1)S(1)}, u32[]{:S(2)}, u32[]{:S(2)}) collective-permute-start(bf16[1,64,128]{2,1,0:T(8,128)(2,1)S(1)} %convert_bitcast_fusion), channel_id=1, source_target_pairs={{0,8},{4,12},{8,0},{12,4},{16,24},{20,28},{24,16},{28,20},{1,9},{5... | collective-permute-start | bytes 49160 | tf_op jit(solution)/shard_map/ppermute | solution.py:258
  4.4 1.7 %collective-permute-done = bf16[1,64,128]{2,1,0:T(8,128)(2,1)S(1)} collective-permute-done((bf16[1,64,128]{2,1,0:T(8,128)(2,1)S(1)}, bf16[1,64,128]{2,1,0:T(8,128)(2,1)S(1)}, u32[]{:S(2)}, u32[]{:S(2)}) %collective-permute-start) | collective-permute-done | bytes 16416 | tf_op jit(solution)/shard_map/ppermute | solution.py:258
  6.2 3.0 %collective-permute-start.1 = (bf16[2,64,128]{2,1,0:T(8,128)(2,1)S(1)}, bf16[2,64,128]{2,1,0:T(8,128)(2,1)S(1)}, u32[]{:S(2)}, u32[]{:S(2)}) collective-permute-start(bf16[2,64,128]{2,1,0:T(8,128)(2,1)S(1)} %pad_maximum_fusion.5), channel_id=1, source_target_pairs={{0,16},{4,20},{8,24},{12,28},{16,0},{20,4},{24,8},{28,12},{1,17},{... | collective-permute-start | bytes 98312 | tf_op jit(solution)/shard_map/ppermute | solution.py:258
  9.2 1.9 %collective-permute-done.1 = bf16[2,64,128]{2,1,0:T(8,128)(2,1)S(1)} collective-permute-done((bf16[2,64,128]{2,1,0:T(8,128)(2,1)S(1)}, bf16[2,64,128]{2,1,0:T(8,128)(2,1)S(1)}, u32[]{:S(2)}, u32[]{:S(2)}) %collective-permute-start.1) | collective-permute-done | bytes 32800 | tf_op jit(solution)/shard_map/ppermute | solution.py:258
  11.1 0.1 collective-permute-start.2
  11.2 1.2 %collective-permute-done.2 = bf16[4,64,128]{2,1,0:T(8,128)(2,1)S(1)} collective-permute-done((bf16[4,64,128]{2,1,0:T(8,128)(2,1)S(1)}, bf16[4,64,128]{2,1,0:T(8,128)(2,1)S(1)}, u32[]{:S(2)}, u32[]{:S(2)}) %collective-permute-start.2) | collective-permute-done | bytes 65568 | tf_op jit(solution)/shard_map/ppermute | solution.py:258
  12.4 0.7 pad_maximum_fusion.2
  13.1 1.8 %collective-permute-start.3 = (bf16[1,8,64,128]{3,2,1,0:T(8,128)(2,1)S(1)}, bf16[1,8,64,128]{3,2,1,0:T(8,128)(2,1)S(1)}, u32[]{:S(2)}, u32[]{:S(2)}) collective-permute-start(bf16[1,8,64,128]{3,2,1,0:T(8,128)(2,1)S(1)} %get-tuple-element.20), channel_id=1, source_target_pairs={{0,1},{1,0},{2,3},{3,2},{4,5},{5,4},{6,7},{7,6},{8,9},{9,8},{10,11... | collective-permute-start | bytes 393224 | tf_op jit(solution)/shard_map/ppermute | solution.py:258
  14.9 0.7 broadcast_in_dim.20.q_gain_ref
  15.6 0.7 broadcast_in_dim.21.k_gain_ref
  16.3 2.4 %collective-permute-done.3 = bf16[1,8,64,128]{3,2,1,0:T(8,128)(2,1)S(1)} collective-permute-done((bf16[1,8,64,128]{3,2,1,0:T(8,128)(2,1)S(1)}, bf16[1,8,64,128]{3,2,1,0:T(8,128)(2,1)S(1)}, u32[]{:S(2)}, u32[]{:S(2)}) %collective-permute-start.3) | collective-permute-done | bytes 131104 | tf_op jit(solution)/shard_map/ppermute | solution.py:258
  18.7 0.0 copy-start.5
  18.7 0.7 pad_maximum_fusion.1
  19.5 1.8 %collective-permute-start.4 = (bf16[2,8,64,128]{3,2,1,0:T(8,128)(2,1)}, bf16[2,8,64,128]{3,2,1,0:T(8,128)(2,1)}, u32[]{:S(2)}, u32[]{:S(2)}) collective-permute-start(bf16[2,8,64,128]{3,2,1,0:T(8,128)(2,1)} %pad_maximum_fusion.1), channel_id=1, source_target_pairs={{0,2},{1,3},{2,0},{3,1},{4,6},{5,7},{6,4},{7,5},{8,10},{9,11},{10,... | collective-permute-start | bytes 786440 | tf_op jit(solution)/shard_map/ppermute | solution.py:258
  21.3 0.0 copy-done.5
  21.3 0.0 copy-start
  21.3 0.7 copy-done
  21.9 0.0 copy-start.2
  21.9 1.1 %copy-done.2 = f32[32,3,1536]{2,0,1:T(8,128)S(1)} copy-done((f32[32,3,1536]{2,0,1:T(8,128)S(1)}, f32[32,3,1536]{2,0,1:T(8,128)}, u32[]{:S(2)}) %copy-start.2) | copy-done | bytes 589848
  23.0 0.0 copy-start.3
  23.0 0.9 copy-done.3
  23.9 0.0 copy-start.4
  23.9 0.9 copy-done.4
  24.8 14.6 %tables.1 = (bf16[8,80,768]{2,1,0:T(8,128)(2,1)S(1)}, bf16[8,80,768]{2,1,0:T(8,128)(2,1)S(1)}, bf16[4,80,768]{2,1,0:T(8,128)(2,1)S(1)}, f32[8,80,80]{2,1,0:T(8,1...) custom-call(s32[8]{0:T(128)S(1)} %copy-done, ...), custom_call_target="tpu_custom_call" | custom-call | flops 6000000000 | bytes 18000000 | tf_op jit(solution)/shard_map/tables/pallas_call | solution.py:295
  39.5 0.0 collective-permute-done.4
  39.5 1.0 %pad_maximum_fusion.z_ref = bf16[4,8,64,128]{3,2,1,0:T(8,128)(2,1)S(1)} fusion(bf16[2,8,64,128]{3,2,1,0:T(8,128)(2,1)} %collective-permute-done.4, bf16[1,8,64,128]{3,2,1,0:T(8,128)(2,1)} %copy-done.5, bf16[1,8,64,128]{3,2,1,0:T(8,128)(2,1)S(1)} %get-tuple-element.20), kind=kLoop, calls=%fused_computation | loop fusion | flops 524288 | bytes 1048576 | tf_op jit(solution)/shard_map/concatenate | solution.py:331
  40.5 0.0 copy-start.1
  40.5 47.7 %attend.1 = f32[4,64,128]{2,1,0:T(8,128)S(1)} custom-call(bf16[4,8,64,128]{3,2,1,0:T(8,128)(2,1)S(1)} %pad_maximum_fusion.z_ref, bf16[8,80,768]{2,1,0:T(8,128)(2,1)S(1)} %get-tuple-element.11.ak_ref, bf16[8,80,768]{2,1,0:T(8,128)(2,1)S(1)} %get-tuple-element.12.av_ref, bf16[4,80,768]{2,1,0:T(8,128)(2,1)S(1)} %get-tuple-element.13.aq_ref, ...), custom_call_target="tpu_custom_call" | custom-call | flops 30000001024 | bytes 8000000 | tf_op jit(solution)/shard_map/attend/pallas_call | solution.py:335
  88.3 0.1 collective-permute-start.5
  88.3 0.0 copy-done.1
  88.3 0.6 fusion.5
  90.9 0.0 collective-permute-done.5
  90.9 1.3 %fusion.3 = f32[8,128]{1,0:T(8,128)} fusion(f32[136,128]{1,0:T(8,128)S(1)} %maximum_add_fusion, bf16[8,64,128]{2,1,0:T(8,128)(2,1)} %get-tuple-element.19, s32[]{:T(128)S(6)} %select_n.46, s32[]{:T(128)S(6)} %select_n.38, f32[]{:T(128)} %bitcast.21), kind=kLoop, calls=%fused_computation.14 | loop fusion | flops 3072 | bytes 10252 | tf_op jit(solution)/shard_map/add | solution.py:373
  92.2 1.4 %fusion.2 = (f32[1,128,64]{1,2,0:T(8,128)}, f32[1,128,64]{1,2,0:T(8,128)}) fusion(f32[136,128]{1,0:T(8,128)S(1)} %maximum_add_fusion, f32[128,64]{0,1:T(8,128)} %param.12, f32[]{:T(128)S(6)} %div.8, bf16[8,64,128]{2,1,0:T(8,128)(2,1)} %get-tuple-element.19, s32[]{:T(128)S(6)} %select_n.42, pred[]{:T(512)S(6)} %eq.3), kind=kLoop, calls=%fused_computation.9 | loop fusion | flops 32768 | bytes 180233 | tf_op jit(solution)/shard_map/broadcast_in_dim | solution.py:374
  (7 shorter events, 0.1 us)
Async XLA Ops:
  1.4 4.8 %collective-permute-start = (bf16[1,64,128]{2,1,0:T(8,128)(2,1)S(1)}, bf16[1,64,128]{2,1,0:T(8,128)(2,1)S(1)}, u32[]{:S(2)}, u32[]{:S(2)}) collective-permute-start(bf16[1,64,128]{2,1,0:T(8,128)(2,1)S(1)} %convert_bitcast_fusion), channel_id=1, source_target_pairs={{0,8},{4,12},{8,0},{12,4},{16,24},{20,28},{24,16},{28,20},{1,9},{5... | collective-permute-start | bytes 49160 | tf_op jit(solution)/shard_map/ppermute | solution.py:258
  6.2 4.9 %collective-permute-start.1 = (bf16[2,64,128]{2,1,0:T(8,128)(2,1)S(1)}, bf16[2,64,128]{2,1,0:T(8,128)(2,1)S(1)}, u32[]{:S(2)}, u32[]{:S(2)}) collective-permute-start(bf16[2,64,128]{2,1,0:T(8,128)(2,1)S(1)} %pad_maximum_fusion.5), channel_id=1, source_target_pairs={{0,16},{4,20},{8,24},{12,28},{16,0},{20,4},{24,8},{28,12},{1,17},{... | collective-permute-start | bytes 98312 | tf_op jit(solution)/shard_map/ppermute | solution.py:258
  11.1 1.3 %collective-permute-start.2 = (bf16[4,64,128]{2,1,0:T(8,128)(2,1)S(1)}, bf16[4,64,128]{2,1,0:T(8,128)(2,1)S(1)}, u32[]{:S(2)}, u32[]{:S(2)}) collective-permute-start(bf16[4,64,128]{2,1,0:T(8,128)(2,1)S(1)} %pad_maximum_fusion.4), channel_id=1, source_target_pairs={{0,4},{4,0},{8,12},{12,8},{16,20},{20,16},{24,28},{28,24},{1,5},{5... | collective-permute-start | bytes 196616 | tf_op jit(solution)/shard_map/ppermute | solution.py:258
  13.1 5.6 %collective-permute-start.3 = (bf16[1,8,64,128]{3,2,1,0:T(8,128)(2,1)S(1)}, bf16[1,8,64,128]{3,2,1,0:T(8,128)(2,1)S(1)}, u32[]{:S(2)}, u32[]{:S(2)}) collective-permute-start(bf16[1,8,64,128]{3,2,1,0:T(8,128)(2,1)S(1)} %get-tuple-element.20), channel_id=1, source_target_pairs={{0,1},{1,0},{2,3},{3,2},{4,5},{5,4},{6,7},{7,6},{8,9},{9,8},{10,11... | collective-permute-start | bytes 393224 | tf_op jit(solution)/shard_map/ppermute | solution.py:258
  18.7 2.5 %copy-start.5 = (bf16[1,8,64,128]{3,2,1,0:T(8,128)(2,1)}, bf16[1,8,64,128]{3,2,1,0:T(8,128)(2,1)S(1)}, u32[]{:S(2)}) copy-start(bf16[1,8,64,128]{3,2,1,0:T(8,128)(2,1)S(1)} %collective-permute-done.3) | copy-start | bytes 393220
  19.5 20.0 %collective-permute-start.4 = (bf16[2,8,64,128]{3,2,1,0:T(8,128)(2,1)}, bf16[2,8,64,128]{3,2,1,0:T(8,128)(2,1)}, u32[]{:S(2)}, u32[]{:S(2)}) collective-permute-start(bf16[2,8,64,128]{3,2,1,0:T(8,128)(2,1)} %pad_maximum_fusion.1), channel_id=1, source_target_pairs={{0,2},{1,3},{2,0},{3,1},{4,6},{5,7},{6,4},{7,5},{8,10},{9,11},{10,... | collective-permute-start | bytes 786440 | tf_op jit(solution)/shard_map/ppermute | solution.py:258
  21.3 0.7 copy-start
  21.9 1.1 %copy-start.2 = (f32[32,3,1536]{2,0,1:T(8,128)S(1)}, f32[32,3,1536]{2,0,1:T(8,128)}, u32[]{:S(2)}) copy-start(f32[32,3,1536]{2,0,1:T(8,128)} %param.14) | copy-start | bytes 1769476
  23.0 0.9 copy-start.3
  23.9 0.9 copy-start.4
  40.5 47.8 %copy-start.1 = (s32[8]{0:T(128)S(1)}, s32[8]{0:T(128)}, u32[]{:S(2)}) copy-start(s32[8]{0:T(128)} %step_ref.1) | copy-start | bytes 100
  88.3 2.6 %collective-permute-start.5 = (f32[136,128]{1,0:T(8,128)S(1)}, f32[136,128]{1,0:T(8,128)S(1)}, u32[]{:S(2)}, u32[]{:S(2)}) collective-permute-start(f32[136,128]{1,0:T(8,128)S(1)} %pad_maximum_fusion.3), channel_id=1, source_target_pairs={{0,4},{4,0},{8,12},{12,8},{16,20},{20,16},{24,28},{28,24},{1,5},{5... | collective-permute-start | bytes 208904 | tf_op jit(solution)/shard_map/ppermute | solution.py:258

commit v2 on v0

v2 whole, which is shorter than its diff:
```python
import functools
import math

import jax
import jax.numpy as jnp
from jax import lax
from jax.experimental import pallas as pl
from jax.experimental.pallas import tpu as pltpu
from jax.sharding import PartitionSpec as P

HEAD_DIM = 128
EPS = 1e-06
UROWS = 80
GROUPS = 4
CHUNK = 256
EXACT = lax.Precision.HIGHEST
VMEM = pl.BlockSpec(memory_space=pltpu.VMEM)
SMEM = pl.BlockSpec(memory_space=pltpu.SMEM)
ANY = pl.BlockSpec(memory_space=pl.ANY)


def nt_dot(a, b, **kw):
    return lax.dot_general(a, b, (((1,), (1,)), ((), ())), preferred_element_type=jnp.float32, **kw)


def tn_dot(a, b, **kw):
    return lax.dot_general(a, b, (((0,), (0,)), ((), ())), preferred_element_type=jnp.float32, **kw)


def nn_dot(a, b, **kw):
    return jnp.dot(a, b, preferred_element_type=jnp.float32, **kw)


def frame_at(place, mine, frames):
    half = frames // 2
    return mine ^ (((place % half) << 1) | (place // half))


def place_of(frame, mine, frames):
    apart = mine ^ frame
    return (apart >> 1) + (apart & 1) * (frames // 2)


def query_frames(mine, frames):
    first = mine - (mine & 1)
    return (first, first + 1, jnp.minimum(first + 2, frames - 1), 0 * first)


def copies_of(pairs, sems, first):
    made = [pltpu.make_async_copy(src, dst, sems.at[first + i]) for i, (src, dst) in enumerate(pairs)]
    for copy in made:
        copy.start()
    return made


def column(j, half):
    core = lax.axis_index("queue") & 1
    return pl.multiple_of(core * half + j * CHUNK, CHUNK)


def fetches(qkv_ref, wbuf, sems, base, half):
    def fetch(j):
        at = pl.multiple_of(base + column(j, half), CHUNK)
        return pltpu.make_async_copy(qkv_ref.at[:, pl.ds(at, CHUNK)], wbuf.at[j], sems.at[j])

    return fetch


def gained(made, gain, count, j, table_ref, square_ref):
    low = made.astype(jnp.bfloat16)
    for f in range(count):
        block = low[f * UROWS : (f + 1) * UROWS, :]
        square_ref[f] += nt_dot(block, block)
    table = (made * gain).astype(jnp.bfloat16)
    at = pl.multiple_of(j * CHUNK, CHUNK)
    for f in range(count):
        table_ref[f, :, pl.ds(at, CHUNK)] = table[f * UROWS : (f + 1) * UROWS, :]


def key_tables(frames, step_hbm, time_hbm, patch_hbm, qkv_ref, gain_hbm, ak_ref, hk_ref, lhs_ref, gram_ref, step_ref, time_ref, patch_ref, gain_ref, wbuf, sems):
    channels, feature = patch_ref.shape
    half = ak_ref.shape[2]
    mine = lax.axis_index("queue")
    count = half // CHUNK
    fetch = fetches(qkv_ref, wbuf, sems, feature, half)
    at = pl.multiple_of((mine & 1) * half, CHUNK)
    small = copies_of(
        (
            (step_hbm, step_ref),
            (patch_hbm, patch_ref),
            (time_hbm.at[0:2], time_ref),
            (gain_hbm.at[pl.ds(at, half)], gain_ref),
        ),
        sems,
        count,
    )
    for j in range(count):
        fetch(j).start()
    for copy in small:
        copy.wait()
    patch = patch_ref[...].astype(jnp.float32)
    centred = patch - jnp.mean(patch, axis=-1, keepdims=True)
    gram_ref[...] = nt_dot(centred, centred, precision=EXACT) / feature
    rest = UROWS - channels
    first_row = lax.broadcasted_iota(jnp.int32, (rest, feature), 0) == 0
    for place in range(frames):
        level = step_ref[frame_at(place, mine, frames)]
        shift = time_ref[0, pl.ds(level, 1), :]
        scale = time_ref[1, pl.ds(level, 1), :]
        lhs_ref[place * UROWS : place * UROWS + channels, :] = (centred * (1.0 + scale)).astype(jnp.bfloat16)
        lhs_ref[place * UROWS + channels : (place + 1) * UROWS, :] = jnp.where(
            first_row, jnp.broadcast_to(shift, (rest, feature)), 0.0
        ).astype(jnp.bfloat16)
    hk_ref[...] = jnp.zeros_like(hk_ref)

    def run(j, carry):
        fetch(j).wait()
        gain = gain_ref[pl.ds(pl.multiple_of(j * CHUNK, CHUNK), CHUNK)].reshape(1, CHUNK)
        gained(nn_dot(lhs_ref[...], wbuf[j]), gain, frames, j, ak_ref, hk_ref)
        return carry

    lax.fori_loop(0, count, run, 0)


def value_tables(frames, lhs_ref, qkv_ref, av_ref, wbuf, sems):
    feature = lhs_ref.shape[1]
    half = av_ref.shape[2]
    count = half // CHUNK
    fetch = fetches(qkv_ref, wbuf, sems, 2 * feature, half)
    for j in range(count):
        fetch(j).start()

    def run(j, carry):
        fetch(j).wait()
        made = nn_dot(lhs_ref[...], wbuf[j]).astype(jnp.bfloat16)
        at = pl.multiple_of(j * CHUNK, CHUNK)
        for f in range(frames):
            av_ref[f, :, pl.ds(at, CHUNK)] = made[f * UROWS : (f + 1) * UROWS, :]
        return carry

    lax.fori_loop(0, count, run, 0)


def query_tables(frames, step_hbm, time_hbm, patch_hbm, lhs_ref, qkv_ref, gain_hbm, out_hbm, head_hbm, aq_ref, hq_ref, mix_ref, skip_ref, step_ref, time_ref, patch_ref, head_ref, gain_ref, lhs_q, head_g, obuf, wbuf, sems):
    channels, _ = patch_ref.shape
    half = aq_ref.shape[2]
    mine = lax.axis_index("queue")
    count = half // CHUNK
    fetch = fetches(qkv_ref, wbuf, sems, 0, half)
    at = pl.multiple_of((mine & 1) * half, CHUNK)
    small = copies_of(
        (
            (step_hbm, step_ref),
            (gain_hbm.at[pl.ds(at, half)], gain_ref),
            (time_hbm.at[2], time_ref),
            (patch_hbm, patch_ref),
            (head_hbm, head_ref),
        ),
        sems,
        count,
    )
    for j in range(count):
        fetch(j).start()
    out_copy = pltpu.make_async_copy(out_hbm.at[pl.ds(at, half), :], obuf, sems.at[count + len(small)])
    out_copy.start()
    for copy in small:
        copy.wait()
    head = head_ref[...].astype(jnp.float32)
    for g, frame in enumerate(query_frames(mine, frames)):
        place = place_of(frame, mine, frames)
        lhs_q[g * UROWS : (g + 1) * UROWS, :] = lhs_ref[pl.ds(pl.multiple_of(place * UROWS, 16), UROWS), :]
        gate = time_ref[pl.ds(step_ref[frame], 1), :]
        head_g[g * channels : (g + 1) * channels, :] = (head * gate).astype(jnp.bfloat16)
    skip_ref[...] = nt_dot(head_ref[...], patch_ref[...])
    hq_ref[...] = jnp.zeros_like(hq_ref)

    def run(j, carry):
        fetch(j).wait()
        gain = gain_ref[pl.ds(pl.multiple_of(j * CHUNK, CHUNK), CHUNK)].reshape(1, CHUNK)
        gained(nn_dot(lhs_q[...], wbuf[j]), gain, GROUPS, j, aq_ref, hq_ref)
        return carry

    lax.fori_loop(0, count, run, 0)
    out_copy.wait()
    mixed = nt_dot(head_g[...], obuf[...]).astype(jnp.bfloat16)
    for g in range(GROUPS):
        mix_ref[g] = mixed[g * channels : (g + 1) * channels, :]


def split(x):
    high = x.astype(jnp.bfloat16)
    return high, (x - high.astype(jnp.float32)).astype(jnp.bfloat16)


def normed_rows(z, gram, square, feature):
    wide = z.astype(jnp.float32)
    gram_hi, gram_lo = split(gram)
    var = jnp.sum(wide * (nn_dot(gram_hi, z) + nn_dot(gram_lo, z)), axis=0, keepdims=True)
    scaled = wide * lax.rsqrt(var + EPS)
    tail = (UROWS - z.shape[0], z.shape[1])
    ones = (lax.broadcasted_iota(jnp.int32, tail, 0) == 0).astype(jnp.float32)
    rows = jnp.concatenate([scaled, ones], axis=0)
    rows_hi, rows_lo = split(rows)
    square_hi, square_lo = split(square)
    made = nn_dot(square_hi, rows_hi) + nn_dot(square_lo, rows_hi) + nn_dot(square_hi, rows_lo)
    mean_sq = jnp.sum(rows * made, axis=0, keepdims=True) / feature
    return rows, lax.rsqrt(mean_sq + EPS)


def attend_kernel(frames, levels, feature, step_ref, z_ref, far_ref, ak_ref, av_ref, aq_ref, hk_ref, hq_ref, hk_far, hq_far, gram_ref, mix_ref, skip_ref, kept_ref, given_ref, q_s, m_s, o_s, part_s):
    mine = lax.axis_index("queue")
    core = mine & 1
    near = frames // 2
    heads = q_s.shape[0]
    channels, tok = z_ref.shape[2:]
    blocks = z_ref.shape[0]
    step = min(blocks, 4)
    portions = frames * (blocks // step)
    gram = gram_ref[...]
    scaling = HEAD_DIM ** (-0.5) * math.log2(math.e)

    def latent_of(block, frame):
        place = place_of(frame, mine, frames)
        inside = jnp.minimum(place, near - 1)
        outside = jnp.maximum(place - near, 0)
        return jnp.where(
            place < near, z_ref[block, inside].astype(jnp.float32), far_ref[block, outside].astype(jnp.float32)
        )

    for g, frame in enumerate(query_frames(mine, frames)):
        z = latent_of(0, frame).astype(jnp.bfloat16)
        rows, factor = normed_rows(z, gram, hq_ref[g] + hq_far[g], feature)
        made = tn_dot(aq_ref[g], (rows * (factor * scaling)).astype(jnp.bfloat16)).astype(jnp.bfloat16)
        for h in range(heads):
            q_s[h, :, g * tok : (g + 1) * tok] = made[h * HEAD_DIM : (h + 1) * HEAD_DIM, :]

    def portion(safe, source_ref, first, i):
        inside = lax.rem(i, near)
        group = lax.div(i, near)
        place = inside + first
        base = group * step
        z = jnp.concatenate([source_ref[base + b, inside] for b in range(step)], axis=1)
        square = hk_ref[place] + hk_far[inside + near - first]
        rows, factor = normed_rows(z, gram, square, feature)
        key_rows = (rows * factor).T.astype(jnp.bfloat16)
        value_rows = rows.astype(jnp.bfloat16)
        slot = group * frames + place
        at = pl.multiple_of(slot * UROWS, 8)
        asked = [
            nn_dot(ak_ref[place, :, h * HEAD_DIM : (h + 1) * HEAD_DIM], q_s[h]).astype(jnp.bfloat16)
            for h in range(heads)
        ]
        scores = nn_dot(key_rows, asked[0])
        for h in range(heads):
            if safe:
                top = jnp.max(scores, axis=0, keepdims=True)
                m_s[h, pl.ds(slot, 1), :] = top
                scores = scores - top
            weights = jnp.exp2(scores).astype(jnp.bfloat16)
            if h + 1 < heads:
                scores = nn_dot(key_rows, asked[h + 1])
            o_s[h, pl.ds(at, UROWS), :] = nn_dot(value_rows, weights)

    def all_portions(safe):
        for source_ref, first in ((z_ref, 0), (far_ref, near)):

            def run(i, carry, source_ref=source_ref, first=first):
                portion(safe, source_ref, first, i)
                return carry

            lax.fori_loop(0, portions // 2, run, 0)

    all_portions(False)

    def total_weight(h):
        total = o_s[h, channels : channels + 1, :]
        for i in range(1, portions):
            total = total + o_s[h, i * UROWS + channels : i * UROWS + channels + 1, :]
        return total

    flags = jnp.zeros((1, q_s.shape[2]), jnp.float32)
    for h in range(heads):
        total = total_weight(h)
        flags = jnp.maximum(flags, jnp.where((total > 2.0**-60) & (total < 2.0**100), 0.0, 1.0))

    @pl.when(jnp.max(flags) > 0.5)
    def _():
        all_portions(True)

        def rescale(i, carry):
            at = pl.multiple_of(i * UROWS, 8)
            for h in range(heads):
                factor = jnp.exp2(m_s[h, pl.ds(i, 1), :] - jnp.max(m_s[h], axis=0, keepdims=True))
                o_s[h, pl.ds(at, UROWS), :] = o_s[h, pl.ds(at, UROWS), :] * factor
            return carry

        lax.fori_loop(0, portions, rescale, 0)

    lead = jnp.where(core == 0, 1.0, 0.0)
    totals = []
    skip_hi, skip_lo = split(skip_ref[...])
    for frame in query_frames(mine, frames):
        z = latent_of(0, frame).astype(jnp.bfloat16)
        totals.append((nn_dot(skip_hi, z) + nn_dot(skip_lo, z)) * lead)
    for h in range(heads):
        span = slice(h * HEAD_DIM, (h + 1) * HEAD_DIM)
        share = 1.0 / total_weight(h)
        done = jnp.zeros((HEAD_DIM, q_s.shape[2]), jnp.float32)
        for part in range(portions // frames):
            at = slice(part * frames * UROWS, (part + 1) * frames * UROWS)
            mean_rows = (o_s[h, at, :] * share).astype(jnp.bfloat16)
            done = done + tn_dot(av_ref[:, :, span].reshape(frames * UROWS, HEAD_DIM), mean_rows)
        done = done.astype(jnp.bfloat16)
        for g in range(GROUPS):
            totals[g] = totals[g] + nn_dot(mix_ref[g, :, span], done[:, g * tok : (g + 1) * tok])
    for g in range(GROUPS):
        part_s[g] = totals[g]

    def drop(frame):
        before = jnp.where(frame > 0, step_ref[jnp.maximum(frame - 1, 0)], -1)
        return (before.astype(jnp.float32) - step_ref[frame].astype(jnp.float32)) / levels

    lat = channels // frames
    following = jnp.minimum(mine + 1, frames - 1)
    followed = jnp.minimum((mine ^ 1) + 1, frames - 1)
    oldest = latent_of(0, 0 * mine)
    kept_ref[:channels] = part_s[core]
    kept_ref[channels : 2 * channels] = latent_of(0, following) + drop(following) * part_s[core + 1]
    given_ref[:channels] = part_s[1 - core]
    given_ref[channels : 2 * channels] = drop(followed) * part_s[2 - core]
    cleaned = drop(0 * mine) * part_s[GROUPS - 1]
    part_s[0] = cleaned + oldest
    part_s[1] = cleaned
    for i in range(lat):
        kept_ref[2 * channels + i : 2 * channels + i + 1, :] = part_s[0, pl.ds(mine * lat + i, 1), :]
        given_ref[2 * channels + i : 2 * channels + i + 1, :] = part_s[1, pl.ds((mine ^ 1) * lat + i, 1), :]


def finish_kernel(frames, kept_ref, got_ref, tail_ref, velocity_ref, next_ref, leaving_ref):
    channels = velocity_ref.shape[0]
    last = lax.axis_index("queue") == frames - 1
    velocity_ref[...] = kept_ref[:channels] + got_ref[:channels]
    arrived = kept_ref[channels : 2 * channels] + got_ref[channels : 2 * channels]
    next_ref[...] = jnp.where(last, tail_ref[...], arrived)
    leaving_ref[...] = kept_ref[2 * channels :] + got_ref[2 * channels :]


def swapped(value, axis, bit):
    peers = lax.axis_size(axis)
    return lax.ppermute(value, axis, [(i, i ^ bit) for i in range(peers)])


def per_device(
    latents,
    step_index,
    tail_noise,
    patch_weight,
    time_table,
    qkv_weight,
    q_gain,
    k_gain,
    out_weight,
    head_weight,
):
    return one_step(
        latents[0].T,
        step_index,
        tail_noise.T,
        patch_weight,
        time_table.transpose(1, 0, 2),
        qkv_weight,
        q_gain,
        k_gain,
        out_weight,
        head_weight.T,
    )


def shaped(*shapes):
    return [jax.ShapeDtypeStruct(shape, kind) for shape, kind in shapes]


def one_step(latent, step_index, tail, patch, times, qkv, q_gain, k_gain, out_w, head):
    channels, feature = patch.shape
    levels = times.shape[1]
    frames = lax.axis_size("queue")
    peers = lax.axis_size("tok")
    half = feature // 2
    heads = half // HEAD_DIM
    tok = latent.shape[1]
    count = half // CHUNK
    f32, bf16 = jnp.float32, jnp.bfloat16
    params = pltpu.CompilerParams(vmem_limit_bytes=48 << 20)

    ak, hk, lhs, gram = pl.pallas_call(
        functools.partial(key_tables, frames),
        out_shape=shaped(
            ((frames, UROWS, half), bf16),
            ((frames, UROWS, UROWS), f32),
            ((frames * UROWS, feature), bf16),
            ((channels, channels), f32),
        ),
        in_specs=[ANY] * 5,
        out_specs=[VMEM] * 4,
        scratch_shapes=[
            pltpu.SMEM((frames,), jnp.int32),
            pltpu.VMEM((2, levels, feature), f32),
            pltpu.VMEM((channels, feature), bf16),
            pltpu.VMEM((half,), f32),
            pltpu.VMEM((count, feature, CHUNK), bf16),
            pltpu.SemaphoreType.DMA((count + 4,)),
        ],
        compiler_params=params,
        cost_estimate=pl.CostEstimate(flops=2 * 10**9, bytes_accessed=4 * 10**6, transcendentals=0),
        name="key_tables",
    )(step_index, times, patch, qkv, k_gain)
    (av,) = pl.pallas_call(
        functools.partial(value_tables, frames),
        out_shape=shaped(((frames, UROWS, half), bf16)),
        in_specs=[VMEM, ANY],
        out_specs=[VMEM],
        scratch_shapes=[
            pltpu.VMEM((count, feature, CHUNK), bf16),
            pltpu.SemaphoreType.DMA((count,)),
        ],
        compiler_params=params,
        cost_estimate=pl.CostEstimate(flops=2 * 10**9, bytes_accessed=4 * 10**6, transcendentals=0),
        name="value_tables",
    )(lhs, qkv)
    aq, hq, mix, skip = pl.pallas_call(
        functools.partial(query_tables, frames),
        out_shape=shaped(
            ((GROUPS, UROWS, half), bf16),
            ((GROUPS, UROWS, UROWS), f32),
            ((GROUPS, channels, half), bf16),
            ((channels, channels), f32),
        ),
        in_specs=[ANY, ANY, ANY, VMEM, ANY, ANY, ANY, ANY],
        out_specs=[VMEM] * 4,
        scratch_shapes=[
            pltpu.SMEM((frames,), jnp.int32),
            pltpu.VMEM((levels, feature), f32),
            pltpu.VMEM((channels, feature), bf16),
            pltpu.VMEM((channels, feature), bf16),
            pltpu.VMEM((half,), f32),
            pltpu.VMEM((GROUPS * UROWS, feature), bf16),
            pltpu.VMEM((GROUPS * channels, feature), bf16),
            pltpu.VMEM((half, feature), bf16),
            pltpu.VMEM((count, feature, CHUNK), bf16),
            pltpu.SemaphoreType.DMA((count + 6,)),
        ],
        compiler_params=params,
        cost_estimate=pl.CostEstimate(flops=2 * 10**9, bytes_accessed=6 * 10**6, transcendentals=0),
        name="query_tables",
    )(step_index, times, patch, lhs, qkv, q_gain, out_w, head)
    hk_far = swapped(hk, "queue", 1)
    hq_far = swapped(hq, "queue", 1)

    known = latent.astype(bf16)[None]
    bit = 2
    while bit < frames:
        got = swapped(known, "queue", bit)
        known = jnp.concatenate([known, got], axis=0)
        bit *= 2
    known = known[None]
    bit = 1
    while bit < peers:
        got = swapped(known, "tok", bit)
        known = jnp.concatenate([known, got], axis=0)
        bit *= 2
    far = swapped(known, "queue", 1)

    rows = GROUPS * tok
    portions = frames * (peers // min(peers, 4))
    share = channels // frames
    sent = (2 * channels + share, tok)
    kept, given = pl.pallas_call(
        functools.partial(attend_kernel, frames, levels, feature),
        out_shape=shaped((sent, f32), (sent, f32)),
        in_specs=[SMEM] + [VMEM] * 12,
        out_specs=[VMEM] * 2,
        scratch_shapes=[
            pltpu.VMEM((heads, HEAD_DIM, rows), bf16),
            pltpu.VMEM((heads, portions, rows), f32),
            pltpu.VMEM((heads, portions * UROWS, rows), f32),
            pltpu.VMEM((GROUPS, channels, tok), f32),
        ],
        compiler_params=params,
        cost_estimate=pl.CostEstimate(flops=30 * 10**9, bytes_accessed=8 * 10**6, transcendentals=13 * 10**6),
        name="attend",
    )(step_index, known, far, ak, av, aq, hk, hq, hk_far, hq_far, gram, mix, skip)
    got = swapped(given, "queue", 1)
    velocity, queue_next, leaving = pl.pallas_call(
        functools.partial(finish_kernel, frames),
        out_shape=shaped(((channels, tok), f32), ((channels, tok), f32), ((share, tok), f32)),
        in_specs=[VMEM] * 3,
        out_specs=[VMEM] * 3,
        name="finish",
    )(kept, got, tail)
    return (velocity.T[None], queue_next.T[None], leaving)


def solution(mesh):
    placed = (P("queue", "tok", None), P(), P("tok", None), P(), P(), P(), P(), P(), P(), P())
    return jax.shard_map(
        per_device,
        mesh=mesh,
        in_specs=placed,
        out_specs=(P("queue", "tok", None), P("queue", "tok", None), P("queue", "tok")),
        check_vma=False,
    )
```

time: 240 us -> 77.4 us (0.32)
  local copies, waits for them, and re-layouts: 63.4 us -> 4.59 us
  matrix products: 56.7 us -> 0 us
  Pallas kernels: 0 us -> 52.9 us
  blocking collectives: 43.2 us -> 0 us
  other arithmetic: 23.2 us -> 0.82 us
  waiting for transfers between devices: 23.3 us -> 7.32 us
  between operations: 15.7 us -> 0.74 us
    dot_general x23 -> x0, matrix products: 56.7 us -> none  [the longest x8 18.6 us: fold_keys(): jnp.einsum('rhk,khd->rhd', weights.astype(jnp.bfloat16), value_rows, pref...]
    pallas_call x0 -> x5, Pallas kernels: none -> 52.9 us  [the longest x1 39.2 us: one_step(): pl.pallas_call(functools.partial(attend_kernel, frames, levels, feature),...]
    psum x1 -> x0, blocking collectives: 28.7 us -> none  [spread(): return lax.psum(jnp.where(mine, value, jnp.zeros_like(value)), axis)]
    while x41 -> x0, local copies, waits for them, and re-layouts: 28.3 us -> none
    all_to_all x3 -> x0, waiting for transfers between devices: 23.3 us -> none  [the longest x1 21.1 us: per_device(): lax.all_to_all(state[2][None].astype(jnp.bfloat16), 'tok', split_axis=1,...]
    all_gather x1 -> x0, blocking collectives: 14.5 us -> none  [per_device(): lax.all_gather(latent.astype(jnp.bfloat16), 'queue', axis=0, tiled=True)]
    dynamic_slice x17 -> x0, local copies, waits for them, and re-layouts: 13.8 us -> none  [the longest x16 12.4 us: per_device(): lax.scan(step_frame, fresh_state(frame_rows, head_count, head_size), ever...]
    reduce_sum x13 -> x0, other arithmetic: 11.2 us -> none  [the longest x8 4.55 us: fold_keys(): run_sum = run_sum * factor + jnp.sum(weights, axis=-1)]
  transfers between devices with their start and end apart: 5 -> 8, of which waited for: 2 -> 4; matrix products, arithmetic and copies ran while one was open for 15% -> 0% of each run, Pallas kernels for 0% -> 16%
where the time goes in v2:
time: 77.4 us; the launch traced here: 77 us
  Pallas kernels  52.9 us (68%)
  starting transfers between devices  10.6 us (14%)
  waiting for transfers between devices  7.32 us (9%)
  local copies, waits for them, and re-layouts  4.59 us (6%)
  other arithmetic  0.82 us (1%)
    pallas_call x1, Pallas kernels, one_step(): pl.pallas_call(functools.partial(attend_kernel, frames, levels, feature),...  39.2 us
    ppermute x8, starting transfers between devices, swapped(): return lax.ppermute(value, axis, [(i, i ^ bit) for i in range(peers)])  10.6 us
    ppermute x8, waiting for transfers between devices, swapped(): return lax.ppermute(value, axis, [(i, i ^ bit) for i in range(peers)])  7.32 us
    pallas_call x1, Pallas kernels, one_step(): pl.pallas_call(functools.partial(query_tables, frames), out_shape=shaped(...  4.61 us
    unnamed x16, local copies, waits for them, and re-layouts  4.59 us
    pallas_call x1, Pallas kernels, one_step(): pl.pallas_call(functools.partial(key_tables, frames), out_shape=shaped(((...  4.36 us
    pallas_call x1, Pallas kernels, one_step(): pl.pallas_call(functools.partial(value_tables, frames), out_shape=shaped(...  3.18 us
    pallas_call x1, Pallas kernels, one_step(): pl.pallas_call(functools.partial(finish_kernel, frames), out_shape=shaped...  1.55 us
  transfers between devices with their start and end apart: 8, of which 4 were waited for; matrix products, arithmetic and copies ran while one was open for 0% of the time, Pallas kernels for 16%

profile of v2, /device:TPU:0, one launch (start us, length us, event | category | flops | bytes accessed | tf_op | source)
XLA Modules:
  0.0 77.0 jit_solution(12925616544345036610)
XLA Ops:
  0.6 0.8 convert_bitcast_fusion
  1.4 3.1 %collective-permute-start = (bf16[1,64,128]{2,1,0:T(8,128)(2,1)S(1)}, bf16[1,64,128]{2,1,0:T(8,128)(2,1)S(1)}, u32[]{:S(2)}, u32[]{:S(2)}) collective-permute-start(bf16[1,64,128]{2,1,0:T(8,128)(2,1)S(1)} %convert_bitcast_fusion), channel_id=1, source_target_pairs={{0,8},{4,12},{8,0},{12,4},{16,24},{20,28},{24,16},{28,20},{1,9},{5... | collective-permute-start | bytes 49160 | tf_op jit(solution)/shard_map/ppermute | solution.py:350
  4.4 1.7 %collective-permute-done = bf16[1,64,128]{2,1,0:T(8,128)(2,1)S(1)} collective-permute-done((bf16[1,64,128]{2,1,0:T(8,128)(2,1)S(1)}, bf16[1,64,128]{2,1,0:T(8,128)(2,1)S(1)}, u32[]{:S(2)}, u32[]{:S(2)}) %collective-permute-start) | collective-permute-done | bytes 16416 | tf_op jit(solution)/shard_map/ppermute | solution.py:350
  6.2 3.0 %collective-permute-start.1 = (bf16[2,64,128]{2,1,0:T(8,128)(2,1)S(1)}, bf16[2,64,128]{2,1,0:T(8,128)(2,1)S(1)}, u32[]{:S(2)}, u32[]{:S(2)}) collective-permute-start(bf16[2,64,128]{2,1,0:T(8,128)(2,1)S(1)} %pad_maximum_fusion.2), channel_id=1, source_target_pairs={{0,16},{4,20},{8,24},{12,28},{16,0},{20,4},{24,8},{28,12},{1,17},{... | collective-permute-start | bytes 98312 | tf_op jit(solution)/shard_map/ppermute | solution.py:350
  9.2 1.9 %collective-permute-done.1 = bf16[2,64,128]{2,1,0:T(8,128)(2,1)S(1)} collective-permute-done((bf16[2,64,128]{2,1,0:T(8,128)(2,1)S(1)}, bf16[2,64,128]{2,1,0:T(8,128)(2,1)S(1)}, u32[]{:S(2)}, u32[]{:S(2)}) %collective-permute-start.1) | collective-permute-done | bytes 32800 | tf_op jit(solution)/shard_map/ppermute | solution.py:350
  11.1 1.9 %collective-permute-start.2 = (bf16[1,4,64,128]{3,2,1,0:T(8,128)(2,1)S(1)}, bf16[1,4,64,128]{3,2,1,0:T(8,128)(2,1)S(1)}, u32[]{:S(2)}, u32[]{:S(2)}) collective-permute-start(bf16[1,4,64,128]{3,2,1,0:T(8,128)(2,1)S(1)} %maximum_bitcast_fusion), channel_id=1, source_target_pairs={{0,1},{1,0},{2,3},{3,2},{4,5},{5,4},{6,7},{7,6},{8,9},{9,8},{10,11... | collective-permute-start | bytes 196616 | tf_op jit(solution)/shard_map/ppermute | solution.py:350
  13.0 2.4 %collective-permute-done.2 = bf16[1,4,64,128]{3,2,1,0:T(8,128)(2,1)S(1)} collective-permute-done((bf16[1,4,64,128]{3,2,1,0:T(8,128)(2,1)S(1)}, bf16[1,4,64,128]{3,2,1,0:T(8,128)(2,1)S(1)}, u32[]{:S(2)}, u32[]{:S(2)}) %collective-permute-start.2) | collective-permute-done | bytes 65568 | tf_op jit(solution)/shard_map/ppermute | solution.py:350
  15.5 1.9 %collective-permute-start.3 = (bf16[2,4,64,128]{3,2,1,0:T(8,128)(2,1)S(1)}, bf16[2,4,64,128]{3,2,1,0:T(8,128)(2,1)S(1)}, u32[]{:S(2)}, u32[]{:S(2)}) collective-permute-start(bf16[2,4,64,128]{3,2,1,0:T(8,128)(2,1)S(1)} %pad_maximum_fusion.1), channel_id=1, source_target_pairs={{0,2},{1,3},{2,0},{3,1},{4,6},{5,7},{6,4},{7,5},{8,10},{9,11},{10,... | collective-permute-start | bytes 393224 | tf_op jit(solution)/shard_map/ppermute | solution.py:350
  17.4 0.0 copy-start
  17.4 1.1 %copy-done = f32[32,3,1536]{2,0,1:T(8,128)S(1)} copy-done((f32[32,3,1536]{2,0,1:T(8,128)S(1)}, f32[32,3,1536]{2,0,1:T(8,128)}, u32[]{:S(2)}) %copy-start) | copy-done | bytes 589848
  18.4 0.0 copy-start.1
  18.4 0.9 %copy-done.1 = bf16[64,1536]{1,0:T(8,128)(2,1)S(1)} copy-done((bf16[64,1536]{1,0:T(8,128)(2,1)S(1)}, bf16[64,1536]{1,0:T(8,128)(2,1)}, u32[]{:S(2)}) %copy-start.1) | copy-done | bytes 196632
  19.4 0.0 copy-start.4
  19.4 0.7 copy-done.4
  20.1 0.0 copy-start.6
  20.1 0.7 copy-done.6
  20.7 0.0 copy-start.2
  20.7 0.0 copy-start.5
  20.7 4.4 %key_tables.1 = (bf16[8,80,768]{2,1,0:T(8,128)(2,1)S(1)}, f32[8,80,80]{2,1,0:T(8,128)S(1)}, bf16[640,1536]{1,0:T(8,128)(2,1)S(1)}, f32[64,64]{1,0:T(8,128)S(1)}) custom-call(s32[8]{0:T(128)S(1)} %copy-done.6, f32[3,32,1536]{2,1,0:T(8,128)S(1)} %bitcast.17, bf16[64,1536]{1,0:T(8,128)(2,1)S(1)} %copy-done.1, bf16[1536,4608]{1,0:T(8,128)(2,1)} %qkv_ref.5, ...), custom_call_target="tpu_custom_call" | custom-call | flops 2000000000 | bytes 4000000 | tf_op jit(solution)/shard_map/key_tables/pallas_call | solution.py:395
  25.1 0.1 collective-permute-start.5
  25.2 0.0 collective-permute-done.3
  25.2 0.6 collective-permute-start.4
  25.8 0.0 copy-done.2
  25.8 0.0 copy-done.5
  25.8 4.6 %query_tables.1 = (bf16[4,80,768]{2,1,0:T(8,128)(2,1)S(1)}, f32[4,80,80]{2,1,0:T(8,128)S(1)}, bf16[4,64,768]{2,1,0:T(8,128)(2,1)S(1)}, f32[64,64]{1,0:T(8,128)S(1)}) custom-call(s32[8]{0:T(128)S(1)} %copy-done.6, f32[3,32,1536]{2,1,0:T(8,128)S(1)} %bitcast.18, bf16[64,1536]{1,0:T(8,128)(2,1)S(1)} %copy-done.1, ...), custom_call_target="tpu_custom_call" | custom-call | flops 2000000000 | bytes 6000000 | tf_op jit(solution)/shard_map/query_tables/pallas_call | solution.py:430
  30.4 0.1 collective-permute-start.6
  30.5 3.2 %value_tables.1.av_ref = bf16[8,80,768]{2,1,0:T(8,128)(2,1)S(1)} custom-call(bf16[640,1536]{1,0:T(8,128)(2,1)S(1)} %get-tuple-element.17.lhs_ref, bf16[1536,4608]{1,0:T(8,128)(2,1)} %qkv_ref.5), custom_call_target="tpu_custom_call" | custom-call | flops 2000000000 | bytes 4000000 | tf_op jit(solution)/shard_map/value_tables/pallas_call | solution.py:417
  33.7 0.0 collective-permute-done.6.hq_far
  33.7 0.0 collective-permute-done.5.hk_far
  33.7 0.0 collective-permute-done.4.far_ref
  33.7 39.2 %attend.1 = (f32[136,128]{1,0:T(8,128)S(1)}, f32[136,128]{1,0:T(8,128)S(1)}) custom-call(s32[8]{0:T(128)S(1)} %copy-done.6, bf16[4,4,64,128]{3,2,1,0:T(8,128)(2,1)S(1)} %pad_maximum_fusion.z_ref, bf16[4,4,64,128]{3,2,1,0:T(8,128)(2,1)S(1)} %collective-permute-done.4.far_ref, bf16[8,80,768]{2,1,0:T(8,128)(2,1)S(1)} %get-tuple-element.16.ak_ref, ...), custom_call_target="tpu_custom_call" | custom-call | flops 30000001024 | bytes 8000000 | tf_op jit(solution)/shard_map/attend/pallas_call | solution.py:477
  73.0 0.0 copy-start.3
  73.0 0.6 copy-done.3
  73.6 0.0 collective-permute-start.7
  73.6 1.3 %collective-permute-done.7.got_ref = f32[136,128]{1,0:T(8,128)S(1)} collective-permute-done((f32[136,128]{1,0:T(8,128)S(1)}, f32[136,128]{1,0:T(8,128)S(1)}, u32[]{:S(2)}, u32[]{:S(2)}) %collective-permute-start.7) | collective-permute-done | bytes 69664 | tf_op jit(solution)/shard_map/ppermute | solution.py:350
  74.9 0.0 copy-start.7
  74.9 0.6 copy-done.7
  75.5 1.6 %finish.1 = (f32[64,128]{1,0:T(8,128)}, f32[64,128]{1,0:T(8,128)}, f32[8,128]{1,0:T(8,128)}) custom-call(f32[136,128]{1,0:T(8,128)} %copy-done.3, f32[136,128]{1,0:T(8,128)} %copy-done.7, f32[64,128]{1,0:T(8,128)} %bitcast.20), custom_call_target="tpu_custom_call" | custom-call | tf_op jit(solution)/shard_map/finish/pallas_call | solution.py:493
  (4 shorter events, 0.1 us)
Async XLA Ops:
  1.4 4.8 %collective-permute-start = (bf16[1,64,128]{2,1,0:T(8,128)(2,1)S(1)}, bf16[1,64,128]{2,1,0:T(8,128)(2,1)S(1)}, u32[]{:S(2)}, u32[]{:S(2)}) collective-permute-start(bf16[1,64,128]{2,1,0:T(8,128)(2,1)S(1)} %convert_bitcast_fusion), channel_id=1, source_target_pairs={{0,8},{4,12},{8,0},{12,4},{16,24},{20,28},{24,16},{28,20},{1,9},{5... | collective-permute-start | bytes 49160 | tf_op jit(solution)/shard_map/ppermute | solution.py:350
  6.2 4.9 %collective-permute-start.1 = (bf16[2,64,128]{2,1,0:T(8,128)(2,1)S(1)}, bf16[2,64,128]{2,1,0:T(8,128)(2,1)S(1)}, u32[]{:S(2)}, u32[]{:S(2)}) collective-permute-start(bf16[2,64,128]{2,1,0:T(8,128)(2,1)S(1)} %pad_maximum_fusion.2), channel_id=1, source_target_pairs={{0,16},{4,20},{8,24},{12,28},{16,0},{20,4},{24,8},{28,12},{1,17},{... | collective-permute-start | bytes 98312 | tf_op jit(solution)/shard_map/ppermute | solution.py:350
  11.1 4.3 %collective-permute-start.2 = (bf16[1,4,64,128]{3,2,1,0:T(8,128)(2,1)S(1)}, bf16[1,4,64,128]{3,2,1,0:T(8,128)(2,1)S(1)}, u32[]{:S(2)}, u32[]{:S(2)}) collective-permute-start(bf16[1,4,64,128]{3,2,1,0:T(8,128)(2,1)S(1)} %maximum_bitcast_fusion), channel_id=1, source_target_pairs={{0,1},{1,0},{2,3},{3,2},{4,5},{5,4},{6,7},{7,6},{8,9},{9,8},{10,11... | collective-permute-start | bytes 196616 | tf_op jit(solution)/shard_map/ppermute | solution.py:350
  15.5 9.7 %collective-permute-start.3 = (bf16[2,4,64,128]{3,2,1,0:T(8,128)(2,1)S(1)}, bf16[2,4,64,128]{3,2,1,0:T(8,128)(2,1)S(1)}, u32[]{:S(2)}, u32[]{:S(2)}) collective-permute-start(bf16[2,4,64,128]{3,2,1,0:T(8,128)(2,1)S(1)} %pad_maximum_fusion.1), channel_id=1, source_target_pairs={{0,2},{1,3},{2,0},{3,1},{4,6},{5,7},{6,4},{7,5},{8,10},{9,11},{10,... | collective-permute-start | bytes 393224 | tf_op jit(solution)/shard_map/ppermute | solution.py:350
  17.4 1.1 %copy-start = (f32[32,3,1536]{2,0,1:T(8,128)S(1)}, f32[32,3,1536]{2,0,1:T(8,128)}, u32[]{:S(2)}) copy-start(f32[32,3,1536]{2,0,1:T(8,128)} %param.14) | copy-start | bytes 1769476
  18.4 0.9 %copy-start.1 = (bf16[64,1536]{1,0:T(8,128)(2,1)S(1)}, bf16[64,1536]{1,0:T(8,128)(2,1)}, u32[]{:S(2)}) copy-start(bf16[64,1536]{1,0:T(8,128)(2,1)} %patch_hbm.3) | copy-start | bytes 589828
  19.4 0.7 copy-start.4
  20.1 0.7 copy-start.6
  20.7 5.1 %copy-start.2 = (bf16[1536,64]{0,1:T(8,128)(2,1)S(1)}, bf16[1536,64]{0,1:T(8,128)(2,1)}, u32[]{:S(2)}) copy-start(bf16[1536,64]{0,1:T(8,128)(2,1)} %param.19) | copy-start | bytes 589828
  20.7 5.1 %copy-start.5 = (f32[1536]{0:T(1024)S(1)}, f32[1536]{0:T(1024)}, u32[]{:S(2)}) copy-start(f32[1536]{0:T(1024)} %gain_hbm.3) | copy-start | bytes 18436
  25.1 8.6 %collective-permute-start.5 = (f32[8,80,80]{2,1,0:T(8,128)S(1)}, f32[8,80,80]{2,1,0:T(8,128)S(1)}, u32[]{:S(2)}, u32[]{:S(2)}) collective-permute-start(f32[8,80,80]{2,1,0:T(8,128)S(1)} %get-tuple-element.19.hk_ref), channel_id=1, source_target_pairs={{0,4},{4,0},{8,12},{12,8},{16,20},{20,16},{24,28},{28,24},{1,5},{5... | collective-permute-start | bytes 614408 | tf_op jit(solution)/shard_map/ppermute | solution.py:350
  25.2 8.5 %collective-permute-start.4 = (bf16[4,4,64,128]{3,2,1,0:T(8,128)(2,1)S(1)}, bf16[4,4,64,128]{3,2,1,0:T(8,128)(2,1)S(1)}, u32[]{:S(2)}, u32[]{:S(2)}) collective-permute-start(bf16[4,4,64,128]{3,2,1,0:T(8,128)(2,1)S(1)} %pad_maximum_fusion.z_ref), channel_id=1, source_target_pairs={{0,4},{4,0},{8,12},{12,8},{16,20},{20,16},{24,28},{28,24},{1,5},{5... | collective-permute-start | bytes 786440 | tf_op jit(solution)/shard_map/ppermute | solution.py:350
  30.4 3.3 %collective-permute-start.6 = (f32[4,80,80]{2,1,0:T(8,128)S(1)}, f32[4,80,80]{2,1,0:T(8,128)S(1)}, u32[]{:S(2)}, u32[]{:S(2)}) collective-permute-start(f32[4,80,80]{2,1,0:T(8,128)S(1)} %get-tuple-element.20.hq_ref), channel_id=1, source_target_pairs={{0,4},{4,0},{8,12},{12,8},{16,20},{20,16},{24,28},{28,24},{1,5},{5... | collective-permute-start | bytes 307208 | tf_op jit(solution)/shard_map/ppermute | solution.py:350
  73.0 0.6 copy-start.3
  73.6 1.3 %collective-permute-start.7 = (f32[136,128]{1,0:T(8,128)S(1)}, f32[136,128]{1,0:T(8,128)S(1)}, u32[]{:S(2)}, u32[]{:S(2)}) collective-permute-start(f32[136,128]{1,0:T(8,128)S(1)} %get-tuple-element.25), channel_id=1, source_target_pairs={{0,4},{4,0},{8,12},{12,8},{16,20},{20,16},{24,28},{28,24},{1,5},{5... | collective-permute-start | bytes 208904 | tf_op jit(solution)/shard_map/ppermute | solution.py:350
  74.9 0.6 copy-start.7

commit v3 on v2

v3 whole, which is shorter than its diff:
```python
import functools
import math

import jax
import jax.numpy as jnp
from jax import lax
from jax.experimental import pallas as pl
from jax.experimental.pallas import tpu as pltpu
from jax.sharding import PartitionSpec as P

HEAD_DIM = 128
EPS = 1e-06
UROWS = 80
GROUPS = 4
CHUNK = 256
UNROLL = 2
LIM_TAB = 62500000
EXACT = lax.Precision.HIGHEST
VMEM = pl.BlockSpec(memory_space=pltpu.VMEM)
SMEM = pl.BlockSpec(memory_space=pltpu.SMEM)
HBM = pl.BlockSpec(memory_space=pltpu.HBM)


def nt_dot(a, b, **kw):
    return lax.dot_general(a, b, (((1,), (1,)), ((), ())), preferred_element_type=jnp.float32, **kw)


def tn_dot(a, b, **kw):
    return lax.dot_general(a, b, (((0,), (0,)), ((), ())), preferred_element_type=jnp.float32, **kw)


def nn_dot(a, b, **kw):
    return jnp.dot(a, b, preferred_element_type=jnp.float32, **kw)


def frame_at(place, mine, frames):
    half = frames // 2
    return mine ^ (((place % half) << 1) | (place // half))


def place_of(frame, mine, frames):
    apart = mine ^ frame
    return (apart >> 1) + (apart & 1) * (frames // 2)


def query_frames(mine, frames):
    first = mine - (mine & 1)
    return (first, first + 1, jnp.minimum(first + 2, frames - 1), 0 * first)


def copies_of(pairs, sems, first):
    made = [pltpu.make_async_copy(src, dst, sems.at[first + i]) for i, (src, dst) in enumerate(pairs)]
    for copy in made:
        copy.start()
    return made


def gained(made, gain, first, count, j, table_ref, square_ref):
    low = made.astype(jnp.bfloat16)
    for f in range(count):
        block = low[f * UROWS : (f + 1) * UROWS, :]
        square_ref[first + f] += nt_dot(block, block)
    keep(low if gain is None else (made * gain).astype(jnp.bfloat16), first, count, j, table_ref)


def keep(table, first, count, j, table_ref):
    at = pl.multiple_of(j * CHUNK, CHUNK)
    for f in range(count):
        table_ref[first + f, :, pl.ds(at, CHUNK)] = table[f * UROWS : (f + 1) * UROWS, :]


def centred_patch(patch_ref):
    patch = patch_ref[...].astype(jnp.float32)
    return patch - jnp.mean(patch, axis=-1, keepdims=True)


def fill_rows(lhs, centred, which, step_ref, time_ref):
    channels, feature = centred.shape
    rest = UROWS - channels
    first_row = lax.broadcasted_iota(jnp.int32, (rest, feature), 0) == 0
    for n, frame in enumerate(which):
        level = step_ref[frame]
        shift = time_ref[0, pl.ds(level, 1), :]
        scale = time_ref[1, pl.ds(level, 1), :]
        lhs[n * UROWS : n * UROWS + channels, :] = (centred * (1.0 + scale)).astype(jnp.bfloat16)
        lhs[n * UROWS + channels : (n + 1) * UROWS, :] = jnp.where(
            first_row, jnp.broadcast_to(shift, (rest, feature)), 0.0
        ).astype(jnp.bfloat16)


def tables_kernel(frames, step_hbm, time_hbm, patch_hbm, qkv_hbm, q_gain_hbm, k_gain_hbm, out_hbm, head_hbm, tab_hbm, av_hbm, mix_hbm, sq_ref, step_ref, time_ref, patch_ref, head_ref, q_gain_ref, k_gain_ref, lhs, lhs_q, head_g, tab_ref, av_ref, mix_ref, obuf, wbuf, sems):
    channels, feature = patch_ref.shape
    half = tab_ref.shape[2]
    count = half // CHUNK
    mine = lax.axis_index("queue")
    start = pl.multiple_of((mine & 1) * half, CHUNK)
    small = copies_of(
        (
            (step_hbm, step_ref),
            (patch_hbm, patch_ref),
            (time_hbm, time_ref),
            (head_hbm, head_ref),
            (q_gain_hbm.at[pl.ds(start, half)], q_gain_ref),
            (k_gain_hbm.at[pl.ds(start, half)], k_gain_ref),
        ),
        sems,
        0,
    )
    big = len(small)

    def fetch(part, j):
        base = (feature, 2 * feature, 0)[part]
        at = pl.multiple_of(base + start + j * CHUNK, CHUNK)
        slot = part * count + j
        return pltpu.make_async_copy(qkv_hbm.at[:, pl.ds(at, CHUNK)], wbuf.at[slot], sems.at[big + slot])

    for part in range(3):
        for j in range(count):
            fetch(part, j).start()
    after = big + 3 * count
    out_copy = pltpu.make_async_copy(out_hbm.at[pl.ds(start, half), :], obuf, sems.at[after])
    out_copy.start()
    for copy in small:
        copy.wait()
    centred = centred_patch(patch_ref)
    fill_rows(lhs, centred, [frame_at(p, mine, frames) for p in range(frames)], step_ref, time_ref)
    sq_ref[...] = jnp.zeros_like(sq_ref)
    sq_ref[frames + GROUPS, :channels, :channels] = nt_dot(centred, centred, precision=EXACT) / feature

    def key_step(j, carry):
        fetch(0, j).wait()
        gained(nn_dot(lhs[...], wbuf[j]), None, 0, frames, j, tab_ref, sq_ref)
        return carry

    lax.fori_loop(0, count, key_step, 0)
    done = copies_of(((tab_ref.at[:frames], tab_hbm.at[:frames]),), sems, after + 1)

    def value_step(j, carry):
        fetch(1, j).wait()
        keep(nn_dot(lhs[...], wbuf[count + j]).astype(jnp.bfloat16), 0, frames, j, av_ref)
        return carry

    lax.fori_loop(0, count, value_step, 0)
    done += copies_of(((av_ref, av_hbm),), sems, after + 2)
    which = query_frames(mine, frames)
    head = head_ref[...].astype(jnp.float32)
    for g, frame in enumerate(which):
        place = place_of(frame, mine, frames)
        lhs_q[g * UROWS : (g + 1) * UROWS, :] = lhs[pl.ds(pl.multiple_of(place * UROWS, 16), UROWS), :]
        gate = time_ref[2, pl.ds(step_ref[frame], 1), :]
        head_g[g * channels : (g + 1) * channels, :] = (head * gate).astype(jnp.bfloat16)
    sq_ref[frames + GROUPS + 1, :channels, :channels] = nt_dot(head_ref[...], patch_ref[...])

    def query_step(j, carry):
        fetch(2, j).wait()
        span = pl.ds(pl.multiple_of(j * CHUNK, CHUNK), CHUNK)
        gain = (q_gain_ref[span] * k_gain_ref[span]).reshape(1, CHUNK)
        gained(nn_dot(lhs_q[...], wbuf[2 * count + j]), gain, frames, GROUPS, j, tab_ref, sq_ref)
        return carry

    lax.fori_loop(0, count, query_step, 0)
    done += copies_of(((tab_ref.at[frames:], tab_hbm.at[frames:]),), sems, after + 3)
    out_copy.wait()
    mixed = nt_dot(head_g[...], obuf[...]).astype(jnp.bfloat16)
    for g in range(GROUPS):
        mix_ref[g] = mixed[g * channels : (g + 1) * channels, :]
    done += copies_of(((mix_ref, mix_hbm),), sems, after + 4)
    for copy in done:
        copy.wait()


def split(x):
    high = x.astype(jnp.bfloat16)
    return high, (x - high.astype(jnp.float32)).astype(jnp.bfloat16)


def normed_rows(z, gram, square, feature):
    wide = z.astype(jnp.float32)
    gram_hi, gram_lo = split(gram)
    var = jnp.sum(wide * (nn_dot(gram_hi, z) + nn_dot(gram_lo, z)), axis=0, keepdims=True)
    scaled = wide * lax.rsqrt(jnp.maximum(var, 0.0) + EPS)
    tail = (UROWS - z.shape[0], z.shape[1])
    ones = (lax.broadcasted_iota(jnp.int32, tail, 0) == 0).astype(jnp.float32)
    rows = jnp.concatenate([scaled, ones], axis=0)
    rows_hi, rows_lo = split(rows)
    square_hi, square_lo = split(square)
    made = nn_dot(square_hi, rows_hi) + nn_dot(square_lo, rows_hi) + nn_dot(square_hi, rows_lo)
    mean_sq = jnp.sum(rows * made, axis=0, keepdims=True) / feature
    return rows, lax.rsqrt(jnp.maximum(mean_sq, 0.0) + EPS)


def latent_of(near_ref, far_ref, frame, frames):
    half = frames // 2
    place = place_of(frame, lax.axis_index("queue"), frames)
    inside = near_ref[jnp.minimum(place, half - 1)]
    outside = far_ref[jnp.maximum(place - half, 0)]
    return jnp.where(place < half, inside.astype(jnp.float32), outside.astype(jnp.float32))


def ask_kernel(frames, feature, near_ref, far_ref, tab_ref, sq_ref, sq_far, asked_ref, q_s):
    mine = lax.axis_index("queue")
    heads = q_s.shape[0]
    channels, tok = near_ref.shape[1:]
    gram = sq_ref[frames + GROUPS, :channels, :channels]
    scaling = HEAD_DIM ** (-0.5) * math.log2(math.e)
    for g, frame in enumerate(query_frames(mine, frames)):
        z = latent_of(near_ref, far_ref, frame, frames).astype(jnp.bfloat16)
        rows, factor = normed_rows(z, gram, sq_ref[frames + g] + sq_far[frames + g], feature)
        made = tn_dot(tab_ref[frames + g], (rows * (factor * scaling)).astype(jnp.bfloat16)).astype(jnp.bfloat16)
        for h in range(heads):
            q_s[h, :, g * tok : (g + 1) * tok] = made[h * HEAD_DIM : (h + 1) * HEAD_DIM, :]
    for h in range(heads):
        table = tab_ref[:frames, :, h * HEAD_DIM : (h + 1) * HEAD_DIM].reshape(frames * UROWS, HEAD_DIM)
        asked_ref[h] = nn_dot(table, q_s[h]).astype(jnp.bfloat16)


def each_portion(feature, sources, asked_ref, squares, gram, emit, safe=False):
    heads = asked_ref.shape[0]
    for blocks, first in sources:
        held = blocks[0].shape[0]
        step = min(len(blocks), 4)
        ways = UNROLL if held % UNROLL == 0 else 1
        for group in range(len(blocks) // step):
            used = blocks[group * step : (group + 1) * step]

            def run(i, carry, used=used, first=first, group=group, ways=ways):
                items = []
                for way in range(ways):
                    inside = i * ways + way
                    place = first + inside
                    z = jnp.concatenate([block[inside] for block in used], axis=1)
                    rows, factor = normed_rows(z, gram, squares(place), feature)
                    key_rows = (rows * factor).T.astype(jnp.bfloat16)
                    value_rows = rows.astype(jnp.bfloat16)
                    items += [(h, place, key_rows, value_rows) for h in range(heads)]

                def scores_of(item):
                    h, place, key_rows, _ = item
                    return nn_dot(key_rows, asked_ref[h, rows_at(place), :])

                scores = scores_of(items[0])
                for n, (h, place, unused, value_rows) in enumerate(items):
                    top = None
                    if safe:
                        top = jnp.max(scores, axis=0, keepdims=True)
                        scores = scores - top
                    weights = jnp.exp2(scores).astype(jnp.bfloat16)
                    if n + 1 < len(items):
                        scores = scores_of(items[n + 1])
                    emit(h, place, group, top, nn_dot(value_rows, weights))
                return carry

            lax.fori_loop(0, held // ways, run, 0)


def squares_of(hk_ref, hk_far, frames):
    half = frames // 2
    return lambda place: hk_ref[place] + hk_far[lax.rem(place + half, frames)]


def rows_at(place):
    return pl.ds(pl.multiple_of(place * UROWS, 16), UROWS)


def attend_kernel(frames, levels, feature, step_ref, near_0, near_ref, far_0, far_ref, asked_ref, av_ref, mix_ref, sq_ref, sq_far, kept_ref, given_ref, m_s, o_s, part_s):
    mine = lax.axis_index("queue")
    core = mine & 1
    heads = asked_ref.shape[0]
    blocks, half, channels, tok = near_ref.shape
    gram = sq_ref[frames + GROUPS, :channels, :channels]
    squares = squares_of(sq_ref, sq_far, frames)
    sources = tuple(
        ([own] + [rest.at[b] for b in range(blocks)], first)
        for own, rest, first in ((near_0, near_ref, 0), (far_0, far_ref, half))
    )

    def emit(h, place, group, top, made):
        if group == 0:
            o_s[h, rows_at(place), :] = made
        else:
            o_s[h, rows_at(place), :] += made

    each_portion(feature, sources, asked_ref, squares, gram, emit)

    def total_weight(h):
        total = o_s[h, channels : channels + 1, :]
        for i in range(1, frames):
            total = total + o_s[h, i * UROWS + channels : i * UROWS + channels + 1, :]
        return total

    flags = jnp.zeros((1, o_s.shape[2]), jnp.float32)
    for h in range(heads):
        total = total_weight(h)
        flags = jnp.maximum(flags, jnp.where((total > 2.0**-60) & (total < 2.0**100), 0.0, 1.0))

    @pl.when(jnp.max(flags) > 0.5)
    def _():
        m_s[...] = jnp.full_like(m_s, -1e30)
        o_s[...] = jnp.zeros_like(o_s)

        def shifted(h, place, group, top, made):
            row = pl.ds(place, 1)
            before = m_s[h, row, :]
            after = jnp.maximum(before, top)
            m_s[h, row, :] = after
            o_s[h, rows_at(place), :] = o_s[h, rows_at(place), :] * jnp.exp2(before - after) + made * jnp.exp2(
                top - after
            )

        each_portion(feature, sources, asked_ref, squares, gram, shifted, safe=True)

        def rescale(i, carry):
            for h in range(heads):
                factor = jnp.exp2(m_s[h, pl.ds(i, 1), :] - jnp.max(m_s[h], axis=0, keepdims=True))
                o_s[h, rows_at(i), :] = o_s[h, rows_at(i), :] * factor
            return carry

        lax.fori_loop(0, frames, rescale, 0)

    lead = jnp.where(core == 0, 1.0, 0.0)
    totals = []
    skip_hi, skip_lo = split(sq_ref[frames + GROUPS + 1, :channels, :channels])
    for frame in query_frames(mine, frames):
        z = latent_of(near_0, far_0, frame, frames).astype(jnp.bfloat16)
        totals.append((nn_dot(skip_hi, z) + nn_dot(skip_lo, z)) * lead)
    for h in range(heads):
        span = slice(h * HEAD_DIM, (h + 1) * HEAD_DIM)
        mean_rows = (o_s[h] * (1.0 / total_weight(h))).astype(jnp.bfloat16)
        done = tn_dot(av_ref[:, :, span].reshape(frames * UROWS, HEAD_DIM), mean_rows).astype(jnp.bfloat16)
        for g in range(GROUPS):
            totals[g] = totals[g] + nn_dot(mix_ref[g, :, span], done[:, g * tok : (g + 1) * tok])
    for g in range(GROUPS):
        part_s[g] = totals[g]

    def drop(frame):
        before = jnp.where(frame > 0, step_ref[jnp.maximum(frame - 1, 0)], -1)
        return (before.astype(jnp.float32) - step_ref[frame].astype(jnp.float32)) / levels

    lat = channels // frames
    following = jnp.minimum(mine + 1, frames - 1)
    followed = jnp.minimum((mine ^ 1) + 1, frames - 1)
    kept_ref[:channels] = part_s[core]
    kept_ref[channels : 2 * channels] = (
        latent_of(near_0, far_0, following, frames) + drop(following) * part_s[core + 1]
    )
    given_ref[:channels] = part_s[1 - core]
    given_ref[channels : 2 * channels] = drop(followed) * part_s[2 - core]
    cleaned = drop(0 * mine) * part_s[GROUPS - 1]
    part_s[0] = cleaned + latent_of(near_0, far_0, 0 * mine, frames)
    part_s[1] = cleaned
    for i in range(lat):
        kept_ref[2 * channels + i : 2 * channels + i + 1, :] = part_s[0, pl.ds(mine * lat + i, 1), :]
        given_ref[2 * channels + i : 2 * channels + i + 1, :] = part_s[1, pl.ds((mine ^ 1) * lat + i, 1), :]


def finish_kernel(frames, kept_ref, got_ref, tail_ref, velocity_ref, next_ref, leaving_ref):
    channels = velocity_ref.shape[0]
    last = lax.axis_index("queue") == frames - 1
    velocity_ref[...] = kept_ref[:channels] + got_ref[:channels]
    arrived = kept_ref[channels : 2 * channels] + got_ref[channels : 2 * channels]
    next_ref[...] = jnp.where(last, tail_ref[...], arrived)
    leaving_ref[...] = kept_ref[2 * channels :] + got_ref[2 * channels :]


def swapped(value, axis, bit):
    peers = lax.axis_size(axis)
    return lax.ppermute(value, axis, [(i, i ^ bit) for i in range(peers)])


def per_device(
    latents,
    step_index,
    tail_noise,
    patch_weight,
    time_table,
    qkv_weight,
    q_gain,
    k_gain,
    out_weight,
    head_weight,
):
    return one_step(
        latents[0].T,
        step_index,
        tail_noise.T,
        patch_weight,
        time_table.transpose(1, 0, 2),
        qkv_weight,
        q_gain,
        k_gain,
        out_weight,
        head_weight.T,
    )


def shaped(*shapes):
    return [jax.ShapeDtypeStruct(shape, kind) for shape, kind in shapes]


def one_step(latent, step_index, tail, patch, times, qkv, q_gain, k_gain, out_w, head):
    channels, feature = patch.shape
    levels = times.shape[1]
    frames = lax.axis_size("queue")
    peers = lax.axis_size("tok")
    half = feature // 2
    heads = half // HEAD_DIM
    tok = latent.shape[1]
    count = half // CHUNK
    f32, bf16 = jnp.float32, jnp.bfloat16
    params = pltpu.CompilerParams(vmem_limit_bytes=(24 << 20) * max(1, frames // 8))

    made = (
        ((frames + GROUPS, UROWS, half), bf16),
        ((frames, UROWS, half), bf16),
        ((GROUPS, channels, half), bf16),
    )
    tab, av, mix, sq = pl.pallas_call(
        functools.partial(tables_kernel, frames),
        out_shape=shaped(*made, ((frames + GROUPS + 2, UROWS, UROWS), f32)),
        in_specs=[HBM] * 8,
        out_specs=[HBM] * 3 + [VMEM],
        scratch_shapes=[
            pltpu.SMEM((frames,), jnp.int32),
            pltpu.VMEM((3, levels, feature), f32),
            pltpu.VMEM((channels, feature), bf16),
            pltpu.VMEM((channels, feature), bf16),
            pltpu.VMEM((half,), f32),
            pltpu.VMEM((half,), f32),
            pltpu.VMEM((frames * UROWS, feature), bf16),
            pltpu.VMEM((GROUPS * UROWS, feature), bf16),
            pltpu.VMEM((GROUPS * channels, feature), bf16),
        ]
        + [pltpu.VMEM(*shape) for shape in made]
        + [
            pltpu.VMEM((half, feature), bf16),
            pltpu.VMEM((3 * count, feature, CHUNK), bf16),
            pltpu.SemaphoreType.DMA((3 * count + 11,)),
        ],
        compiler_params=pltpu.CompilerParams(vmem_limit_bytes=LIM_TAB),
        name="tables",
    )(step_index, times, patch, qkv, q_gain, k_gain, out_w, head)
    sq_far = swapped(sq, "queue", 1)

    own = latent.astype(bf16)[None]
    parts = [own]
    for apart in range(2, frames, 2):
        parts.append(swapped(own, "queue", apart))
    known = jnp.concatenate(parts, axis=0)
    own_far = swapped(known, "queue", 1)
    rows = GROUPS * tok
    (asked,) = pl.pallas_call(
        functools.partial(ask_kernel, frames, feature),
        out_shape=shaped(((heads, frames * UROWS, rows), bf16)),
        in_specs=[VMEM] * 5,
        out_specs=[VMEM],
        scratch_shapes=[pltpu.VMEM((heads, HEAD_DIM, rows), bf16)],
        compiler_params=params,
        cost_estimate=pl.CostEstimate(flops=10**9, bytes_accessed=4 * 10**6, transcendentals=0),
        name="ask",
    )(known, own_far, tab, sq, sq_far)

    parts = []
    for apart in range(1, peers):
        parts.append(swapped(known, "tok", apart)[None])
    near = jnp.concatenate(parts, axis=0)
    far = swapped(near, "queue", 1)

    share = channels // frames
    sent = (2 * channels + share, tok)
    kept, given = pl.pallas_call(
        functools.partial(attend_kernel, frames, levels, feature),
        out_shape=shaped((sent, f32), (sent, f32)),
        in_specs=[SMEM] + [VMEM] * 9,
        out_specs=[VMEM] * 2,
        scratch_shapes=[
            pltpu.VMEM((heads, frames, rows), f32),
            pltpu.VMEM((heads, frames * UROWS, rows), f32),
            pltpu.VMEM((GROUPS, channels, tok), f32),
        ],
        compiler_params=params,
        cost_estimate=pl.CostEstimate(flops=8 * 10**9, bytes_accessed=8 * 10**6, transcendentals=6 * 10**6),
        name="attend",
    )(step_index, known, near, own_far, far, asked, av, mix, sq, sq_far)
    got = swapped(given, "queue", 1)
    velocity, queue_next, leaving = pl.pallas_call(
        functools.partial(finish_kernel, frames),
        out_shape=shaped(((channels, tok), f32), ((channels, tok), f32), ((share, tok), f32)),
        in_specs=[VMEM] * 3,
        out_specs=[VMEM] * 3,
        compiler_params=pltpu.CompilerParams(vmem_limit_bytes=4 << 20),
        name="finish",
    )(kept, got, tail)
    return (velocity.T[None], queue_next.T[None], leaving)


def solution(mesh):
    placed = (P("queue", "tok", None), P(), P("tok", None), P(), P(), P(), P(), P(), P(), P())
    return jax.shard_map(
        per_device,
        mesh=mesh,
        in_specs=placed,
        out_specs=(P("queue", "tok", None), P("queue", "tok", None), P("queue", "tok")),
        check_vma=False,
    )
```

time: 77.4 us -> 68.4 us (0.88)
  Pallas kernels: 52.9 us -> 48 us
  local copies, waits for them, and re-layouts: 4.59 us -> 2.46 us
  waiting for transfers between devices: 7.32 us -> 6.23 us
    pallas_call x1, Pallas kernels: 39.2 us -> 33.5 us  [one_step(): pl.pallas_call(functools.partial(attend_kernel, frames, levels, feature),...]
    unnamed x16 -> x14, local copies, waits for them, and re-layouts: 4.59 us -> 2.46 us
    pallas_call x3 -> x2, Pallas kernels: 12.2 us -> 13.8 us  [the longest x1 11.4 us: one_step(): pl.pallas_call(functools.partial(tables_kernel, frames), out_shape=shaped...]
    ppermute x8 -> x10, waiting for transfers between devices: 7.32 us -> 6.23 us  [swapped(): return lax.ppermute(value, axis, [(i, i ^ bit) for i in range(peers)])]
    pallas_call x1, Pallas kernels: 1.55 us -> 0.63 us  [one_step(): pl.pallas_call(functools.partial(finish_kernel, frames), out_shape=shaped...]
    ppermute x8 -> x10, starting transfers between devices: 10.6 us -> 9.91 us  [swapped(): return lax.ppermute(value, axis, [(i, i ^ bit) for i in range(peers)])]
  transfers between devices with their start and end apart: 8 -> 10, of which waited for: 4 -> 5; matrix products, arithmetic and copies ran while one was open for 0% -> 0% of each run, Pallas kernels for 16% -> 20%
where the time goes in v3:
time: 68.4 us; the launch traced here: 68.1 us
  Pallas kernels  48 us (70%)
  starting transfers between devices  9.91 us (14%)
  waiting for transfers between devices  6.23 us (9%)
  local copies, waits for them, and re-layouts  2.46 us (4%)
  other arithmetic  0.8 us (1%)
  between operations  0.79 us (1%)
    pallas_call x1, Pallas kernels, one_step(): pl.pallas_call(functools.partial(attend_kernel, frames, levels, feature),...  33.5 us
    pallas_call x1, Pallas kernels, one_step(): pl.pallas_call(functools.partial(tables_kernel, frames), out_shape=shaped...  11.4 us
    ppermute x10, starting transfers between devices, swapped(): return lax.ppermute(value, axis, [(i, i ^ bit) for i in range(peers)])  9.91 us
    ppermute x10, waiting for transfers between devices, swapped(): return lax.ppermute(value, axis, [(i, i ^ bit) for i in range(peers)])  6.23 us
    unnamed x14, local copies, waits for them, and re-layouts  2.46 us
    pallas_call x1, Pallas kernels, one_step(): pl.pallas_call(functools.partial(ask_kernel, frames, feature), out_shape=...  2.39 us
  transfers between devices with their start and end apart: 10, of which 5 were waited for; matrix products, arithmetic and copies ran while one was open for 0% of the time, Pallas kernels for 20%

profile of v3, /device:TPU:0, one launch (start us, length us, event | category | flops | bytes accessed | tf_op | source)
XLA Modules:
  0.0 68.1 jit_solution(1524174739962303709)
XLA Ops:
  0.6 0.8 %convert_bitcast_fusion = bf16[1,64,128]{2,1,0:T(8,128)(2,1)S(1)} fusion(f32[1,128,64]{1,2,0:T(8,128)} %param.10), kind=kLoop, calls=%fused_computation.2 | loop fusion | flops 8192 | bytes 49152 | tf_op jit(solution)/shard_map/broadcast_in_dim | solution.py:444
  1.4 5.1 %collective-permute-start.2 = (bf16[1,64,128]{2,1,0:T(8,128)(2,1)S(1)}, bf16[1,64,128]{2,1,0:T(8,128)(2,1)S(1)}, u32[]{:S(2)}, u32[]{:S(2)}) collective-permute-start(bf16[1,64,128]{2,1,0:T(8,128)(2,1)S(1)} %convert_bitcast_fusion), channel_id=1, source_target_pairs={{0,24},{4,28},{8,16},{12,20},{16,8},{20,12},{24,0},{28,4},{1,25},{... | collective-permute-start | bytes 49160 | tf_op jit(solution)/shard_map/ppermute | solution.py:367
  6.5 0.0 collective-permute-start.1
  6.5 0.6 collective-permute-start
  7.0 11.4 %tables.1 = (bf16[12,80,768]{2,1,0:T(8,128)(2,1)}, bf16[8,80,768]{2,1,0:T(8,128)(2,1)}, bf16[4,64,768]{2,1,0:T(8,128)(2,1)}, f32[14,80,80]{2,1,0:T(8,128)}) custom-call(s32[8]{0:T(128)} %step_ref.1, f32[3,32,1536]{2,1,0:T(8,128)} %bitcast.19, bf16[64,1536]{1,0:T(8,128)(2,1)} %patch_hbm.1, bf16[1536,4608]{1,0:T(8,128)(2,1)} %qkv_hbm.1, f32[1536]{0:T(1024)} %q_gain_hbm.1, ...), custom_call_target="tpu_custom_call" | custom-call | tf_op jit(solution)/shard_map/tables/pallas_call | solution.py:417
  18.5 0.0 copy-start.4
  18.5 0.0 copy-start.6
  18.5 0.1 collective-permute-start.8
  18.6 0.0 collective-permute-done.2
  18.6 0.0 collective-permute-done.1
  18.6 0.0 collective-permute-done
  18.6 2.7 %collective-permute-start.5 = (bf16[4,64,128]{2,1,0:T(8,128)(2,1)S(1)}, bf16[4,64,128]{2,1,0:T(8,128)(2,1)S(1)}, u32[]{:S(2)}, u32[]{:S(2)}) collective-permute-start(bf16[4,64,128]{2,1,0:T(8,128)(2,1)S(1)} %pad_maximum_fusion.1.near_ref.near_0), channel_id=1, source_target_pairs={{0,3},{1,2},{2,1},{3,0},{4,7},{5,6},{6,5},{7,4},{8,11},{9,10},{10,... | collective-permute-start | bytes 196616 | tf_op jit(solution)/shard_map/ppermute | solution.py:367
  21.4 0.5 collective-permute-start.4
  21.9 0.3 collective-permute-start.3
  22.2 1.9 %collective-permute-done.5 = bf16[4,64,128]{2,1,0:T(8,128)(2,1)S(1)} collective-permute-done((bf16[4,64,128]{2,1,0:T(8,128)(2,1)S(1)}, bf16[4,64,128]{2,1,0:T(8,128)(2,1)S(1)}, u32[]{:S(2)}, u32[]{:S(2)}) %collective-permute-start.5) | collective-permute-done | bytes 65568 | tf_op jit(solution)/shard_map/ppermute | solution.py:367
  24.1 1.5 %collective-permute-done.4 = bf16[4,64,128]{2,1,0:T(8,128)(2,1)S(1)} collective-permute-done((bf16[4,64,128]{2,1,0:T(8,128)(2,1)S(1)}, bf16[4,64,128]{2,1,0:T(8,128)(2,1)S(1)}, u32[]{:S(2)}, u32[]{:S(2)}) %collective-permute-start.4) | collective-permute-done | bytes 65568 | tf_op jit(solution)/shard_map/ppermute | solution.py:367
  25.6 0.5 collective-permute-done.3
  26.2 0.1 collective-permute-start.7
  26.2 0.5 collective-permute-start.6
  26.7 1.0 %collective-permute-done.6.far_ref.far_0 = bf16[4,64,128]{2,1,0:T(8,128)(2,1)S(1)} collective-permute-done((bf16[4,64,128]{2,1,0:T(8,128)(2,1)S(1)}, bf16[4,64,128]{2,1,0:T(8,128)(2,1)S(1)}, u32[]{:S(2)}, u32[]{:S(2)}) %collective-permute-start.6) | collective-permute-done | bytes 65568 | tf_op jit(solution)/shard_map/ppermute | solution.py:367
  27.8 0.0 collective-permute-done.8.sq_far
  27.8 0.0 copy-start
  27.8 1.4 %copy-done = bf16[12,80,768]{2,1,0:T(8,128)(2,1)S(1)} copy-done((bf16[12,80,768]{2,1,0:T(8,128)(2,1)S(1)}, bf16[12,80,768]{2,1,0:T(8,128)(2,1)}, u32[]{:S(2)}) %copy-start) | copy-done | bytes 1474584
  29.1 0.0 copy-start.1
  29.1 1.1 %copy-done.1 = f32[14,80,80]{2,1,0:T(8,128)S(1)} copy-done((f32[14,80,80]{2,1,0:T(8,128)S(1)}, f32[14,80,80]{2,1,0:T(8,128)}, u32[]{:S(2)}) %copy-start.1) | copy-done | bytes 358424
  30.2 0.0 copy-start.2
  30.2 0.0 copy-start.5
  30.2 2.4 %ask.1.asked_ref = bf16[6,640,512]{2,1,0:T(8,128)(2,1)S(1)} custom-call(bf16[4,64,128]{2,1,0:T(8,128)(2,1)S(1)} %pad_maximum_fusion.1.near_ref.near_0, bf16[4,64,128]{2,1,0:T(8,128)(2,1)S(1)} %collective-permute-done.6.far_ref.far_0, bf16[12,80,768]{2,1,0:T(8,128)(2,1)S(1)} %copy-done, f32[14,80,80]{2,1,0:T(8,128)S(1)} %copy-done.1, ...), custom_call_target="tpu_custom_call" | custom-call | flops 1000000000 | bytes 4000000 | tf_op jit(solution)/shard_map/ask/pallas_call | solution.py:451
  32.6 0.0 collective-permute-done.7.far_ref
  32.6 0.0 copy-done.4
  32.6 0.0 copy-done.6
  32.6 0.0 copy-done.2
  32.6 0.0 copy-done.5
  32.6 0.0 copy-start.3
  32.7 33.5 %attend.1 = (f32[136,128]{1,0:T(8,128)S(1)}, f32[136,128]{1,0:T(8,128)S(1)}) custom-call(s32[8]{0:T(128)S(1)} %copy-done.4, bf16[4,64,128]{2,1,0:T(8,128)(2,1)S(1)} %pad_maximum_fusion.1.near_ref.near_0, bf16[3,4,64,128]{3,2,1,0:T(8,128)(2,1)S(1)} %pad_maximum_fusion.near_ref, bf16[4,64,128]{2,1,0:T(8,128)(2,1)S(1)} %collective-permute-done.6.far_ref.far_0, ...), custom_call_target="tpu_custom_call" | custom-call | flops 8000000000 | bytes 8000000 | tf_op jit(solution)/shard_map/attend/pallas_call | solution.py:470
  66.2 0.1 collective-permute-start.9
  66.2 1.2 %collective-permute-done.9.got_ref = f32[136,128]{1,0:T(8,128)S(1)} collective-permute-done((f32[136,128]{1,0:T(8,128)S(1)}, f32[136,128]{1,0:T(8,128)S(1)}, u32[]{:S(2)}, u32[]{:S(2)}) %collective-permute-start.9) | collective-permute-done | bytes 69664 | tf_op jit(solution)/shard_map/ppermute | solution.py:367
  67.5 0.0 copy-done.3
  67.5 0.6 finish.1
  (2 shorter events, 0.0 us)
Async XLA Ops:
  1.4 17.2 %collective-permute-start.2 = (bf16[1,64,128]{2,1,0:T(8,128)(2,1)S(1)}, bf16[1,64,128]{2,1,0:T(8,128)(2,1)S(1)}, u32[]{:S(2)}, u32[]{:S(2)}) collective-permute-start(bf16[1,64,128]{2,1,0:T(8,128)(2,1)S(1)} %convert_bitcast_fusion), channel_id=1, source_target_pairs={{0,24},{4,28},{8,16},{12,20},{16,8},{20,12},{24,0},{28,4},{1,25},{... | collective-permute-start | bytes 49160 | tf_op jit(solution)/shard_map/ppermute | solution.py:367
  6.5 12.1 %collective-permute-start.1 = (bf16[1,64,128]{2,1,0:T(8,128)(2,1)S(1)}, bf16[1,64,128]{2,1,0:T(8,128)(2,1)S(1)}, u32[]{:S(2)}, u32[]{:S(2)}) collective-permute-start(bf16[1,64,128]{2,1,0:T(8,128)(2,1)S(1)} %convert_bitcast_fusion), channel_id=1, source_target_pairs={{0,16},{4,20},{8,24},{12,28},{16,0},{20,4},{24,8},{28,12},{1,17},{... | collective-permute-start | bytes 49160 | tf_op jit(solution)/shard_map/ppermute | solution.py:367
  6.5 12.1 %collective-permute-start = (bf16[1,64,128]{2,1,0:T(8,128)(2,1)S(1)}, bf16[1,64,128]{2,1,0:T(8,128)(2,1)S(1)}, u32[]{:S(2)}, u32[]{:S(2)}) collective-permute-start(bf16[1,64,128]{2,1,0:T(8,128)(2,1)S(1)} %convert_bitcast_fusion), channel_id=1, source_target_pairs={{0,8},{4,12},{8,0},{12,4},{16,24},{20,28},{24,16},{28,20},{1,9},{5... | collective-permute-start | bytes 49160 | tf_op jit(solution)/shard_map/ppermute | solution.py:367
  18.5 14.1 %copy-start.4 = (s32[8]{0:T(128)S(1)}, s32[8]{0:T(128)}, u32[]{:S(2)}) copy-start(s32[8]{0:T(128)} %step_ref.1) | copy-start | bytes 100
  18.5 14.1 %copy-start.6 = (bf16[4,64,768]{2,1,0:T(8,128)(2,1)S(1)}, bf16[4,64,768]{2,1,0:T(8,128)(2,1)}, u32[]{:S(2)}) copy-start(bf16[4,64,768]{2,1,0:T(8,128)(2,1)} %get-tuple-element.15.mix_ref) | copy-start | bytes 1179652
  18.5 9.3 %collective-permute-start.8 = (f32[14,80,80]{2,1,0:T(8,128)}, f32[14,80,80]{2,1,0:T(8,128)S(1)}, u32[]{:S(2)}, u32[]{:S(2)}) collective-permute-start(f32[14,80,80]{2,1,0:T(8,128)} %get-tuple-element.13.sq_ref), channel_id=1, source_target_pairs={{0,4},{4,0},{8,12},{12,8},{16,20},{20,16},{24,28},{28,24},{1,5},{5... | collective-permute-start | bytes 1075208 | tf_op jit(solution)/shard_map/ppermute | solution.py:367
  18.6 5.5 %collective-permute-start.5 = (bf16[4,64,128]{2,1,0:T(8,128)(2,1)S(1)}, bf16[4,64,128]{2,1,0:T(8,128)(2,1)S(1)}, u32[]{:S(2)}, u32[]{:S(2)}) collective-permute-start(bf16[4,64,128]{2,1,0:T(8,128)(2,1)S(1)} %pad_maximum_fusion.1.near_ref.near_0), channel_id=1, source_target_pairs={{0,3},{1,2},{2,1},{3,0},{4,7},{5,6},{6,5},{7,4},{8,11},{9,10},{10,... | collective-permute-start | bytes 196616 | tf_op jit(solution)/shard_map/ppermute | solution.py:367
  21.4 4.3 %collective-permute-start.4 = (bf16[4,64,128]{2,1,0:T(8,128)(2,1)S(1)}, bf16[4,64,128]{2,1,0:T(8,128)(2,1)S(1)}, u32[]{:S(2)}, u32[]{:S(2)}) collective-permute-start(bf16[4,64,128]{2,1,0:T(8,128)(2,1)S(1)} %pad_maximum_fusion.1.near_ref.near_0), channel_id=1, source_target_pairs={{0,2},{1,3},{2,0},{3,1},{4,6},{5,7},{6,4},{7,5},{8,10},{9,11},{10,... | collective-permute-start | bytes 196616 | tf_op jit(solution)/shard_map/ppermute | solution.py:367
  21.9 4.3 %collective-permute-start.3 = (bf16[4,64,128]{2,1,0:T(8,128)(2,1)S(1)}, bf16[4,64,128]{2,1,0:T(8,128)(2,1)S(1)}, u32[]{:S(2)}, u32[]{:S(2)}) collective-permute-start(bf16[4,64,128]{2,1,0:T(8,128)(2,1)S(1)} %pad_maximum_fusion.1.near_ref.near_0), channel_id=1, source_target_pairs={{0,1},{1,0},{2,3},{3,2},{4,5},{5,4},{6,7},{7,6},{8,9},{9,8},{10,11... | collective-permute-start | bytes 196616 | tf_op jit(solution)/shard_map/ppermute | solution.py:367
  26.2 6.4 %collective-permute-start.7 = (bf16[3,4,64,128]{3,2,1,0:T(8,128)(2,1)S(1)}, bf16[3,4,64,128]{3,2,1,0:T(8,128)(2,1)S(1)}, u32[]{:S(2)}, u32[]{:S(2)}) collective-permute-start(bf16[3,4,64,128]{3,2,1,0:T(8,128)(2,1)S(1)} %pad_maximum_fusion.near_ref), channel_id=1, source_target_pairs={{0,4},{4,0},{8,12},{12,8},{16,20},{20,16},{24,28},{28,24},{1,5},{5... | collective-permute-start | bytes 589832 | tf_op jit(solution)/shard_map/ppermute | solution.py:367
  26.2 1.5 %collective-permute-start.6 = (bf16[4,64,128]{2,1,0:T(8,128)(2,1)S(1)}, bf16[4,64,128]{2,1,0:T(8,128)(2,1)S(1)}, u32[]{:S(2)}, u32[]{:S(2)}) collective-permute-start(bf16[4,64,128]{2,1,0:T(8,128)(2,1)S(1)} %pad_maximum_fusion.1.near_ref.near_0), channel_id=1, source_target_pairs={{0,4},{4,0},{8,12},{12,8},{16,20},{20,16},{24,28},{28,24},{1,5},{5... | collective-permute-start | bytes 196616 | tf_op jit(solution)/shard_map/ppermute | solution.py:367
  27.8 1.4 %copy-start = (bf16[12,80,768]{2,1,0:T(8,128)(2,1)S(1)}, bf16[12,80,768]{2,1,0:T(8,128)(2,1)}, u32[]{:S(2)}) copy-start(bf16[12,80,768]{2,1,0:T(8,128)(2,1)} %get-tuple-element.12.tab_ref) | copy-start | bytes 4423684
  29.1 1.1 %copy-start.1 = (f32[14,80,80]{2,1,0:T(8,128)S(1)}, f32[14,80,80]{2,1,0:T(8,128)}, u32[]{:S(2)}) copy-start(f32[14,80,80]{2,1,0:T(8,128)} %get-tuple-element.13.sq_ref) | copy-start | bytes 1075204
  30.2 2.4 %copy-start.2 = (f32[14,80,80]{2,1,0:T(8,128)S(1)}, f32[14,80,80]{2,1,0:T(8,128)}, u32[]{:S(2)}) copy-start(f32[14,80,80]{2,1,0:T(8,128)} %get-tuple-element.13.sq_ref) | copy-start | bytes 1075204
  30.2 2.4 %copy-start.5 = (bf16[8,80,768]{2,1,0:T(8,128)(2,1)S(1)}, bf16[8,80,768]{2,1,0:T(8,128)(2,1)}, u32[]{:S(2)}) copy-start(bf16[8,80,768]{2,1,0:T(8,128)(2,1)} %get-tuple-element.14.av_ref) | copy-start | bytes 2949124
  32.6 34.9 %copy-start.3 = (f32[128,64]{0,1:T(8,128)S(1)}, f32[128,64]{0,1:T(8,128)}, u32[]{:S(2)}) copy-start(f32[128,64]{0,1:T(8,128)} %param.12) | copy-start | bytes 98308
  66.2 1.3 %collective-permute-start.9 = (f32[136,128]{1,0:T(8,128)S(1)}, f32[136,128]{1,0:T(8,128)S(1)}, u32[]{:S(2)}, u32[]{:S(2)}) collective-permute-start(f32[136,128]{1,0:T(8,128)S(1)} %get-tuple-element.17), channel_id=1, source_target_pairs={{0,4},{4,0},{8,12},{12,8},{16,20},{20,16},{24,28},{28,24},{1,5},{5... | collective-permute-start | bytes 208904 | tf_op jit(solution)/shard_map/ppermute | solution.py:367

commit v4 on v3

--- a/solution.py
+++ b/solution.py
@@ -13,7 +13,9 @@
 UROWS = 80
 GROUPS = 4
 CHUNK = 256
-UNROLL = 2
+UNROLL = 4
+PIECES = 2
+WIDE = 512
 LIM_TAB = 62500000
 EXACT = lax.Precision.HIGHEST
 VMEM = pl.BlockSpec(memory_space=pltpu.VMEM)
@@ -55,18 +57,26 @@
     return made
 
 
-def gained(made, gain, first, count, j, table_ref, square_ref):
-    low = made.astype(jnp.bfloat16)
-    for f in range(count):
-        block = low[f * UROWS : (f + 1) * UROWS, :]
-        square_ref[first + f] += nt_dot(block, block)
-    keep(low if gain is None else (made * gain).astype(jnp.bfloat16), first, count, j, table_ref)
-
-
-def keep(table, first, count, j, table_ref):
-    at = pl.multiple_of(j * CHUNK, CHUNK)
-    for f in range(count):
-        table_ref[first + f, :, pl.ds(at, CHUNK)] = table[f * UROWS : (f + 1) * UROWS, :]
+def span_of(j):
+    return pl.ds(pl.multiple_of(j * CHUNK, CHUNK), CHUNK)
+
+
+def spread_rows(made, count, channels, f):
+    shift = made[count * channels + f : count * channels + f + 1, :]
+    rest = (UROWS - channels, made.shape[1])
+    first = lax.broadcasted_iota(jnp.int32, rest, 0) == 0
+    return made[f * channels : (f + 1) * channels, :], jnp.where(first, jnp.broadcast_to(shift, rest), 0.0)
+
+
+def packed_shifts(rows, feature):
+    room = packed(len(rows)) - len(rows)
+    if room:
+        rows = rows + [jnp.zeros((room, feature), jnp.float32)]
+    return jnp.concatenate(rows, axis=0).astype(jnp.bfloat16)
+
+
+def packed(count):
+    return -(-count // 16) * 16
 
 
 def centred_patch(patch_ref):
@@ -74,21 +84,7 @@
     return patch - jnp.mean(patch, axis=-1, keepdims=True)
 
 
-def fill_rows(lhs, centred, which, step_ref, time_ref):
-    channels, feature = centred.shape
-    rest = UROWS - channels
-    first_row = lax.broadcasted_iota(jnp.int32, (rest, feature), 0) == 0
-    for n, frame in enumerate(which):
-        level = step_ref[frame]
-        shift = time_ref[0, pl.ds(level, 1), :]
-        scale = time_ref[1, pl.ds(level, 1), :]
-        lhs[n * UROWS : n * UROWS + channels, :] = (centred * (1.0 + scale)).astype(jnp.bfloat16)
-        lhs[n * UROWS + channels : (n + 1) * UROWS, :] = jnp.where(
-            first_row, jnp.broadcast_to(shift, (rest, feature)), 0.0
-        ).astype(jnp.bfloat16)
-
-
-def tables_kernel(frames, step_hbm, time_hbm, patch_hbm, qkv_hbm, q_gain_hbm, k_gain_hbm, out_hbm, head_hbm, tab_hbm, av_hbm, mix_hbm, sq_ref, step_ref, time_ref, patch_ref, head_ref, q_gain_ref, k_gain_ref, lhs, lhs_q, head_g, tab_ref, av_ref, mix_ref, obuf, wbuf, sems):
+def tables_kernel(frames, step_hbm, time_hbm, patch_hbm, qkv_hbm, q_gain_hbm, k_gain_hbm, out_hbm, head_hbm, tab_hbm, av_hbm, mix_hbm, sq_ref, step_ref, time_ref, patch_ref, head_ref, q_gain_ref, k_gain_ref, lhs, lhs_q, head_g, kv_ref, tab_ref, mix_ref, obuf, wbuf, sems):
     channels, feature = patch_ref.shape
     half = tab_ref.shape[2]
     count = half // CHUNK
@@ -110,56 +106,81 @@
 
     def fetch(part, j):
         base = (feature, 2 * feature, 0)[part]
-        at = pl.multiple_of(base + start + j * CHUNK, CHUNK)
-        slot = part * count + j
-        return pltpu.make_async_copy(qkv_hbm.at[:, pl.ds(at, CHUNK)], wbuf.at[slot], sems.at[big + slot])
-
-    for part in range(3):
-        for j in range(count):
+        at = pl.multiple_of(base + start, CHUNK)
+        slot = part * PIECES + j
+        rows = pl.ds(j * (feature // PIECES), feature // PIECES)
+        return pltpu.make_async_copy(
+            qkv_hbm.at[rows, pl.ds(at, half)], wbuf.at[rows, part * half : (part + 1) * half], sems.at[big + slot]
+        )
+
+    for part in (0, 1):
+        for j in range(PIECES):
             fetch(part, j).start()
-    after = big + 3 * count
+    after = big + 3 * PIECES
     out_copy = pltpu.make_async_copy(out_hbm.at[pl.ds(start, half), :], obuf, sems.at[after])
-    out_copy.start()
     for copy in small:
         copy.wait()
     centred = centred_patch(patch_ref)
-    fill_rows(lhs, centred, [frame_at(p, mine, frames) for p in range(frames)], step_ref, time_ref)
+    shifts = []
+    for place in range(frames):
+        level = step_ref[frame_at(place, mine, frames)]
+        shifts.append(time_ref[0, pl.ds(level, 1), :])
+        scale = time_ref[1, pl.ds(level, 1), :]
+        lhs[place * channels : (place + 1) * channels, :] = (centred * (1.0 + scale)).astype(jnp.bfloat16)
+    lhs[frames * channels :, :] = packed_shifts(shifts, feature)
     sq_ref[...] = jnp.zeros_like(sq_ref)
     sq_ref[frames + GROUPS, :channels, :channels] = nt_dot(centred, centred, precision=EXACT) / feature
 
-    def key_step(j, carry):
-        fetch(0, j).wait()
-        gained(nn_dot(lhs[...], wbuf[j]), None, 0, frames, j, tab_ref, sq_ref)
+    for part in (0, 1):
+        for j in range(PIECES):
+            fetch(part, j).wait()
+    for j in range(PIECES):
+        fetch(2, j).start()
+    out_copy.start()
+
+    def pair_step(j, carry):
+        span = pl.ds(pl.multiple_of(j * WIDE, WIDE), WIDE)
+        made = nn_dot(lhs[...], wbuf[:, span])
+        for f in range(frames):
+            top, tail = spread_rows(made, frames, channels, f)
+            kv_ref[f, :channels, span] = top.astype(jnp.bfloat16)
+            kv_ref[f, channels:, span] = tail.astype(jnp.bfloat16)
         return carry
 
-    lax.fori_loop(0, count, key_step, 0)
-    done = copies_of(((tab_ref.at[:frames], tab_hbm.at[:frames]),), sems, after + 1)
-
-    def value_step(j, carry):
-        fetch(1, j).wait()
-        keep(nn_dot(lhs[...], wbuf[count + j]).astype(jnp.bfloat16), 0, frames, j, av_ref)
-        return carry
-
-    lax.fori_loop(0, count, value_step, 0)
-    done += copies_of(((av_ref, av_hbm),), sems, after + 2)
+    lax.fori_loop(0, 2 * half // WIDE, pair_step, 0)
+    done = copies_of(
+        ((kv_ref.at[:, :, :half], tab_hbm.at[:frames]), (kv_ref.at[:, :, half:], av_hbm)), sems, after + 1
+    )
+    for f in range(frames):
+        block = kv_ref[f, :, :half]
+        sq_ref[f] = nt_dot(block, block)
     which = query_frames(mine, frames)
     head = head_ref[...].astype(jnp.float32)
     for g, frame in enumerate(which):
         place = place_of(frame, mine, frames)
-        lhs_q[g * UROWS : (g + 1) * UROWS, :] = lhs[pl.ds(pl.multiple_of(place * UROWS, 16), UROWS), :]
+        at = pl.ds(pl.multiple_of(place * channels, 16), channels)
+        lhs_q[g * channels : (g + 1) * channels, :] = lhs[at, :]
         gate = time_ref[2, pl.ds(step_ref[frame], 1), :]
         head_g[g * channels : (g + 1) * channels, :] = (head * gate).astype(jnp.bfloat16)
+    shifts = [time_ref[0, pl.ds(step_ref[frame], 1), :] for frame in which]
+    lhs_q[GROUPS * channels :, :] = packed_shifts(shifts, feature)
     sq_ref[frames + GROUPS + 1, :channels, :channels] = nt_dot(head_ref[...], patch_ref[...])
 
+    for j in range(PIECES):
+        fetch(2, j).wait()
+
     def query_step(j, carry):
-        fetch(2, j).wait()
-        span = pl.ds(pl.multiple_of(j * CHUNK, CHUNK), CHUNK)
-        gain = (q_gain_ref[span] * k_gain_ref[span]).reshape(1, CHUNK)
-        gained(nn_dot(lhs_q[...], wbuf[2 * count + j]), gain, frames, GROUPS, j, tab_ref, sq_ref)
+        gain = (q_gain_ref[span_of(j)] * k_gain_ref[span_of(j)]).reshape(1, CHUNK)
+        made = nn_dot(lhs_q[...], wbuf[:, pl.ds(pl.multiple_of(2 * half + j * CHUNK, CHUNK), CHUNK)])
+        for g in range(GROUPS):
+            both = jnp.concatenate(spread_rows(made, GROUPS, channels, g), axis=0)
+            low = both.astype(jnp.bfloat16)
+            sq_ref[frames + g] += nt_dot(low, low)
+            tab_ref[g, :, span_of(j)] = (both * gain).astype(jnp.bfloat16)
         return carry
 
     lax.fori_loop(0, count, query_step, 0)
-    done += copies_of(((tab_ref.at[frames:], tab_hbm.at[frames:]),), sems, after + 3)
+    done += copies_of(((tab_ref, tab_hbm.at[frames:]),), sems, after + 3)
     out_copy.wait()
     mixed = nt_dot(head_g[...], obuf[...]).astype(jnp.bfloat16)
     for g in range(GROUPS):
@@ -214,43 +235,38 @@
         asked_ref[h] = nn_dot(table, q_s[h]).astype(jnp.bfloat16)
 
 
-def each_portion(feature, sources, asked_ref, squares, gram, emit, safe=False):
+def each_portion(feature, z_s, asked_ref, squares, gram, emit, safe=False):
     heads = asked_ref.shape[0]
-    for blocks, first in sources:
-        held = blocks[0].shape[0]
-        step = min(len(blocks), 4)
-        ways = UNROLL if held % UNROLL == 0 else 1
-        for group in range(len(blocks) // step):
-            used = blocks[group * step : (group + 1) * step]
-
-            def run(i, carry, used=used, first=first, group=group, ways=ways):
-                items = []
-                for way in range(ways):
-                    inside = i * ways + way
-                    place = first + inside
-                    z = jnp.concatenate([block[inside] for block in used], axis=1)
-                    rows, factor = normed_rows(z, gram, squares(place), feature)
-                    key_rows = (rows * factor).T.astype(jnp.bfloat16)
-                    value_rows = rows.astype(jnp.bfloat16)
-                    items += [(h, place, key_rows, value_rows) for h in range(heads)]
-
-                def scores_of(item):
-                    h, place, key_rows, _ = item
-                    return nn_dot(key_rows, asked_ref[h, rows_at(place), :])
-
-                scores = scores_of(items[0])
-                for n, (h, place, unused, value_rows) in enumerate(items):
-                    top = None
-                    if safe:
-                        top = jnp.max(scores, axis=0, keepdims=True)
-                        scores = scores - top
-                    weights = jnp.exp2(scores).astype(jnp.bfloat16)
-                    if n + 1 < len(items):
-                        scores = scores_of(items[n + 1])
-                    emit(h, place, group, top, nn_dot(value_rows, weights))
-                return carry
-
-            lax.fori_loop(0, held // ways, run, 0)
+    groups, frames = z_s.shape[:2]
+    ways = UNROLL if frames % UNROLL == 0 else 1
+    for group in range(groups):
+
+        def run(i, carry, group=group):
+            items = []
+            for way in range(ways):
+                place = i * ways + way
+                rows, factor = normed_rows(z_s[group, place], gram, squares(place), feature)
+                key_rows = (rows * factor).T.astype(jnp.bfloat16)
+                value_rows = rows.astype(jnp.bfloat16)
+                items += [(h, place, key_rows, value_rows) for h in range(heads)]
+
+            def scores_of(item):
+                h, place, key_rows, _ = item
+                return nn_dot(key_rows, asked_ref[h, rows_at(place), :])
+
+            scores = scores_of(items[0])
+            for n, (h, place, unused, value_rows) in enumerate(items):
+                top = None
+                if safe:
+                    top = jnp.max(scores, axis=0, keepdims=True)
+                    scores = scores - top
+                weights = jnp.exp2(scores).astype(jnp.bfloat16)
+                if n + 1 < len(items):
+                    scores = scores_of(items[n + 1])
+                emit(h, place, group, top, nn_dot(value_rows, weights))
+            return carry
+
+        lax.fori_loop(0, frames // ways, run, 0)
 
 
 def squares_of(hk_ref, hk_far, frames):
@@ -262,17 +278,18 @@
     return pl.ds(pl.multiple_of(place * UROWS, 16), UROWS)
 
 
-def attend_kernel(frames, levels, feature, step_ref, near_0, near_ref, far_0, far_ref, asked_ref, av_ref, mix_ref, sq_ref, sq_far, kept_ref, given_ref, m_s, o_s, part_s):
+def attend_kernel(frames, levels, feature, step_ref, near_0, near_ref, far_0, far_ref, asked_ref, av_ref, mix_ref, sq_ref, sq_far, kept_ref, given_ref, z_s, m_s, o_s, part_s):
     mine = lax.axis_index("queue")
     core = mine & 1
     heads = asked_ref.shape[0]
     blocks, half, channels, tok = near_ref.shape
     gram = sq_ref[frames + GROUPS, :channels, :channels]
     squares = squares_of(sq_ref, sq_far, frames)
-    sources = tuple(
-        ([own] + [rest.at[b] for b in range(blocks)], first)
-        for own, rest, first in ((near_0, near_ref, 0), (far_0, far_ref, half))
-    )
+    step = z_s.shape[3] // tok
+    for n in range(blocks + 1):
+        at = slice((n % step) * tok, (n % step + 1) * tok)
+        z_s[n // step, :half, :, at] = near_0[...] if n == 0 else near_ref[n - 1]
+        z_s[n // step, half:, :, at] = far_0[...] if n == 0 else far_ref[n - 1]
 
     def emit(h, place, group, top, made):
         if group == 0:
@@ -280,7 +297,7 @@
         else:
             o_s[h, rows_at(place), :] += made
 
-    each_portion(feature, sources, asked_ref, squares, gram, emit)
+    each_portion(feature, z_s, asked_ref, squares, gram, emit)
 
     def total_weight(h):
         total = o_s[h, channels : channels + 1, :]
@@ -307,7 +324,7 @@
                 top - after
             )
 
-        each_portion(feature, sources, asked_ref, squares, gram, shifted, safe=True)
+        each_portion(feature, z_s, asked_ref, squares, gram, shifted, safe=True)
 
         def rescale(i, carry):
             for h in range(heads):
@@ -405,7 +422,6 @@
     half = feature // 2
     heads = half // HEAD_DIM
     tok = latent.shape[1]
-    count = half // CHUNK
     f32, bf16 = jnp.float32, jnp.bfloat16
     params = pltpu.CompilerParams(vmem_limit_bytes=(24 << 20) * max(1, frames // 8))
 
@@ -426,15 +442,17 @@
             pltpu.VMEM((channels, feature), bf16),
             pltpu.VMEM((half,), f32),
             pltpu.VMEM((half,), f32),
-            pltpu.VMEM((frames * UROWS, feature), bf16),
-            pltpu.VMEM((GROUPS * UROWS, feature), bf16),
+            pltpu.VMEM((frames * channels + packed(frames), feature), bf16),
+            pltpu.VMEM((GROUPS * channels + packed(GROUPS), feature), bf16),
             pltpu.VMEM((GROUPS * channels, feature), bf16),
         ]
-        + [pltpu.VMEM(*shape) for shape in made]
         + [
+            pltpu.VMEM((frames, UROWS, 2 * half), bf16),
+            pltpu.VMEM((GROUPS, UROWS, half), bf16),
+            pltpu.VMEM((GROUPS, channels, half), bf16),
             pltpu.VMEM((half, feature), bf16),
-            pltpu.VMEM((3 * count, feature, CHUNK), bf16),
-            pltpu.SemaphoreType.DMA((3 * count + 11,)),
+            pltpu.VMEM((feature, 3 * half), bf16),
+            pltpu.SemaphoreType.DMA((3 * PIECES + 11,)),
         ],
         compiler_params=pltpu.CompilerParams(vmem_limit_bytes=LIM_TAB),
         name="tables",
@@ -465,6 +483,7 @@
     near = jnp.concatenate(parts, axis=0)
     far = swapped(near, "queue", 1)
 
+    held = min(peers, 4)
     share = channels // frames
     sent = (2 * channels + share, tok)
     kept, given = pl.pallas_call(
@@ -473,6 +492,7 @@
         in_specs=[SMEM] + [VMEM] * 9,
         out_specs=[VMEM] * 2,
         scratch_shapes=[
+            pltpu.VMEM((peers // held, frames, channels, held * tok), bf16),
             pltpu.VMEM((heads, frames, rows), f32),
             pltpu.VMEM((heads, frames * UROWS, rows), f32),
             pltpu.VMEM((GROUPS, channels, tok), f32),

time: 68.4 us -> 66.9 us (0.978)
  Pallas kernels: 48 us -> 46.5 us
    pallas_call x1, Pallas kernels: 33.5 us -> 32.6 us  [one_step(): pl.pallas_call(functools.partial(attend_kernel, frames, levels, feature),...]
where the time goes in v4:
time: 66.9 us; the launch traced here: 66.7 us
  Pallas kernels  46.5 us (70%)
  starting transfers between devices  9.91 us (15%)
  waiting for transfers between devices  6.24 us (9%)
  local copies, waits for them, and re-layouts  2.46 us (4%)
  other arithmetic  0.8 us (1%)
  between operations  0.79 us (1%)
    pallas_call x1, Pallas kernels, one_step(): pl.pallas_call(functools.partial(attend_kernel, frames, levels, feature),...  32.6 us
    pallas_call x1, Pallas kernels, one_step(): pl.pallas_call(functools.partial(tables_kernel, frames), out_shape=shaped...  10.9 us
    ppermute x10, starting transfers between devices, swapped(): return lax.ppermute(value, axis, [(i, i ^ bit) for i in range(peers)])  9.91 us
    ppermute x10, waiting for transfers between devices, swapped(): return lax.ppermute(value, axis, [(i, i ^ bit) for i in range(peers)])  6.24 us
    unnamed x14, local copies, waits for them, and re-layouts  2.46 us
    pallas_call x1, Pallas kernels, one_step(): pl.pallas_call(functools.partial(ask_kernel, frames, feature), out_shape=...  2.39 us
  transfers between devices with their start and end apart: 10, of which 5 were waited for; matrix products, arithmetic and copies ran while one was open for 0% of the time, Pallas kernels for 20%

profile of v4, /device:TPU:0, one launch (start us, length us, event | category | flops | bytes accessed | tf_op | source)
XLA Modules:
  0.0 66.7 jit_solution(16628824250320596371)
XLA Ops:
  0.6 0.8 %convert_bitcast_fusion = bf16[1,64,128]{2,1,0:T(8,128)(2,1)S(1)} fusion(f32[1,128,64]{1,2,0:T(8,128)} %param.10), kind=kLoop, calls=%fused_computation.2 | loop fusion | flops 8192 | bytes 49152 | tf_op jit(solution)/shard_map/broadcast_in_dim | solution.py:462
  1.4 5.1 %collective-permute-start.2 = (bf16[1,64,128]{2,1,0:T(8,128)(2,1)S(1)}, bf16[1,64,128]{2,1,0:T(8,128)(2,1)S(1)}, u32[]{:S(2)}, u32[]{:S(2)}) collective-permute-start(bf16[1,64,128]{2,1,0:T(8,128)(2,1)S(1)} %convert_bitcast_fusion), channel_id=1, source_target_pairs={{0,24},{4,28},{8,16},{12,20},{16,8},{20,12},{24,0},{28,4},{1,25},{... | collective-permute-start | bytes 49160 | tf_op jit(solution)/shard_map/ppermute | solution.py:384
  6.5 0.0 collective-permute-start.1
  6.5 0.6 collective-permute-start
  7.0 10.9 %tables.1 = (bf16[12,80,768]{2,1,0:T(8,128)(2,1)}, bf16[8,80,768]{2,1,0:T(8,128)(2,1)}, bf16[4,64,768]{2,1,0:T(8,128)(2,1)}, f32[14,80,80]{2,1,0:T(8,128)}) custom-call(s32[8]{0:T(128)} %step_ref.1, f32[3,32,1536]{2,1,0:T(8,128)} %bitcast.19, bf16[64,1536]{1,0:T(8,128)(2,1)} %patch_hbm.1, bf16[1536,4608]{1,0:T(8,128)(2,1)} %qkv_hbm.1, f32[1536]{0:T(1024)} %q_gain_hbm.1, ...), custom_call_target="tpu_custom_call" | custom-call | tf_op jit(solution)/shard_map/tables/pallas_call | solution.py:433
  17.9 0.0 copy-start.4
  18.0 0.0 copy-start.6
  18.0 0.1 collective-permute-start.8
  18.0 0.0 collective-permute-done.2
  18.1 0.0 collective-permute-done.1
  18.1 0.0 collective-permute-done
  18.1 2.7 %collective-permute-start.5 = (bf16[4,64,128]{2,1,0:T(8,128)(2,1)S(1)}, bf16[4,64,128]{2,1,0:T(8,128)(2,1)S(1)}, u32[]{:S(2)}, u32[]{:S(2)}) collective-permute-start(bf16[4,64,128]{2,1,0:T(8,128)(2,1)S(1)} %pad_maximum_fusion.1.near_ref.near_0), channel_id=1, source_target_pairs={{0,3},{1,2},{2,1},{3,0},{4,7},{5,6},{6,5},{7,4},{8,11},{9,10},{10,... | collective-permute-start | bytes 196616 | tf_op jit(solution)/shard_map/ppermute | solution.py:384
  20.8 0.5 collective-permute-start.4
  21.3 0.3 collective-permute-start.3
  21.7 1.9 %collective-permute-done.5 = bf16[4,64,128]{2,1,0:T(8,128)(2,1)S(1)} collective-permute-done((bf16[4,64,128]{2,1,0:T(8,128)(2,1)S(1)}, bf16[4,64,128]{2,1,0:T(8,128)(2,1)S(1)}, u32[]{:S(2)}, u32[]{:S(2)}) %collective-permute-start.5) | collective-permute-done | bytes 65568 | tf_op jit(solution)/shard_map/ppermute | solution.py:384
  23.6 1.5 %collective-permute-done.4 = bf16[4,64,128]{2,1,0:T(8,128)(2,1)S(1)} collective-permute-done((bf16[4,64,128]{2,1,0:T(8,128)(2,1)S(1)}, bf16[4,64,128]{2,1,0:T(8,128)(2,1)S(1)}, u32[]{:S(2)}, u32[]{:S(2)}) %collective-permute-start.4) | collective-permute-done | bytes 65568 | tf_op jit(solution)/shard_map/ppermute | solution.py:384
  25.1 0.5 collective-permute-done.3
  25.6 0.1 collective-permute-start.7
  25.7 0.5 collective-permute-start.6
  26.2 1.0 %collective-permute-done.6.far_ref.far_0 = bf16[4,64,128]{2,1,0:T(8,128)(2,1)S(1)} collective-permute-done((bf16[4,64,128]{2,1,0:T(8,128)(2,1)S(1)}, bf16[4,64,128]{2,1,0:T(8,128)(2,1)S(1)}, u32[]{:S(2)}, u32[]{:S(2)}) %collective-permute-start.6) | collective-permute-done | bytes 65568 | tf_op jit(solution)/shard_map/ppermute | solution.py:384
  27.2 0.0 collective-permute-done.8.sq_far
  27.2 0.0 copy-start
  27.2 1.4 %copy-done = bf16[12,80,768]{2,1,0:T(8,128)(2,1)S(1)} copy-done((bf16[12,80,768]{2,1,0:T(8,128)(2,1)S(1)}, bf16[12,80,768]{2,1,0:T(8,128)(2,1)}, u32[]{:S(2)}) %copy-start) | copy-done | bytes 1474584
  28.6 0.0 copy-start.1
  28.6 1.1 %copy-done.1 = f32[14,80,80]{2,1,0:T(8,128)S(1)} copy-done((f32[14,80,80]{2,1,0:T(8,128)S(1)}, f32[14,80,80]{2,1,0:T(8,128)}, u32[]{:S(2)}) %copy-start.1) | copy-done | bytes 358424
  29.7 0.0 copy-start.2
  29.7 0.0 copy-start.5
  29.7 2.4 %ask.1.asked_ref = bf16[6,640,512]{2,1,0:T(8,128)(2,1)S(1)} custom-call(bf16[4,64,128]{2,1,0:T(8,128)(2,1)S(1)} %pad_maximum_fusion.1.near_ref.near_0, bf16[4,64,128]{2,1,0:T(8,128)(2,1)S(1)} %collective-permute-done.6.far_ref.far_0, bf16[12,80,768]{2,1,0:T(8,128)(2,1)S(1)} %copy-done, f32[14,80,80]{2,1,0:T(8,128)S(1)} %copy-done.1, ...), custom_call_target="tpu_custom_call" | custom-call | flops 1000000000 | bytes 4000000 | tf_op jit(solution)/shard_map/ask/pallas_call | solution.py:469
  32.1 0.0 collective-permute-done.7.far_ref
  32.1 0.0 copy-done.4
  32.1 0.0 copy-done.6
  32.1 0.0 copy-done.2
  32.1 0.0 copy-done.5
  32.1 0.0 copy-start.3
  32.1 32.6 %attend.1 = (f32[136,128]{1,0:T(8,128)S(1)}, f32[136,128]{1,0:T(8,128)S(1)}) custom-call(s32[8]{0:T(128)S(1)} %copy-done.4, bf16[4,64,128]{2,1,0:T(8,128)(2,1)S(1)} %pad_maximum_fusion.1.near_ref.near_0, bf16[3,4,64,128]{3,2,1,0:T(8,128)(2,1)S(1)} %pad_maximum_fusion.near_ref, bf16[4,64,128]{2,1,0:T(8,128)(2,1)S(1)} %collective-permute-done.6.far_ref.far_0, ...), custom_call_target="tpu_custom_call" | custom-call | flops 8000000000 | bytes 8000000 | tf_op jit(solution)/shard_map/attend/pallas_call | solution.py:489
  64.7 0.1 collective-permute-start.9
  64.8 1.2 %collective-permute-done.9.got_ref = f32[136,128]{1,0:T(8,128)S(1)} collective-permute-done((f32[136,128]{1,0:T(8,128)S(1)}, f32[136,128]{1,0:T(8,128)S(1)}, u32[]{:S(2)}, u32[]{:S(2)}) %collective-permute-start.9) | collective-permute-done | bytes 69664 | tf_op jit(solution)/shard_map/ppermute | solution.py:384
  66.0 0.0 copy-done.3
  66.0 0.6 finish.1
  (2 shorter events, 0.0 us)
Async XLA Ops:
  1.4 16.7 %collective-permute-start.2 = (bf16[1,64,128]{2,1,0:T(8,128)(2,1)S(1)}, bf16[1,64,128]{2,1,0:T(8,128)(2,1)S(1)}, u32[]{:S(2)}, u32[]{:S(2)}) collective-permute-start(bf16[1,64,128]{2,1,0:T(8,128)(2,1)S(1)} %convert_bitcast_fusion), channel_id=1, source_target_pairs={{0,24},{4,28},{8,16},{12,20},{16,8},{20,12},{24,0},{28,4},{1,25},{... | collective-permute-start | bytes 49160 | tf_op jit(solution)/shard_map/ppermute | solution.py:384
  6.5 11.6 %collective-permute-start.1 = (bf16[1,64,128]{2,1,0:T(8,128)(2,1)S(1)}, bf16[1,64,128]{2,1,0:T(8,128)(2,1)S(1)}, u32[]{:S(2)}, u32[]{:S(2)}) collective-permute-start(bf16[1,64,128]{2,1,0:T(8,128)(2,1)S(1)} %convert_bitcast_fusion), channel_id=1, source_target_pairs={{0,16},{4,20},{8,24},{12,28},{16,0},{20,4},{24,8},{28,12},{1,17},{... | collective-permute-start | bytes 49160 | tf_op jit(solution)/shard_map/ppermute | solution.py:384
  6.5 11.6 %collective-permute-start = (bf16[1,64,128]{2,1,0:T(8,128)(2,1)S(1)}, bf16[1,64,128]{2,1,0:T(8,128)(2,1)S(1)}, u32[]{:S(2)}, u32[]{:S(2)}) collective-permute-start(bf16[1,64,128]{2,1,0:T(8,128)(2,1)S(1)} %convert_bitcast_fusion), channel_id=1, source_target_pairs={{0,8},{4,12},{8,0},{12,4},{16,24},{20,28},{24,16},{28,20},{1,9},{5... | collective-permute-start | bytes 49160 | tf_op jit(solution)/shard_map/ppermute | solution.py:384
  17.9 14.1 %copy-start.4 = (s32[8]{0:T(128)S(1)}, s32[8]{0:T(128)}, u32[]{:S(2)}) copy-start(s32[8]{0:T(128)} %step_ref.1) | copy-start | bytes 100
  18.0 14.1 %copy-start.6 = (bf16[4,64,768]{2,1,0:T(8,128)(2,1)S(1)}, bf16[4,64,768]{2,1,0:T(8,128)(2,1)}, u32[]{:S(2)}) copy-start(bf16[4,64,768]{2,1,0:T(8,128)(2,1)} %get-tuple-element.15.mix_ref) | copy-start | bytes 1179652
  18.0 9.3 %collective-permute-start.8 = (f32[14,80,80]{2,1,0:T(8,128)}, f32[14,80,80]{2,1,0:T(8,128)S(1)}, u32[]{:S(2)}, u32[]{:S(2)}) collective-permute-start(f32[14,80,80]{2,1,0:T(8,128)} %get-tuple-element.13.sq_ref), channel_id=1, source_target_pairs={{0,4},{4,0},{8,12},{12,8},{16,20},{20,16},{24,28},{28,24},{1,5},{5... | collective-permute-start | bytes 1075208 | tf_op jit(solution)/shard_map/ppermute | solution.py:384
  18.1 5.5 %collective-permute-start.5 = (bf16[4,64,128]{2,1,0:T(8,128)(2,1)S(1)}, bf16[4,64,128]{2,1,0:T(8,128)(2,1)S(1)}, u32[]{:S(2)}, u32[]{:S(2)}) collective-permute-start(bf16[4,64,128]{2,1,0:T(8,128)(2,1)S(1)} %pad_maximum_fusion.1.near_ref.near_0), channel_id=1, source_target_pairs={{0,3},{1,2},{2,1},{3,0},{4,7},{5,6},{6,5},{7,4},{8,11},{9,10},{10,... | collective-permute-start | bytes 196616 | tf_op jit(solution)/shard_map/ppermute | solution.py:384
  20.8 4.3 %collective-permute-start.4 = (bf16[4,64,128]{2,1,0:T(8,128)(2,1)S(1)}, bf16[4,64,128]{2,1,0:T(8,128)(2,1)S(1)}, u32[]{:S(2)}, u32[]{:S(2)}) collective-permute-start(bf16[4,64,128]{2,1,0:T(8,128)(2,1)S(1)} %pad_maximum_fusion.1.near_ref.near_0), channel_id=1, source_target_pairs={{0,2},{1,3},{2,0},{3,1},{4,6},{5,7},{6,4},{7,5},{8,10},{9,11},{10,... | collective-permute-start | bytes 196616 | tf_op jit(solution)/shard_map/ppermute | solution.py:384
  21.3 4.3 %collective-permute-start.3 = (bf16[4,64,128]{2,1,0:T(8,128)(2,1)S(1)}, bf16[4,64,128]{2,1,0:T(8,128)(2,1)S(1)}, u32[]{:S(2)}, u32[]{:S(2)}) collective-permute-start(bf16[4,64,128]{2,1,0:T(8,128)(2,1)S(1)} %pad_maximum_fusion.1.near_ref.near_0), channel_id=1, source_target_pairs={{0,1},{1,0},{2,3},{3,2},{4,5},{5,4},{6,7},{7,6},{8,9},{9,8},{10,11... | collective-permute-start | bytes 196616 | tf_op jit(solution)/shard_map/ppermute | solution.py:384
  25.6 6.4 %collective-permute-start.7 = (bf16[3,4,64,128]{3,2,1,0:T(8,128)(2,1)S(1)}, bf16[3,4,64,128]{3,2,1,0:T(8,128)(2,1)S(1)}, u32[]{:S(2)}, u32[]{:S(2)}) collective-permute-start(bf16[3,4,64,128]{3,2,1,0:T(8,128)(2,1)S(1)} %pad_maximum_fusion.near_ref), channel_id=1, source_target_pairs={{0,4},{4,0},{8,12},{12,8},{16,20},{20,16},{24,28},{28,24},{1,5},{5... | collective-permute-start | bytes 589832 | tf_op jit(solution)/shard_map/ppermute | solution.py:384
  25.7 1.5 %collective-permute-start.6 = (bf16[4,64,128]{2,1,0:T(8,128)(2,1)S(1)}, bf16[4,64,128]{2,1,0:T(8,128)(2,1)S(1)}, u32[]{:S(2)}, u32[]{:S(2)}) collective-permute-start(bf16[4,64,128]{2,1,0:T(8,128)(2,1)S(1)} %pad_maximum_fusion.1.near_ref.near_0), channel_id=1, source_target_pairs={{0,4},{4,0},{8,12},{12,8},{16,20},{20,16},{24,28},{28,24},{1,5},{5... | collective-permute-start | bytes 196616 | tf_op jit(solution)/shard_map/ppermute | solution.py:384
  27.2 1.4 %copy-start = (bf16[12,80,768]{2,1,0:T(8,128)(2,1)S(1)}, bf16[12,80,768]{2,1,0:T(8,128)(2,1)}, u32[]{:S(2)}) copy-start(bf16[12,80,768]{2,1,0:T(8,128)(2,1)} %get-tuple-element.12.tab_ref) | copy-start | bytes 4423684
  28.6 1.1 %copy-start.1 = (f32[14,80,80]{2,1,0:T(8,128)S(1)}, f32[14,80,80]{2,1,0:T(8,128)}, u32[]{:S(2)}) copy-start(f32[14,80,80]{2,1,0:T(8,128)} %get-tuple-element.13.sq_ref) | copy-start | bytes 1075204
  29.7 2.4 %copy-start.2 = (f32[14,80,80]{2,1,0:T(8,128)S(1)}, f32[14,80,80]{2,1,0:T(8,128)}, u32[]{:S(2)}) copy-start(f32[14,80,80]{2,1,0:T(8,128)} %get-tuple-element.13.sq_ref) | copy-start | bytes 1075204
  29.7 2.4 %copy-start.5 = (bf16[8,80,768]{2,1,0:T(8,128)(2,1)S(1)}, bf16[8,80,768]{2,1,0:T(8,128)(2,1)}, u32[]{:S(2)}) copy-start(bf16[8,80,768]{2,1,0:T(8,128)(2,1)} %get-tuple-element.14.av_ref) | copy-start | bytes 2949124
  32.1 33.9 %copy-start.3 = (f32[128,64]{0,1:T(8,128)S(1)}, f32[128,64]{0,1:T(8,128)}, u32[]{:S(2)}) copy-start(f32[128,64]{0,1:T(8,128)} %param.12) | copy-start | bytes 98308
  64.7 1.3 %collective-permute-start.9 = (f32[136,128]{1,0:T(8,128)S(1)}, f32[136,128]{1,0:T(8,128)S(1)}, u32[]{:S(2)}, u32[]{:S(2)}) collective-permute-start(f32[136,128]{1,0:T(8,128)S(1)} %get-tuple-element.17), channel_id=1, source_target_pairs={{0,4},{4,0},{8,12},{12,8},{16,20},{20,16},{24,28},{28,24},{1,5},{5... | collective-permute-start | bytes 208904 | tf_op jit(solution)/shard_map/ppermute | solution.py:384

commit v5 on v4

--- a/solution.py
+++ b/solution.py
@@ -14,7 +14,6 @@
 GROUPS = 4
 CHUNK = 256
 UNROLL = 4
-PIECES = 2
 WIDE = 512
 LIM_TAB = 62500000
 EXACT = lax.Precision.HIGHEST
@@ -104,19 +103,16 @@
     )
     big = len(small)
 
-    def fetch(part, j):
-        base = (feature, 2 * feature, 0)[part]
-        at = pl.multiple_of(base + start, CHUNK)
-        slot = part * PIECES + j
-        rows = pl.ds(j * (feature // PIECES), feature // PIECES)
+    def fetch(n):
+        base = jnp.where(n < count, feature, jnp.where(n < 2 * count, 2 * feature - half, -2 * half))
+        at = pl.multiple_of(base + start + n * CHUNK, CHUNK)
         return pltpu.make_async_copy(
-            qkv_hbm.at[rows, pl.ds(at, half)], wbuf.at[rows, part * half : (part + 1) * half], sems.at[big + slot]
+            qkv_hbm.at[:, pl.ds(at, CHUNK)], wbuf.at[:, span_of(n)], sems.at[big + n]
         )
 
-    for part in (0, 1):
-        for j in range(PIECES):
-            fetch(part, j).start()
-    after = big + 3 * PIECES
+    for n in range(2 * count):
+        fetch(n).start()
+    after = big + 3 * count
     out_copy = pltpu.make_async_copy(out_hbm.at[pl.ds(start, half), :], obuf, sems.at[after])
     for copy in small:
         copy.wait()
@@ -131,14 +127,19 @@
     sq_ref[...] = jnp.zeros_like(sq_ref)
     sq_ref[frames + GROUPS, :channels, :channels] = nt_dot(centred, centred, precision=EXACT) / feature
 
-    for part in (0, 1):
-        for j in range(PIECES):
-            fetch(part, j).wait()
-    for j in range(PIECES):
-        fetch(2, j).start()
+    ratio = WIDE // CHUNK
+    for n in range(ratio):
+        fetch(n).wait()
+    for n in range(2 * count, 3 * count):
+        fetch(n).start()
     out_copy.start()
 
     def pair_step(j, carry):
+        @pl.when(j > 0)
+        def _():
+            for n in range(ratio):
+                fetch(j * ratio + n).wait()
+
         span = pl.ds(pl.multiple_of(j * WIDE, WIDE), WIDE)
         made = nn_dot(lhs[...], wbuf[:, span])
         for f in range(frames):
@@ -166,10 +167,9 @@
     lhs_q[GROUPS * channels :, :] = packed_shifts(shifts, feature)
     sq_ref[frames + GROUPS + 1, :channels, :channels] = nt_dot(head_ref[...], patch_ref[...])
 
-    for j in range(PIECES):
-        fetch(2, j).wait()
 
     def query_step(j, carry):
+        fetch(2 * count + j).wait()
         gain = (q_gain_ref[span_of(j)] * k_gain_ref[span_of(j)]).reshape(1, CHUNK)
         made = nn_dot(lhs_q[...], wbuf[:, pl.ds(pl.multiple_of(2 * half + j * CHUNK, CHUNK), CHUNK)])
         for g in range(GROUPS):
@@ -422,6 +422,7 @@
     half = feature // 2
     heads = half // HEAD_DIM
     tok = latent.shape[1]
+    count = half // CHUNK
     f32, bf16 = jnp.float32, jnp.bfloat16
     params = pltpu.CompilerParams(vmem_limit_bytes=(24 << 20) * max(1, frames // 8))
 
@@ -452,7 +453,7 @@
             pltpu.VMEM((GROUPS, channels, half), bf16),
             pltpu.VMEM((half, feature), bf16),
             pltpu.VMEM((feature, 3 * half), bf16),
-            pltpu.SemaphoreType.DMA((3 * PIECES + 11,)),
+            pltpu.SemaphoreType.DMA((3 * count + 11,)),
         ],
         compiler_params=pltpu.CompilerParams(vmem_limit_bytes=LIM_TAB),
         name="tables",

time: 66.9 us -> 66.1 us (0.988)
  Pallas kernels: 46.5 us -> 45.7 us
    pallas_call x1, Pallas kernels: 10.9 us -> 10.1 us  [one_step(): pl.pallas_call(functools.partial(tables_kernel, frames), out_shape=shaped...]
  transfers between devices with their start and end apart: 10 -> 10, of which waited for: 5 -> 5; matrix products, arithmetic and copies ran while one was open for 0% -> 0% of each run, Pallas kernels for 20% -> 19%
where the time goes in v5:
time: 66.1 us; the launch traced here: 65.8 us
  Pallas kernels  45.7 us (69%)
  starting transfers between devices  9.91 us (15%)
  waiting for transfers between devices  6.23 us (9%)
  local copies, waits for them, and re-layouts  2.46 us (4%)
  other arithmetic  0.8 us (1%)
  between operations  0.79 us (1%)
    pallas_call x1, Pallas kernels, one_step(): pl.pallas_call(functools.partial(attend_kernel, frames, levels, feature),...  32.6 us
    pallas_call x1, Pallas kernels, one_step(): pl.pallas_call(functools.partial(tables_kernel, frames), out_shape=shaped...  10.1 us
    ppermute x10, starting transfers between devices, swapped(): return lax.ppermute(value, axis, [(i, i ^ bit) for i in range(peers)])  9.91 us
    ppermute x10, waiting for transfers between devices, swapped(): return lax.ppermute(value, axis, [(i, i ^ bit) for i in range(peers)])  6.23 us
    unnamed x14, local copies, waits for them, and re-layouts  2.46 us
    pallas_call x1, Pallas kernels, one_step(): pl.pallas_call(functools.partial(ask_kernel, frames, feature), out_shape=...  2.39 us
  transfers between devices with their start and end apart: 10, of which 5 were waited for; matrix products, arithmetic and copies ran while one was open for 0% of the time, Pallas kernels for 19%

profile of v5, /device:TPU:0, one launch (start us, length us, event | category | flops | bytes accessed | tf_op | source)
XLA Modules:
  0.0 65.8 jit_solution(5764353181806078583)
XLA Ops:
  0.6 0.8 %convert_bitcast_fusion = bf16[1,64,128]{2,1,0:T(8,128)(2,1)S(1)} fusion(f32[1,128,64]{1,2,0:T(8,128)} %param.10), kind=kLoop, calls=%fused_computation.2 | loop fusion | flops 8192 | bytes 49152 | tf_op jit(solution)/shard_map/broadcast_in_dim | solution.py:463
  1.4 5.1 %collective-permute-start.2 = (bf16[1,64,128]{2,1,0:T(8,128)(2,1)S(1)}, bf16[1,64,128]{2,1,0:T(8,128)(2,1)S(1)}, u32[]{:S(2)}, u32[]{:S(2)}) collective-permute-start(bf16[1,64,128]{2,1,0:T(8,128)(2,1)S(1)} %convert_bitcast_fusion), channel_id=1, source_target_pairs={{0,24},{4,28},{8,16},{12,20},{16,8},{20,12},{24,0},{28,4},{1,25},{... | collective-permute-start | bytes 49160 | tf_op jit(solution)/shard_map/ppermute | solution.py:384
  6.5 0.0 collective-permute-start.1
  6.5 0.6 collective-permute-start
  7.0 10.1 %tables.1 = (bf16[12,80,768]{2,1,0:T(8,128)(2,1)}, bf16[8,80,768]{2,1,0:T(8,128)(2,1)}, bf16[4,64,768]{2,1,0:T(8,128)(2,1)}, f32[14,80,80]{2,1,0:T(8,128)}) custom-call(s32[8]{0:T(128)} %step_ref.1, f32[3,32,1536]{2,1,0:T(8,128)} %bitcast.19, bf16[64,1536]{1,0:T(8,128)(2,1)} %patch_hbm.1, bf16[1536,4608]{1,0:T(8,128)(2,1)} %qkv_hbm.1, f32[1536]{0:T(1024)} %q_gain_hbm.1, ...), custom_call_target="tpu_custom_call" | custom-call | tf_op jit(solution)/shard_map/tables/pallas_call | solution.py:434
  17.1 0.0 copy-start.4
  17.1 0.0 copy-start.6
  17.1 0.1 collective-permute-start.8
  17.2 0.0 collective-permute-done.2
  17.2 0.0 collective-permute-done.1
  17.2 0.0 collective-permute-done
  17.3 2.7 %collective-permute-start.5 = (bf16[4,64,128]{2,1,0:T(8,128)(2,1)S(1)}, bf16[4,64,128]{2,1,0:T(8,128)(2,1)S(1)}, u32[]{:S(2)}, u32[]{:S(2)}) collective-permute-start(bf16[4,64,128]{2,1,0:T(8,128)(2,1)S(1)} %pad_maximum_fusion.1.near_ref.near_0), channel_id=1, source_target_pairs={{0,3},{1,2},{2,1},{3,0},{4,7},{5,6},{6,5},{7,4},{8,11},{9,10},{10,... | collective-permute-start | bytes 196616 | tf_op jit(solution)/shard_map/ppermute | solution.py:384
  20.0 0.5 collective-permute-start.4
  20.5 0.3 collective-permute-start.3
  20.8 1.9 %collective-permute-done.5 = bf16[4,64,128]{2,1,0:T(8,128)(2,1)S(1)} collective-permute-done((bf16[4,64,128]{2,1,0:T(8,128)(2,1)S(1)}, bf16[4,64,128]{2,1,0:T(8,128)(2,1)S(1)}, u32[]{:S(2)}, u32[]{:S(2)}) %collective-permute-start.5) | collective-permute-done | bytes 65568 | tf_op jit(solution)/shard_map/ppermute | solution.py:384
  22.7 1.5 %collective-permute-done.4 = bf16[4,64,128]{2,1,0:T(8,128)(2,1)S(1)} collective-permute-done((bf16[4,64,128]{2,1,0:T(8,128)(2,1)S(1)}, bf16[4,64,128]{2,1,0:T(8,128)(2,1)S(1)}, u32[]{:S(2)}, u32[]{:S(2)}) %collective-permute-start.4) | collective-permute-done | bytes 65568 | tf_op jit(solution)/shard_map/ppermute | solution.py:384
  24.3 0.5 collective-permute-done.3
  24.8 0.1 collective-permute-start.7
  24.9 0.5 collective-permute-start.6
  25.4 1.0 %collective-permute-done.6.far_ref.far_0 = bf16[4,64,128]{2,1,0:T(8,128)(2,1)S(1)} collective-permute-done((bf16[4,64,128]{2,1,0:T(8,128)(2,1)S(1)}, bf16[4,64,128]{2,1,0:T(8,128)(2,1)S(1)}, u32[]{:S(2)}, u32[]{:S(2)}) %collective-permute-start.6) | collective-permute-done | bytes 65568 | tf_op jit(solution)/shard_map/ppermute | solution.py:384
  26.4 0.0 collective-permute-done.8.sq_far
  26.4 0.0 copy-start
  26.4 1.4 %copy-done = bf16[12,80,768]{2,1,0:T(8,128)(2,1)S(1)} copy-done((bf16[12,80,768]{2,1,0:T(8,128)(2,1)S(1)}, bf16[12,80,768]{2,1,0:T(8,128)(2,1)}, u32[]{:S(2)}) %copy-start) | copy-done | bytes 1474584
  27.8 0.0 copy-start.1
  27.8 1.1 %copy-done.1 = f32[14,80,80]{2,1,0:T(8,128)S(1)} copy-done((f32[14,80,80]{2,1,0:T(8,128)S(1)}, f32[14,80,80]{2,1,0:T(8,128)}, u32[]{:S(2)}) %copy-start.1) | copy-done | bytes 358424
  28.8 0.0 copy-start.2
  28.8 0.0 copy-start.5
  28.8 2.4 %ask.1.asked_ref = bf16[6,640,512]{2,1,0:T(8,128)(2,1)S(1)} custom-call(bf16[4,64,128]{2,1,0:T(8,128)(2,1)S(1)} %pad_maximum_fusion.1.near_ref.near_0, bf16[4,64,128]{2,1,0:T(8,128)(2,1)S(1)} %collective-permute-done.6.far_ref.far_0, bf16[12,80,768]{2,1,0:T(8,128)(2,1)S(1)} %copy-done, f32[14,80,80]{2,1,0:T(8,128)S(1)} %copy-done.1, ...), custom_call_target="tpu_custom_call" | custom-call | flops 1000000000 | bytes 4000000 | tf_op jit(solution)/shard_map/ask/pallas_call | solution.py:470
  31.2 0.0 collective-permute-done.7.far_ref
  31.3 0.0 copy-done.4
  31.3 0.0 copy-done.6
  31.3 0.0 copy-done.2
  31.3 0.0 copy-done.5
  31.3 0.0 copy-start.3
  31.3 32.6 %attend.1 = (f32[136,128]{1,0:T(8,128)S(1)}, f32[136,128]{1,0:T(8,128)S(1)}) custom-call(s32[8]{0:T(128)S(1)} %copy-done.4, bf16[4,64,128]{2,1,0:T(8,128)(2,1)S(1)} %pad_maximum_fusion.1.near_ref.near_0, bf16[3,4,64,128]{3,2,1,0:T(8,128)(2,1)S(1)} %pad_maximum_fusion.near_ref, bf16[4,64,128]{2,1,0:T(8,128)(2,1)S(1)} %collective-permute-done.6.far_ref.far_0, ...), custom_call_target="tpu_custom_call" | custom-call | flops 8000000000 | bytes 8000000 | tf_op jit(solution)/shard_map/attend/pallas_call | solution.py:490
  63.9 0.1 collective-permute-start.9
  63.9 1.2 %collective-permute-done.9.got_ref = f32[136,128]{1,0:T(8,128)S(1)} collective-permute-done((f32[136,128]{1,0:T(8,128)S(1)}, f32[136,128]{1,0:T(8,128)S(1)}, u32[]{:S(2)}, u32[]{:S(2)}) %collective-permute-start.9) | collective-permute-done | bytes 69664 | tf_op jit(solution)/shard_map/ppermute | solution.py:384
  65.2 0.0 copy-done.3
  65.2 0.6 finish.1
  (2 shorter events, 0.0 us)
Async XLA Ops:
  1.4 15.8 %collective-permute-start.2 = (bf16[1,64,128]{2,1,0:T(8,128)(2,1)S(1)}, bf16[1,64,128]{2,1,0:T(8,128)(2,1)S(1)}, u32[]{:S(2)}, u32[]{:S(2)}) collective-permute-start(bf16[1,64,128]{2,1,0:T(8,128)(2,1)S(1)} %convert_bitcast_fusion), channel_id=1, source_target_pairs={{0,24},{4,28},{8,16},{12,20},{16,8},{20,12},{24,0},{28,4},{1,25},{... | collective-permute-start | bytes 49160 | tf_op jit(solution)/shard_map/ppermute | solution.py:384
  6.5 10.8 %collective-permute-start.1 = (bf16[1,64,128]{2,1,0:T(8,128)(2,1)S(1)}, bf16[1,64,128]{2,1,0:T(8,128)(2,1)S(1)}, u32[]{:S(2)}, u32[]{:S(2)}) collective-permute-start(bf16[1,64,128]{2,1,0:T(8,128)(2,1)S(1)} %convert_bitcast_fusion), channel_id=1, source_target_pairs={{0,16},{4,20},{8,24},{12,28},{16,0},{20,4},{24,8},{28,12},{1,17},{... | collective-permute-start | bytes 49160 | tf_op jit(solution)/shard_map/ppermute | solution.py:384
  6.5 10.8 %collective-permute-start = (bf16[1,64,128]{2,1,0:T(8,128)(2,1)S(1)}, bf16[1,64,128]{2,1,0:T(8,128)(2,1)S(1)}, u32[]{:S(2)}, u32[]{:S(2)}) collective-permute-start(bf16[1,64,128]{2,1,0:T(8,128)(2,1)S(1)} %convert_bitcast_fusion), channel_id=1, source_target_pairs={{0,8},{4,12},{8,0},{12,4},{16,24},{20,28},{24,16},{28,20},{1,9},{5... | collective-permute-start | bytes 49160 | tf_op jit(solution)/shard_map/ppermute | solution.py:384
  17.1 14.1 %copy-start.4 = (s32[8]{0:T(128)S(1)}, s32[8]{0:T(128)}, u32[]{:S(2)}) copy-start(s32[8]{0:T(128)} %step_ref.1) | copy-start | bytes 100
  17.1 14.1 %copy-start.6 = (bf16[4,64,768]{2,1,0:T(8,128)(2,1)S(1)}, bf16[4,64,768]{2,1,0:T(8,128)(2,1)}, u32[]{:S(2)}) copy-start(bf16[4,64,768]{2,1,0:T(8,128)(2,1)} %get-tuple-element.15.mix_ref) | copy-start | bytes 1179652
  17.1 9.3 %collective-permute-start.8 = (f32[14,80,80]{2,1,0:T(8,128)}, f32[14,80,80]{2,1,0:T(8,128)S(1)}, u32[]{:S(2)}, u32[]{:S(2)}) collective-permute-start(f32[14,80,80]{2,1,0:T(8,128)} %get-tuple-element.13.sq_ref), channel_id=1, source_target_pairs={{0,4},{4,0},{8,12},{12,8},{16,20},{20,16},{24,28},{28,24},{1,5},{5... | collective-permute-start | bytes 1075208 | tf_op jit(solution)/shard_map/ppermute | solution.py:384
  17.3 5.5 %collective-permute-start.5 = (bf16[4,64,128]{2,1,0:T(8,128)(2,1)S(1)}, bf16[4,64,128]{2,1,0:T(8,128)(2,1)S(1)}, u32[]{:S(2)}, u32[]{:S(2)}) collective-permute-start(bf16[4,64,128]{2,1,0:T(8,128)(2,1)S(1)} %pad_maximum_fusion.1.near_ref.near_0), channel_id=1, source_target_pairs={{0,3},{1,2},{2,1},{3,0},{4,7},{5,6},{6,5},{7,4},{8,11},{9,10},{10,... | collective-permute-start | bytes 196616 | tf_op jit(solution)/shard_map/ppermute | solution.py:384
  20.0 4.3 %collective-permute-start.4 = (bf16[4,64,128]{2,1,0:T(8,128)(2,1)S(1)}, bf16[4,64,128]{2,1,0:T(8,128)(2,1)S(1)}, u32[]{:S(2)}, u32[]{:S(2)}) collective-permute-start(bf16[4,64,128]{2,1,0:T(8,128)(2,1)S(1)} %pad_maximum_fusion.1.near_ref.near_0), channel_id=1, source_target_pairs={{0,2},{1,3},{2,0},{3,1},{4,6},{5,7},{6,4},{7,5},{8,10},{9,11},{10,... | collective-permute-start | bytes 196616 | tf_op jit(solution)/shard_map/ppermute | solution.py:384
  20.5 4.3 %collective-permute-start.3 = (bf16[4,64,128]{2,1,0:T(8,128)(2,1)S(1)}, bf16[4,64,128]{2,1,0:T(8,128)(2,1)S(1)}, u32[]{:S(2)}, u32[]{:S(2)}) collective-permute-start(bf16[4,64,128]{2,1,0:T(8,128)(2,1)S(1)} %pad_maximum_fusion.1.near_ref.near_0), channel_id=1, source_target_pairs={{0,1},{1,0},{2,3},{3,2},{4,5},{5,4},{6,7},{7,6},{8,9},{9,8},{10,11... | collective-permute-start | bytes 196616 | tf_op jit(solution)/shard_map/ppermute | solution.py:384
  24.8 6.4 %collective-permute-start.7 = (bf16[3,4,64,128]{3,2,1,0:T(8,128)(2,1)S(1)}, bf16[3,4,64,128]{3,2,1,0:T(8,128)(2,1)S(1)}, u32[]{:S(2)}, u32[]{:S(2)}) collective-permute-start(bf16[3,4,64,128]{3,2,1,0:T(8,128)(2,1)S(1)} %pad_maximum_fusion.near_ref), channel_id=1, source_target_pairs={{0,4},{4,0},{8,12},{12,8},{16,20},{20,16},{24,28},{28,24},{1,5},{5... | collective-permute-start | bytes 589832 | tf_op jit(solution)/shard_map/ppermute | solution.py:384
  24.9 1.5 %collective-permute-start.6 = (bf16[4,64,128]{2,1,0:T(8,128)(2,1)S(1)}, bf16[4,64,128]{2,1,0:T(8,128)(2,1)S(1)}, u32[]{:S(2)}, u32[]{:S(2)}) collective-permute-start(bf16[4,64,128]{2,1,0:T(8,128)(2,1)S(1)} %pad_maximum_fusion.1.near_ref.near_0), channel_id=1, source_target_pairs={{0,4},{4,0},{8,12},{12,8},{16,20},{20,16},{24,28},{28,24},{1,5},{5... | collective-permute-start | bytes 196616 | tf_op jit(solution)/shard_map/ppermute | solution.py:384
  26.4 1.4 %copy-start = (bf16[12,80,768]{2,1,0:T(8,128)(2,1)S(1)}, bf16[12,80,768]{2,1,0:T(8,128)(2,1)}, u32[]{:S(2)}) copy-start(bf16[12,80,768]{2,1,0:T(8,128)(2,1)} %get-tuple-element.12.tab_ref) | copy-start | bytes 4423684
  27.8 1.1 %copy-start.1 = (f32[14,80,80]{2,1,0:T(8,128)S(1)}, f32[14,80,80]{2,1,0:T(8,128)}, u32[]{:S(2)}) copy-start(f32[14,80,80]{2,1,0:T(8,128)} %get-tuple-element.13.sq_ref) | copy-start | bytes 1075204
  28.8 2.4 %copy-start.2 = (f32[14,80,80]{2,1,0:T(8,128)S(1)}, f32[14,80,80]{2,1,0:T(8,128)}, u32[]{:S(2)}) copy-start(f32[14,80,80]{2,1,0:T(8,128)} %get-tuple-element.13.sq_ref) | copy-start | bytes 1075204
  28.8 2.4 %copy-start.5 = (bf16[8,80,768]{2,1,0:T(8,128)(2,1)S(1)}, bf16[8,80,768]{2,1,0:T(8,128)(2,1)}, u32[]{:S(2)}) copy-start(bf16[8,80,768]{2,1,0:T(8,128)(2,1)} %get-tuple-element.14.av_ref) | copy-start | bytes 2949124
  31.3 33.9 %copy-start.3 = (f32[128,64]{0,1:T(8,128)S(1)}, f32[128,64]{0,1:T(8,128)}, u32[]{:S(2)}) copy-start(f32[128,64]{0,1:T(8,128)} %param.12) | copy-start | bytes 98308
  63.9 1.3 %collective-permute-start.9 = (f32[136,128]{1,0:T(8,128)S(1)}, f32[136,128]{1,0:T(8,128)S(1)}, u32[]{:S(2)}, u32[]{:S(2)}) collective-permute-start(f32[136,128]{1,0:T(8,128)S(1)} %get-tuple-element.17), channel_id=1, source_target_pairs={{0,4},{4,0},{8,12},{12,8},{16,20},{20,16},{24,28},{28,24},{1,5},{5... | collective-permute-start | bytes 208904 | tf_op jit(solution)/shard_map/ppermute | solution.py:384

commit v6 on v5

--- a/solution.py
+++ b/solution.py
@@ -14,9 +14,8 @@
 GROUPS = 4
 CHUNK = 256
 UNROLL = 4
-WIDE = 512
+WIDE = 768
 LIM_TAB = 62500000
-EXACT = lax.Precision.HIGHEST
 VMEM = pl.BlockSpec(memory_space=pltpu.VMEM)
 SMEM = pl.BlockSpec(memory_space=pltpu.SMEM)
 HBM = pl.BlockSpec(memory_space=pltpu.HBM)
@@ -125,7 +124,9 @@
         lhs[place * channels : (place + 1) * channels, :] = (centred * (1.0 + scale)).astype(jnp.bfloat16)
     lhs[frames * channels :, :] = packed_shifts(shifts, feature)
     sq_ref[...] = jnp.zeros_like(sq_ref)
-    sq_ref[frames + GROUPS, :channels, :channels] = nt_dot(centred, centred, precision=EXACT) / feature
+    high, low = split(centred)
+    crossed = nt_dot(high, high) + nt_dot(high, low) + nt_dot(low, high)
+    sq_ref[frames + GROUPS, :channels, :channels] = crossed / feature
 
     ratio = WIDE // CHUNK
     for n in range(ratio):
@@ -168,18 +169,15 @@
     sq_ref[frames + GROUPS + 1, :channels, :channels] = nt_dot(head_ref[...], patch_ref[...])
 
 
-    def query_step(j, carry):
-        fetch(2 * count + j).wait()
-        gain = (q_gain_ref[span_of(j)] * k_gain_ref[span_of(j)]).reshape(1, CHUNK)
-        made = nn_dot(lhs_q[...], wbuf[:, pl.ds(pl.multiple_of(2 * half + j * CHUNK, CHUNK), CHUNK)])
-        for g in range(GROUPS):
-            both = jnp.concatenate(spread_rows(made, GROUPS, channels, g), axis=0)
-            low = both.astype(jnp.bfloat16)
-            sq_ref[frames + g] += nt_dot(low, low)
-            tab_ref[g, :, span_of(j)] = (both * gain).astype(jnp.bfloat16)
-        return carry
-
-    lax.fori_loop(0, count, query_step, 0)
+    for n in range(2 * count, 3 * count):
+        fetch(n).wait()
+    gain = (q_gain_ref[...] * k_gain_ref[...]).reshape(1, half)
+    made = nn_dot(lhs_q[...], wbuf[:, 2 * half :])
+    for g in range(GROUPS):
+        both = jnp.concatenate(spread_rows(made, GROUPS, channels, g), axis=0)
+        low = both.astype(jnp.bfloat16)
+        sq_ref[frames + g] = nt_dot(low, low)
+        tab_ref[g] = (both * gain).astype(jnp.bfloat16)
     done += copies_of(((tab_ref, tab_hbm.at[frames:]),), sems, after + 3)
     out_copy.wait()
     mixed = nt_dot(head_g[...], obuf[...]).astype(jnp.bfloat16)

time: 66.1 us -> 65.9 us (level)
  no operation moved by 1% of the time
where the time goes in v6:
time: 65.9 us; the launch traced here: 65.6 us
  Pallas kernels  45.5 us (69%)
  starting transfers between devices  9.91 us (15%)
  waiting for transfers between devices  6.22 us (9%)
  local copies, waits for them, and re-layouts  2.46 us (4%)
  other arithmetic  0.8 us (1%)
  between operations  0.79 us (1%)
    pallas_call x1, Pallas kernels, one_step(): pl.pallas_call(functools.partial(attend_kernel, frames, levels, feature),...  32.6 us
    ppermute x10, starting transfers between devices, swapped(): return lax.ppermute(value, axis, [(i, i ^ bit) for i in range(peers)])  9.91 us
    pallas_call x1, Pallas kernels, one_step(): pl.pallas_call(functools.partial(tables_kernel, frames), out_shape=shaped...  9.89 us
    ppermute x10, waiting for transfers between devices, swapped(): return lax.ppermute(value, axis, [(i, i ^ bit) for i in range(peers)])  6.22 us
    unnamed x14, local copies, waits for them, and re-layouts  2.46 us
    pallas_call x1, Pallas kernels, one_step(): pl.pallas_call(functools.partial(ask_kernel, frames, feature), out_shape=...  2.39 us
  transfers between devices with their start and end apart: 10, of which 5 were waited for; matrix products, arithmetic and copies ran while one was open for 0% of the time, Pallas kernels for 19%

profile of v6, /device:TPU:0, one launch (start us, length us, event | category | flops | bytes accessed | tf_op | source)
XLA Modules:
  0.0 65.6 jit_solution(10554629840798799582)
XLA Ops:
  0.6 0.8 %convert_bitcast_fusion = bf16[1,64,128]{2,1,0:T(8,128)(2,1)S(1)} fusion(f32[1,128,64]{1,2,0:T(8,128)} %param.10), kind=kLoop, calls=%fused_computation.2 | loop fusion | flops 8192 | bytes 49152 | tf_op jit(solution)/shard_map/broadcast_in_dim | solution.py:461
  1.4 5.1 %collective-permute-start.2 = (bf16[1,64,128]{2,1,0:T(8,128)(2,1)S(1)}, bf16[1,64,128]{2,1,0:T(8,128)(2,1)S(1)}, u32[]{:S(2)}, u32[]{:S(2)}) collective-permute-start(bf16[1,64,128]{2,1,0:T(8,128)(2,1)S(1)} %convert_bitcast_fusion), channel_id=1, source_target_pairs={{0,24},{4,28},{8,16},{12,20},{16,8},{20,12},{24,0},{28,4},{1,25},{... | collective-permute-start | bytes 49160 | tf_op jit(solution)/shard_map/ppermute | solution.py:382
  6.5 0.0 collective-permute-start.1
  6.5 0.6 collective-permute-start
  7.0 9.9 %tables.1 = (bf16[12,80,768]{2,1,0:T(8,128)(2,1)}, bf16[8,80,768]{2,1,0:T(8,128)(2,1)}, bf16[4,64,768]{2,1,0:T(8,128)(2,1)}, f32[14,80,80]{2,1,0:T(8,128)}) custom-call(s32[8]{0:T(128)} %step_ref.1, f32[3,32,1536]{2,1,0:T(8,128)} %bitcast.19, bf16[64,1536]{1,0:T(8,128)(2,1)} %patch_hbm.1, bf16[1536,4608]{1,0:T(8,128)(2,1)} %qkv_hbm.1, f32[1536]{0:T(1024)} %q_gain_hbm.1, ...), custom_call_target="tpu_custom_call" | custom-call | tf_op jit(solution)/shard_map/tables/pallas_call | solution.py:432
  16.9 0.0 copy-start.4
  16.9 0.0 copy-start.6
  17.0 0.1 collective-permute-start.8
  17.0 0.0 collective-permute-done.2
  17.0 0.0 collective-permute-done.1
  17.1 0.0 collective-permute-done
  17.1 2.7 %collective-permute-start.5 = (bf16[4,64,128]{2,1,0:T(8,128)(2,1)S(1)}, bf16[4,64,128]{2,1,0:T(8,128)(2,1)S(1)}, u32[]{:S(2)}, u32[]{:S(2)}) collective-permute-start(bf16[4,64,128]{2,1,0:T(8,128)(2,1)S(1)} %pad_maximum_fusion.1.near_ref.near_0), channel_id=1, source_target_pairs={{0,3},{1,2},{2,1},{3,0},{4,7},{5,6},{6,5},{7,4},{8,11},{9,10},{10,... | collective-permute-start | bytes 196616 | tf_op jit(solution)/shard_map/ppermute | solution.py:382
  19.8 0.5 collective-permute-start.4
  20.3 0.3 collective-permute-start.3
  20.6 1.9 %collective-permute-done.5 = bf16[4,64,128]{2,1,0:T(8,128)(2,1)S(1)} collective-permute-done((bf16[4,64,128]{2,1,0:T(8,128)(2,1)S(1)}, bf16[4,64,128]{2,1,0:T(8,128)(2,1)S(1)}, u32[]{:S(2)}, u32[]{:S(2)}) %collective-permute-start.5) | collective-permute-done | bytes 65568 | tf_op jit(solution)/shard_map/ppermute | solution.py:382
  22.5 1.5 %collective-permute-done.4 = bf16[4,64,128]{2,1,0:T(8,128)(2,1)S(1)} collective-permute-done((bf16[4,64,128]{2,1,0:T(8,128)(2,1)S(1)}, bf16[4,64,128]{2,1,0:T(8,128)(2,1)S(1)}, u32[]{:S(2)}, u32[]{:S(2)}) %collective-permute-start.4) | collective-permute-done | bytes 65568 | tf_op jit(solution)/shard_map/ppermute | solution.py:382
  24.1 0.5 collective-permute-done.3
  24.6 0.1 collective-permute-start.7
  24.7 0.5 collective-permute-start.6
  25.2 1.0 %collective-permute-done.6.far_ref.far_0 = bf16[4,64,128]{2,1,0:T(8,128)(2,1)S(1)} collective-permute-done((bf16[4,64,128]{2,1,0:T(8,128)(2,1)S(1)}, bf16[4,64,128]{2,1,0:T(8,128)(2,1)S(1)}, u32[]{:S(2)}, u32[]{:S(2)}) %collective-permute-start.6) | collective-permute-done | bytes 65568 | tf_op jit(solution)/shard_map/ppermute | solution.py:382
  26.2 0.0 collective-permute-done.8.sq_far
  26.2 0.0 copy-start
  26.2 1.4 %copy-done = bf16[12,80,768]{2,1,0:T(8,128)(2,1)S(1)} copy-done((bf16[12,80,768]{2,1,0:T(8,128)(2,1)S(1)}, bf16[12,80,768]{2,1,0:T(8,128)(2,1)}, u32[]{:S(2)}) %copy-start) | copy-done | bytes 1474584
  27.6 0.0 copy-start.1
  27.6 1.1 %copy-done.1 = f32[14,80,80]{2,1,0:T(8,128)S(1)} copy-done((f32[14,80,80]{2,1,0:T(8,128)S(1)}, f32[14,80,80]{2,1,0:T(8,128)}, u32[]{:S(2)}) %copy-start.1) | copy-done | bytes 358424
  28.6 0.0 copy-start.2
  28.6 0.0 copy-start.5
  28.6 2.4 %ask.1.asked_ref = bf16[6,640,512]{2,1,0:T(8,128)(2,1)S(1)} custom-call(bf16[4,64,128]{2,1,0:T(8,128)(2,1)S(1)} %pad_maximum_fusion.1.near_ref.near_0, bf16[4,64,128]{2,1,0:T(8,128)(2,1)S(1)} %collective-permute-done.6.far_ref.far_0, bf16[12,80,768]{2,1,0:T(8,128)(2,1)S(1)} %copy-done, f32[14,80,80]{2,1,0:T(8,128)S(1)} %copy-done.1, ...), custom_call_target="tpu_custom_call" | custom-call | flops 1000000000 | bytes 4000000 | tf_op jit(solution)/shard_map/ask/pallas_call | solution.py:468
  31.0 0.0 collective-permute-done.7.far_ref
  31.1 0.0 copy-done.4
  31.1 0.0 copy-done.6
  31.1 0.0 copy-done.2
  31.1 0.0 copy-done.5
  31.1 0.0 copy-start.3
  31.1 32.6 %attend.1 = (f32[136,128]{1,0:T(8,128)S(1)}, f32[136,128]{1,0:T(8,128)S(1)}) custom-call(s32[8]{0:T(128)S(1)} %copy-done.4, bf16[4,64,128]{2,1,0:T(8,128)(2,1)S(1)} %pad_maximum_fusion.1.near_ref.near_0, bf16[3,4,64,128]{3,2,1,0:T(8,128)(2,1)S(1)} %pad_maximum_fusion.near_ref, bf16[4,64,128]{2,1,0:T(8,128)(2,1)S(1)} %collective-permute-done.6.far_ref.far_0, ...), custom_call_target="tpu_custom_call" | custom-call | flops 8000000000 | bytes 8000000 | tf_op jit(solution)/shard_map/attend/pallas_call | solution.py:488
  63.7 0.1 collective-permute-start.9
  63.7 1.2 %collective-permute-done.9.got_ref = f32[136,128]{1,0:T(8,128)S(1)} collective-permute-done((f32[136,128]{1,0:T(8,128)S(1)}, f32[136,128]{1,0:T(8,128)S(1)}, u32[]{:S(2)}, u32[]{:S(2)}) %collective-permute-start.9) | collective-permute-done | bytes 69664 | tf_op jit(solution)/shard_map/ppermute | solution.py:382
  65.0 0.0 copy-done.3
  65.0 0.6 finish.1
  (2 shorter events, 0.0 us)
Async XLA Ops:
  1.4 15.6 %collective-permute-start.2 = (bf16[1,64,128]{2,1,0:T(8,128)(2,1)S(1)}, bf16[1,64,128]{2,1,0:T(8,128)(2,1)S(1)}, u32[]{:S(2)}, u32[]{:S(2)}) collective-permute-start(bf16[1,64,128]{2,1,0:T(8,128)(2,1)S(1)} %convert_bitcast_fusion), channel_id=1, source_target_pairs={{0,24},{4,28},{8,16},{12,20},{16,8},{20,12},{24,0},{28,4},{1,25},{... | collective-permute-start | bytes 49160 | tf_op jit(solution)/shard_map/ppermute | solution.py:382
  6.5 10.6 %collective-permute-start.1 = (bf16[1,64,128]{2,1,0:T(8,128)(2,1)S(1)}, bf16[1,64,128]{2,1,0:T(8,128)(2,1)S(1)}, u32[]{:S(2)}, u32[]{:S(2)}) collective-permute-start(bf16[1,64,128]{2,1,0:T(8,128)(2,1)S(1)} %convert_bitcast_fusion), channel_id=1, source_target_pairs={{0,16},{4,20},{8,24},{12,28},{16,0},{20,4},{24,8},{28,12},{1,17},{... | collective-permute-start | bytes 49160 | tf_op jit(solution)/shard_map/ppermute | solution.py:382
  6.5 10.6 %collective-permute-start = (bf16[1,64,128]{2,1,0:T(8,128)(2,1)S(1)}, bf16[1,64,128]{2,1,0:T(8,128)(2,1)S(1)}, u32[]{:S(2)}, u32[]{:S(2)}) collective-permute-start(bf16[1,64,128]{2,1,0:T(8,128)(2,1)S(1)} %convert_bitcast_fusion), channel_id=1, source_target_pairs={{0,8},{4,12},{8,0},{12,4},{16,24},{20,28},{24,16},{28,20},{1,9},{5... | collective-permute-start | bytes 49160 | tf_op jit(solution)/shard_map/ppermute | solution.py:382
  16.9 14.1 %copy-start.4 = (s32[8]{0:T(128)S(1)}, s32[8]{0:T(128)}, u32[]{:S(2)}) copy-start(s32[8]{0:T(128)} %step_ref.1) | copy-start | bytes 100
  16.9 14.1 %copy-start.6 = (bf16[4,64,768]{2,1,0:T(8,128)(2,1)S(1)}, bf16[4,64,768]{2,1,0:T(8,128)(2,1)}, u32[]{:S(2)}) copy-start(bf16[4,64,768]{2,1,0:T(8,128)(2,1)} %get-tuple-element.15.mix_ref) | copy-start | bytes 1179652
  17.0 9.3 %collective-permute-start.8 = (f32[14,80,80]{2,1,0:T(8,128)}, f32[14,80,80]{2,1,0:T(8,128)S(1)}, u32[]{:S(2)}, u32[]{:S(2)}) collective-permute-start(f32[14,80,80]{2,1,0:T(8,128)} %get-tuple-element.13.sq_ref), channel_id=1, source_target_pairs={{0,4},{4,0},{8,12},{12,8},{16,20},{20,16},{24,28},{28,24},{1,5},{5... | collective-permute-start | bytes 1075208 | tf_op jit(solution)/shard_map/ppermute | solution.py:382
  17.1 5.5 %collective-permute-start.5 = (bf16[4,64,128]{2,1,0:T(8,128)(2,1)S(1)}, bf16[4,64,128]{2,1,0:T(8,128)(2,1)S(1)}, u32[]{:S(2)}, u32[]{:S(2)}) collective-permute-start(bf16[4,64,128]{2,1,0:T(8,128)(2,1)S(1)} %pad_maximum_fusion.1.near_ref.near_0), channel_id=1, source_target_pairs={{0,3},{1,2},{2,1},{3,0},{4,7},{5,6},{6,5},{7,4},{8,11},{9,10},{10,... | collective-permute-start | bytes 196616 | tf_op jit(solution)/shard_map/ppermute | solution.py:382
  19.8 4.3 %collective-permute-start.4 = (bf16[4,64,128]{2,1,0:T(8,128)(2,1)S(1)}, bf16[4,64,128]{2,1,0:T(8,128)(2,1)S(1)}, u32[]{:S(2)}, u32[]{:S(2)}) collective-permute-start(bf16[4,64,128]{2,1,0:T(8,128)(2,1)S(1)} %pad_maximum_fusion.1.near_ref.near_0), channel_id=1, source_target_pairs={{0,2},{1,3},{2,0},{3,1},{4,6},{5,7},{6,4},{7,5},{8,10},{9,11},{10,... | collective-permute-start | bytes 196616 | tf_op jit(solution)/shard_map/ppermute | solution.py:382
  20.3 4.3 %collective-permute-start.3 = (bf16[4,64,128]{2,1,0:T(8,128)(2,1)S(1)}, bf16[4,64,128]{2,1,0:T(8,128)(2,1)S(1)}, u32[]{:S(2)}, u32[]{:S(2)}) collective-permute-start(bf16[4,64,128]{2,1,0:T(8,128)(2,1)S(1)} %pad_maximum_fusion.1.near_ref.near_0), channel_id=1, source_target_pairs={{0,1},{1,0},{2,3},{3,2},{4,5},{5,4},{6,7},{7,6},{8,9},{9,8},{10,11... | collective-permute-start | bytes 196616 | tf_op jit(solution)/shard_map/ppermute | solution.py:382
  24.6 6.4 %collective-permute-start.7 = (bf16[3,4,64,128]{3,2,1,0:T(8,128)(2,1)S(1)}, bf16[3,4,64,128]{3,2,1,0:T(8,128)(2,1)S(1)}, u32[]{:S(2)}, u32[]{:S(2)}) collective-permute-start(bf16[3,4,64,128]{3,2,1,0:T(8,128)(2,1)S(1)} %pad_maximum_fusion.near_ref), channel_id=1, source_target_pairs={{0,4},{4,0},{8,12},{12,8},{16,20},{20,16},{24,28},{28,24},{1,5},{5... | collective-permute-start | bytes 589832 | tf_op jit(solution)/shard_map/ppermute | solution.py:382
  24.7 1.5 %collective-permute-start.6 = (bf16[4,64,128]{2,1,0:T(8,128)(2,1)S(1)}, bf16[4,64,128]{2,1,0:T(8,128)(2,1)S(1)}, u32[]{:S(2)}, u32[]{:S(2)}) collective-permute-start(bf16[4,64,128]{2,1,0:T(8,128)(2,1)S(1)} %pad_maximum_fusion.1.near_ref.near_0), channel_id=1, source_target_pairs={{0,4},{4,0},{8,12},{12,8},{16,20},{20,16},{24,28},{28,24},{1,5},{5... | collective-permute-start | bytes 196616 | tf_op jit(solution)/shard_map/ppermute | solution.py:382
  26.2 1.4 %copy-start = (bf16[12,80,768]{2,1,0:T(8,128)(2,1)S(1)}, bf16[12,80,768]{2,1,0:T(8,128)(2,1)}, u32[]{:S(2)}) copy-start(bf16[12,80,768]{2,1,0:T(8,128)(2,1)} %get-tuple-element.12.tab_ref) | copy-start | bytes 4423684
  27.6 1.1 %copy-start.1 = (f32[14,80,80]{2,1,0:T(8,128)S(1)}, f32[14,80,80]{2,1,0:T(8,128)}, u32[]{:S(2)}) copy-start(f32[14,80,80]{2,1,0:T(8,128)} %get-tuple-element.13.sq_ref) | copy-start | bytes 1075204
  28.6 2.4 %copy-start.2 = (f32[14,80,80]{2,1,0:T(8,128)S(1)}, f32[14,80,80]{2,1,0:T(8,128)}, u32[]{:S(2)}) copy-start(f32[14,80,80]{2,1,0:T(8,128)} %get-tuple-element.13.sq_ref) | copy-start | bytes 1075204
  28.6 2.4 %copy-start.5 = (bf16[8,80,768]{2,1,0:T(8,128)(2,1)S(1)}, bf16[8,80,768]{2,1,0:T(8,128)(2,1)}, u32[]{:S(2)}) copy-start(bf16[8,80,768]{2,1,0:T(8,128)(2,1)} %get-tuple-element.14.av_ref) | copy-start | bytes 2949124
  31.1 33.9 %copy-start.3 = (f32[128,64]{0,1:T(8,128)S(1)}, f32[128,64]{0,1:T(8,128)}, u32[]{:S(2)}) copy-start(f32[128,64]{0,1:T(8,128)} %param.12) | copy-start | bytes 98308
  63.7 1.3 %collective-permute-start.9 = (f32[136,128]{1,0:T(8,128)S(1)}, f32[136,128]{1,0:T(8,128)S(1)}, u32[]{:S(2)}, u32[]{:S(2)}) collective-permute-start(f32[136,128]{1,0:T(8,128)S(1)} %get-tuple-element.17), channel_id=1, source_target_pairs={{0,4},{4,0},{8,12},{12,8},{16,20},{20,16},{24,28},{28,24},{1,5},{5... | collective-permute-start | bytes 208904 | tf_op jit(solution)/shard_map/ppermute | solution.py:382
